TPU v7x, 256 devices: a whole 4x4x8 slice. The times are simulated.
256 devices in a mesh: seq: 8 (over z_hi, core), req: 32 (over x, z_lo, y).
Axes of the slice: x: 4, y: 4, z: 8 (z_hi: 4, z_lo: 2; z = z_hi * 2 + z_lo), core: 2. Of those that a mesh axis runs over, the one named last changes fastest.
Arguments:
- inputs: bfloat16 [32, 16, 4, 1536], P('req', 'seq'), may hold values from -6 to 6
- parents: int32 [32, 4, 16], P('req'), may hold values from 0 to 15
- block_len: int32 [32, 128], P('req', 'seq'), may hold values from 0 to 128, as said below
- prompt_key_cache: bfloat16 [32, 16384, 512], P('req', 'seq'), may hold values from -230 to 230
- prompt_value_cache: bfloat16 [32, 16384, 512], P('req', 'seq'), may hold values from -6 to 6
- generated_key_cache: bfloat16 [32, 16, 16, 512], P('req', 'seq'), may hold values from -6 to 6
- generated_value_cache: bfloat16 [32, 16, 16, 512], P('req', 'seq'), may hold values from -6 to 6
- gain_attn: float32 [1536], replicated, may hold values from 0.1 to 1.9
- gain_moe: float32 [1536], replicated, may hold values from 0.1 to 1.9
- w_query: bfloat16 [1536, 1536], P(None, 'seq'), may hold values from -0.15625 to 0.15625
- key_projection_weight: bfloat16 [1536, 512], P(None, 'seq'), may hold values from -0.15625 to 0.15625
- value_projection_weight: bfloat16 [1536, 512], P(None, 'seq'), may hold values from -0.15625 to 0.15625
- w_output: bfloat16 [1536, 1536], P('seq'), may hold values from -0.15625 to 0.15625
- w_in: bfloat16 [32, 1536, 1024], P('req'), may hold values from -0.15625 to 0.15625
- w_out: bfloat16 [32, 512, 1536], P('req'), may hold values from -0.25 to 0.25
- routes: int32 [32, 16, 4, 8], P('req', 'seq'), may hold values from 0 to 31, all different within a row; in each aligned block of 8 rows (0 to 7, 8 to 15, ..., all dimensions but the last counted through in order) at most 4 rows name the same one
- gate_weights: float32 [32, 16, 4, 8], P('req', 'seq'), may hold values from 0.05 to 1
Outputs:
- mixed: bfloat16 [32, 16, 4, 1536], P('req', 'seq')
- final_k: bfloat16 [32, 16, 20, 512], P('req', 'seq')
- final_v: bfloat16 [32, 16, 20, 512], P('req', 'seq')
Inputs may be any that keep to these rules, and one draw needn't show every extreme that they name: block_len[r, j] is the number of live positions at the start of block j of request r; 0 marks an empty block; the first block of every request is full. `routes`: among the rows of one device (its 2 beams over all 4 steps, in the order beam then step) no expert is named more than 4 times.
All inputs are finite; a program needn't handle non-finite values.
Results may differ from a plain program's by a relative error of at most 0.025.
Values may be sent and summed in bfloat16 or wider, within the bound.
No kernel may reach another device: no remote copies, remote signals or barrier semaphores. Data moves between devices by JAX's collectives and lax.ppermute only.
A program may use at most 128 MiB of HBM per device.

v0:
```python
from functools import reduce

import jax
import jax.numpy as jnp
from jax import lax
from jax.sharding import PartitionSpec as P

QUERY_HEADS = 24
HEAD_SIZE = 64
BLK = 128


EPSILON = 1e-05
ROPE_BASE = 10000.0
NEGATIVE_FILL = -1e30
SCORE_SCALE = 0.125


def merged(x, axis, join):
    gathered = jax.tree.map(
        lambda a, kind: lax.all_gather(a.astype(kind), axis),
        x,
        jax.tree.map(lambda a: jnp.bfloat16 if a.dtype == jnp.float32 else a.dtype, x),
    )

    def take(source):
        return jax.tree.map(
            lambda a, own: lax.dynamic_index_in_dim(a, source, 0, False).astype(own.dtype),
            gathered,
            x,
        )

    return lax.fori_loop(
        1, lax.axis_size(axis), lambda source, state: join(state, take(source)), take(0)
    )


def rms_scale(values, gain_vector):
    values = values.astype(jnp.float32)
    mean_sq = jnp.mean(values * values, axis=-1, keepdims=True)
    return values * lax.rsqrt(mean_sq + EPSILON) * gain_vector


def apply_rotary(values, token_positions, head_dim):
    lead_shape = values.shape[:-1]
    head_count = values.shape[-1] // head_dim
    shaped = values.reshape(lead_shape + (head_count, head_dim))
    half_dim = head_dim // 2
    frequency = ROPE_BASE ** (-(jnp.arange(half_dim, dtype=jnp.float32) * 2.0 / head_dim))
    angles = token_positions[:, None] * frequency[None, :]
    cosine = jnp.cos(angles)[None, :, None, :]
    sine_part = jnp.sin(angles)[None, :, None, :]
    first_half = shaped[..., :half_dim]
    second = shaped[..., half_dim:]
    turned = jnp.concatenate(
        [first_half * cosine - second * sine_part, second * cosine + first_half * sine_part],
        axis=-1,
    )
    return turned.reshape(values.shape)


def project(row_block, weight):
    flattened_rows = row_block.reshape(-1, row_block.shape[-1])
    result = jnp.dot(flattened_rows, weight, preferred_element_type=jnp.float32)
    return result.reshape(row_block.shape[:-1] + (weight.shape[1],))


def local_partial(decode_query_step, pieces):
    scored = []
    for key_rows, values, live in pieces:
        shaped_keys = key_rows.reshape(
            key_rows.shape[0], decode_query_step.shape[1], decode_query_step.shape[3]
        )
        scores = (
            jnp.einsum(
                "bgjd,kgd->bgjk", decode_query_step, shaped_keys, preferred_element_type=jnp.float32
            )
            * SCORE_SCALE
        )
        mask = live[:, None, None, :]
        scored.append(
            (jnp.where(mask, scores, NEGATIVE_FILL), mask, values.reshape(shaped_keys.shape))
        )
    row_max = reduce(jnp.maximum, [jnp.max(entry[0], axis=-1) for entry in scored])
    denominator = jnp.zeros(row_max.shape, jnp.float32)
    numerator = jnp.zeros(row_max.shape + (decode_query_step.shape[3],), jnp.float32)
    for entry in scored:
        weights = jnp.where(entry[1], jnp.exp(entry[0] - row_max[..., None]), 0.0)
        denominator = denominator + jnp.sum(weights, axis=-1)
        numerator = numerator + jnp.einsum(
            "bgjk,kgd->bgjd",
            weights.astype(jnp.bfloat16),
            entry[2],
            preferred_element_type=jnp.float32,
        )
    return (row_max, denominator, numerator)


def join_partials(first_part, second_part):
    row_max = jnp.maximum(first_part[0], second_part[0])
    first_scale = jnp.exp(first_part[0] - row_max)
    second_scale = jnp.exp(second_part[0] - row_max)
    denominator = first_scale * first_part[1] + second_scale * second_part[1]
    numerator = first_scale[..., None] * first_part[2] + second_scale[..., None] * second_part[2]
    return (row_max, denominator, numerator)


def expert_block(received, w_in, w_out):
    half_dim = w_out.shape[1]
    projected = jnp.einsum("nesd,edf->nesf", received, w_in, preferred_element_type=jnp.float32)
    activation = (jax.nn.silu(projected[..., :half_dim]) * projected[..., half_dim:]).astype(
        jnp.bfloat16
    )
    return jnp.einsum(
        "nesf,efd->nesd", activation, w_out, preferred_element_type=jnp.float32
    ).astype(jnp.bfloat16)


def route_rows(expert_in, route_ids, pair_weights, capacity, dev_count, experts_all, send_rows):
    row_count, top_count = route_ids.shape
    pair_count = row_count * top_count
    chosen = route_ids.reshape(pair_count)
    pair_index = jnp.arange(pair_count, dtype=jnp.int32)
    before = (chosen[:, None] == chosen[None, :]) & (pair_index[None, :] < pair_index[:, None])
    slot_rank = jnp.sum(before.astype(jnp.int32), axis=1)
    slot_index = chosen * capacity + slot_rank
    slot_table = (
        slot_index[:, None] == jnp.arange(experts_all * capacity, dtype=jnp.int32)[None, :]
    ).astype(jnp.float32)
    row_table = (
        (pair_index // top_count)[:, None] == jnp.arange(row_count, dtype=jnp.int32)[None, :]
    ).astype(jnp.float32)
    placing = jnp.dot(slot_table.T, row_table, precision=lax.Precision.HIGHEST)
    buffer = jnp.dot(
        placing.astype(jnp.bfloat16), expert_in, preferred_element_type=jnp.float32
    ).astype(jnp.bfloat16)
    buffer = buffer.reshape(dev_count, experts_all // dev_count, capacity, expert_in.shape[1])
    returned = send_rows(buffer).reshape(experts_all * capacity, expert_in.shape[1])
    mixing = jnp.dot(
        row_table.T * pair_weights.reshape(pair_count)[None, :],
        slot_table,
        precision=lax.Precision.HIGHEST,
    )
    return jnp.dot(mixing, returned.astype(jnp.float32), precision=lax.Precision.HIGHEST)


def local(
    inputs,
    parents,
    block_len,
    prompt_key_cache,
    prompt_value_cache,
    generated_key_cache,
    generated_value_cache,
    gain_attn,
    gain_moe,
    w_query,
    key_projection_weight,
    value_projection_weight,
    w_output,
    w_in,
    w_out,
    routes,
    gate_weights,
):
    rows_here = inputs.shape[1]
    step_count = inputs.shape[2]
    model_width = inputs.shape[3]
    seq_count = lax.axis_size("seq")
    my_seq = lax.axis_index("seq")
    req_count = lax.axis_size("req")
    experts_all = w_in.shape[0] * req_count
    beam_count = rows_here * seq_count
    prefix_len = prompt_key_cache.shape[1]
    tail_len = generated_key_cache.shape[2]
    kv_width = prompt_key_cache.shape[2]
    kv_heads = kv_width // HEAD_SIZE
    group_size = QUERY_HEADS // kv_heads
    token_positions = jnp.arange(step_count, dtype=jnp.float32) + (
        prefix_len * seq_count + tail_len
    )
    normed = rms_scale(inputs[0], gain_attn).astype(jnp.bfloat16)
    normed_all = lax.all_gather(normed, "seq", axis=0, tiled=True)
    query_rows = apply_rotary(project(normed_all, w_query), token_positions, HEAD_SIZE).astype(
        jnp.bfloat16
    )
    updated_keys = apply_rotary(
        project(normed_all, key_projection_weight), token_positions, HEAD_SIZE
    ).astype(jnp.bfloat16)
    updated_values = project(normed_all, value_projection_weight).astype(jnp.bfloat16)
    queries_all = lax.all_gather(query_rows, "seq", axis=2, tiled=True)
    entry_k, entry_v = (
        lax.all_to_all(updated_keys, "seq", split_axis=0, concat_axis=2, tiled=True),
        lax.all_to_all(updated_values, "seq", split_axis=0, concat_axis=2, tiled=True),
    )
    block_count = block_len.shape[1]
    prefix_live = (jnp.arange(BLK, dtype=jnp.int32)[None, :] < block_len[0][:, None]).reshape(
        1, block_count * BLK
    )
    own_ids = my_seq * rows_here + jnp.arange(rows_here, dtype=jnp.int32)
    beam_ids = jnp.arange(beam_count, dtype=jnp.int32)
    tail_owner = (own_ids[:, None] + jnp.zeros((1, tail_len), jnp.int32)).reshape(
        rows_here * tail_len
    )
    fresh_owner = (own_ids[:, None] + jnp.zeros((1, step_count), jnp.int32)).reshape(
        rows_here * step_count
    )
    fresh_step = (
        jnp.zeros((rows_here, 1), jnp.int32) + jnp.arange(step_count, dtype=jnp.int32)[None, :]
    ).reshape(rows_here * step_count)
    my_parents = lax.dynamic_slice_in_dim(parents[0], my_seq * rows_here, rows_here, 1)
    head_width = w_output.shape[0]

    def send_batch(buffer):
        return lax.all_to_all(
            expert_block(
                lax.all_to_all(buffer, "req", split_axis=0, concat_axis=0, tiled=True), w_in, w_out
            ),
            "req",
            split_axis=0,
            concat_axis=0,
            tiled=True,
        )

    beam_key_cache = generated_key_cache[0]
    beam_value_cache = generated_value_cache[0]
    newest_key = jnp.zeros((rows_here, step_count, kv_width), jnp.bfloat16)
    newest_value = jnp.zeros((rows_here, step_count, kv_width), jnp.bfloat16)
    hidden_rows = []
    for decode_step_index in range(step_count):
        chosen_rows = my_parents[decode_step_index]
        received = (
            lax.all_gather(beam_key_cache, "seq", axis=0, tiled=True),
            lax.all_gather(beam_value_cache, "seq", axis=0, tiled=True),
            lax.all_gather(newest_key, "seq", axis=0, tiled=True),
            lax.all_gather(newest_value, "seq", axis=0, tiled=True),
        )
        beam_key_cache = jnp.take(received[0], chosen_rows, axis=0)
        beam_value_cache = jnp.take(received[1], chosen_rows, axis=0)
        newest_key = jnp.take(received[2], chosen_rows, axis=0)
        newest_value = jnp.take(received[3], chosen_rows, axis=0)
        newest_key = newest_key.at[:, decode_step_index].set(entry_k[:, decode_step_index])
        newest_value = newest_value.at[:, decode_step_index].set(entry_v[:, decode_step_index])
        decode_query_step = queries_all[:, decode_step_index].reshape(
            beam_count, kv_heads, group_size, HEAD_SIZE
        )
        tail_live = beam_ids[:, None] == tail_owner[None, :]
        fresh_live = (beam_ids[:, None] == fresh_owner[None, :]) & (
            fresh_step[None, :] <= decode_step_index
        )
        pieces = [
            (prompt_key_cache[0], prompt_value_cache[0], prefix_live),
            (
                beam_key_cache.reshape(rows_here * tail_len, kv_width),
                beam_value_cache.reshape(rows_here * tail_len, kv_width),
                tail_live,
            ),
            (
                newest_key.reshape(rows_here * step_count, kv_width),
                newest_value.reshape(rows_here * step_count, kv_width),
                fresh_live,
            ),
        ]
        partial_state = local_partial(decode_query_step, pieces)
        row_max, denominator, numerator = merged(partial_state, "seq", join_partials)
        attended_heads = (
            (numerator / denominator[..., None])
            .reshape(beam_count, QUERY_HEADS * HEAD_SIZE)
            .astype(jnp.bfloat16)
        )
        own_heads = lax.dynamic_slice_in_dim(attended_heads, my_seq * head_width, head_width, 1)
        attended = lax.psum_scatter(
            jnp.dot(own_heads, w_output, preferred_element_type=jnp.float32).astype(jnp.bfloat16),
            "seq",
            scatter_dimension=0,
            tiled=True,
        ).astype(jnp.float32)
        hidden = inputs[0][:, decode_step_index].astype(jnp.float32) + attended
        hidden_rows.append(hidden)
    stacked = jnp.stack(hidden_rows, axis=1).reshape(rows_here * step_count, model_width)
    expert_in = rms_scale(stacked, gain_moe).astype(jnp.bfloat16)
    capacity = 2 * rows_here * step_count * routes.shape[3] // experts_all
    route_ids = routes[0].reshape(rows_here * step_count, routes.shape[3])
    pair_weights = gate_weights[0].reshape(rows_here * step_count, routes.shape[3])
    summed = route_rows(
        expert_in, route_ids, pair_weights, capacity, req_count, experts_all, send_batch
    )
    mixed = (stacked + summed).astype(jnp.bfloat16).reshape(rows_here, step_count, model_width)
    final_k = jnp.concatenate([beam_key_cache, newest_key], axis=1)
    final_v = jnp.concatenate([beam_value_cache, newest_value], axis=1)
    return (mixed[None], final_k[None], final_v[None])


def solution(mesh):
    placed = (
        P("req", "seq", None, None),
        P("req", None, None),
        P("req", "seq"),
        P("req", "seq", None),
        P("req", "seq", None),
        P("req", "seq", None, None),
        P("req", "seq", None, None),
        P(),
        P(),
        P(None, "seq"),
        P(None, "seq"),
        P(None, "seq"),
        P("seq", None),
        P("req", None, None),
        P("req", None, None),
        P("req", "seq", None, None),
        P("req", "seq", None, None),
    )
    return jax.shard_map(
        local,
        mesh=mesh,
        in_specs=placed,
        out_specs=(
            P("req", "seq", None, None),
            P("req", "seq", None, None),
            P("req", "seq", None, None),
        ),
        check_vma=False,
    )
```

profile of v0, /device:TPU:8, one launch (start us, length us, event | category | flops | bytes accessed | tf_op | source)
XLA Modules:
  0.0 895.3 jit_solution(18292231915327274517)
XLA Ops:
  9.3 18.2 %all_gather.108 = bf16[16,4,1536]{2,1,0:T(4,128)(2,1)S(1)} all-gather(bf16[2,4,1536]{2,1,0:T(4,128)(2,1)S(1)} %fusion.149), channel_id=1, replica_groups=mesh['seq'=8,'req'=32] {'seq'}, dimensions={0}, use_global_device_ids=true | all-gather | bytes 221184 | tf_op jit(solution)/shard_map/all_gather | solution.py:183
  38.5 18.3 %all-gather.3 = bf16[1,16,16,512]{3,2,0,1:T(8,128)(2,1)} all-gather(bf16[1,2,16,512]{3,2,0,1:T(8,128)(2,1)} %bitcast.429), channel_id=5, replica_groups=mesh['seq'=8,'req'=32] {'seq'}, dimensions={1}, use_global_device_ids=true | all-gather | bytes 294912 | tf_op jit(solution)/shard_map/all_gather | solution.py:234
  56.8 16.0 %all-gather = bf16[1,16,16,512]{3,2,0,1:T(8,128)(2,1)} all-gather(bf16[1,2,16,512]{3,2,0,1:T(8,128)(2,1)} %bitcast.430), channel_id=2, replica_groups=mesh['seq'=8,'req'=32] {'seq'}, dimensions={1}, use_global_device_ids=true | all-gather | bytes 294912 | tf_op jit(solution)/shard_map/all_gather | solution.py:233
  75.9 15.7 %all_gather.117 = bf16[16,16,512]{2,1,0:T(8,128)(2,1)} all-gather(bf16[2,16,512]{2,1,0:T(8,128)(2,1)S(1)} %get-tuple-element.1075), channel_id=1, replica_groups=mesh['seq'=8,'req'=32] {'seq'}, dimensions={0}, use_global_device_ids=true | all-gather | bytes 294912 | tf_op jit(solution)/shard_map/all_gather | solution.py:233
  92.3 15.7 %all_gather.121 = bf16[16,16,512]{2,1,0:T(8,128)(2,1)} all-gather(bf16[2,16,512]{2,1,0:T(8,128)(2,1)S(1)} %get-tuple-element.1074), channel_id=1, replica_groups=mesh['seq'=8,'req'=32] {'seq'}, dimensions={0}, use_global_device_ids=true | all-gather | bytes 294912 | tf_op jit(solution)/shard_map/all_gather | solution.py:234
  111.2 15.7 %all_gather.125 = bf16[16,16,512]{2,1,0:T(8,128)(2,1)} all-gather(bf16[2,16,512]{2,1,0:T(8,128)(2,1)S(1)} %get-tuple-element.1073), channel_id=1, replica_groups=mesh['seq'=8,'req'=32] {'seq'}, dimensions={0}, use_global_device_ids=true | all-gather | bytes 294912 | tf_op jit(solution)/shard_map/all_gather | solution.py:233
  127.6 15.7 %all_gather.129 = bf16[16,16,512]{2,1,0:T(8,128)(2,1)} all-gather(bf16[2,16,512]{2,1,0:T(8,128)(2,1)S(1)} %get-tuple-element.1072), channel_id=1, replica_groups=mesh['seq'=8,'req'=32] {'seq'}, dimensions={0}, use_global_device_ids=true | all-gather | bytes 294912 | tf_op jit(solution)/shard_map/all_gather | solution.py:234
  147.0 15.7 %all_gather.133 = bf16[16,16,512]{2,1,0:T(8,128)(2,1)} all-gather(bf16[2,16,512]{2,1,0:T(8,128)(2,1)S(1)} %get-tuple-element.1071), channel_id=1, replica_groups=mesh['seq'=8,'req'=32] {'seq'}, dimensions={0}, use_global_device_ids=true | all-gather | bytes 294912 | tf_op jit(solution)/shard_map/all_gather | solution.py:233
  167.3 20.3 %all_gather.109 = bf16[16,4,1536]{0,1,2:T(4,128)(2,1)S(1)} all-gather(bf16[16,4,192]{0,1,2:T(4,128)(2,1)S(1)} %bitcast.396), channel_id=1, replica_groups=mesh['seq'=8,'req'=32] {'seq'}, dimensions={2}, use_global_device_ids=true | all-gather | bytes 221184 | tf_op jit(solution)/shard_map/all_gather | solution.py:191
  209.1 16.2 %all_gather.137 = bf16[16,16,512]{2,1,0:T(8,128)(2,1)} all-gather(bf16[2,16,512]{2,1,0:T(8,128)(2,1)S(1)} %copy-done.31), channel_id=1, replica_groups=mesh['seq'=8,'req'=32] {'seq'}, dimensions={0}, use_global_device_ids=true | all-gather | bytes 294912 | tf_op jit(solution)/shard_map/all_gather | solution.py:234
  277.7 16.9 %all_gather.118 = bf16[16,4,512]{2,1,0:T(4,128)(2,1)S(1)} all-gather(bf16[2,4,512]{2,1,0:T(4,128)(2,1)S(1)} %scatter.26), channel_id=1, replica_groups=mesh['seq'=8,'req'=32] {'seq'}, dimensions={0}, use_global_device_ids=true | all-gather | bytes 73728 | tf_op jit(solution)/shard_map/all_gather | solution.py:235
  295.5 14.5 %all_gather.122 = bf16[16,4,512]{2,1,0:T(4,128)(2,1)S(1)} all-gather(bf16[2,4,512]{2,1,0:T(4,128)(2,1)S(1)} %scatter.29), channel_id=1, replica_groups=mesh['seq'=8,'req'=32] {'seq'}, dimensions={0}, use_global_device_ids=true | all-gather | bytes 73728 | tf_op jit(solution)/shard_map/all_gather | solution.py:236
  326.9 14.6 %all_gather.130 = bf16[16,4,512]{2,1,0:T(4,128)(2,1)S(1)} all-gather(bf16[2,4,512]{2,1,0:T(4,128)(2,1)S(1)} %scatter.31), channel_id=1, replica_groups=mesh['seq'=8,'req'=32] {'seq'}, dimensions={0}, use_global_device_ids=true | all-gather | bytes 73728 | tf_op jit(solution)/shard_map/all_gather | solution.py:236
  343.6 14.6 %all_gather.134 = bf16[16,4,512]{2,1,0:T(4,128)(2,1)S(1)} all-gather(bf16[2,4,512]{2,1,0:T(4,128)(2,1)S(1)} %scatter.34), channel_id=1, replica_groups=mesh['seq'=8,'req'=32] {'seq'}, dimensions={0}, use_global_device_ids=true | all-gather | bytes 73728 | tf_op jit(solution)/shard_map/all_gather | solution.py:235
  399.3 14.6 %all-gather.11 = bf16[128,8,3]{1,2,0:T(4,128)(2,1)S(1)} all-gather(bf16[16,8,3]{1,2,0:T(4,128)(2,1)S(1)} %copy.349), channel_id=13, replica_groups=mesh['seq'=8,'req'=32] {'seq'}, dimensions={0}, use_global_device_ids=true | all-gather | bytes 6912 | tf_op jit(solution)/shard_map/all_gather | solution.py:21
  418.5 14.6 %all-gather.12 = bf16[128,8,3]{1,2,0:T(4,128)(2,1)S(1)} all-gather(bf16[16,8,3]{1,2,0:T(4,128)(2,1)S(1)} %copy.350), channel_id=14, replica_groups=mesh['seq'=8,'req'=32] {'seq'}, dimensions={0}, use_global_device_ids=true | all-gather | bytes 6912 | tf_op jit(solution)/shard_map/all_gather | solution.py:21
  438.1 15.3 %all-gather.13 = bf16[128,8,3,64]{3,0,2,1:T(8,128)(2,1)S(1)} all-gather(bf16[16,8,3,64]{3,0,2,1:T(8,128)(2,1)S(1)} %fusion.87), channel_id=15, replica_groups=mesh['seq'=8,'req'=32] {'seq'}, dimensions={0}, use_global_device_ids=true | all-gather | bytes 442368 | tf_op jit(solution)/shard_map/all_gather | solution.py:21
  457.7 33.8 %while.87 = (s32[]{:T(128)}, f32[16,8,3]{0,1,2:T(8,128)S(1)}, f32[16,8,3]{0,1,2:T(8,128)S(1)}, f32[16,8,3,64]{3,2,1,0:T(4,128)S(1)}, bf16[8,16,8,3]{1,2,3,0:T(8,...) while((s32[]{:T(128)}, f32[16,8,3]{0,1,2:T(8,128)S(1)}, ...), condition=%wide.region_35.38_spmd, body=%wide.region_34.37_spmd.sunk | while | flops 101381 | bytes 364183 | solution.py:33
  494.9 14.6 %all-gather.8 = bf16[128,8,3]{1,2,0:T(4,128)(2,1)S(1)} all-gather(bf16[16,8,3]{1,2,0:T(4,128)(2,1)S(1)} %copy.330), channel_id=10, replica_groups=mesh['seq'=8,'req'=32] {'seq'}, dimensions={0}, use_global_device_ids=true | all-gather | bytes 6912 | tf_op jit(solution)/shard_map/all_gather | solution.py:21
  512.0 14.6 %all-gather.9 = bf16[128,8,3]{1,2,0:T(4,128)(2,1)S(1)} all-gather(bf16[16,8,3]{1,2,0:T(4,128)(2,1)S(1)} %copy.331), channel_id=11, replica_groups=mesh['seq'=8,'req'=32] {'seq'}, dimensions={0}, use_global_device_ids=true | all-gather | bytes 6912 | tf_op jit(solution)/shard_map/all_gather | solution.py:21
  529.8 15.5 %all-gather.10 = bf16[128,8,3,64]{3,0,2,1:T(8,128)(2,1)S(1)} all-gather(bf16[16,8,3,64]{3,0,2,1:T(8,128)(2,1)S(1)} %fusion.86), channel_id=12, replica_groups=mesh['seq'=8,'req'=32] {'seq'}, dimensions={0}, use_global_device_ids=true | all-gather | bytes 442368 | tf_op jit(solution)/shard_map/all_gather | solution.py:21
  549.6 33.8 %while.86 = (s32[]{:T(128)}, f32[16,8,3]{0,1,2:T(8,128)S(1)}, f32[16,8,3]{0,1,2:T(8,128)S(1)}, f32[16,8,3,64]{3,2,1,0:T(4,128)S(1)}, bf16[8,16,8,3]{1,2,3,0:T(8,...) while((s32[]{:T(128)}, f32[16,8,3]{0,1,2:T(8,128)S(1)}, ...), condition=%wide.region_26.29_spmd, body=%wide.region_25.28_spmd.sunk | while | flops 101381 | bytes 364183 | solution.py:33
  590.0 14.6 %all-gather.5 = bf16[128,8,3]{1,2,0:T(4,128)(2,1)S(1)} all-gather(bf16[16,8,3]{1,2,0:T(4,128)(2,1)S(1)} %copy.310), channel_id=7, replica_groups=mesh['seq'=8,'req'=32] {'seq'}, dimensions={0}, use_global_device_ids=true | all-gather | bytes 6912 | tf_op jit(solution)/shard_map/all_gather | solution.py:21
  607.1 14.6 %all-gather.6 = bf16[128,8,3]{1,2,0:T(4,128)(2,1)S(1)} all-gather(bf16[16,8,3]{1,2,0:T(4,128)(2,1)S(1)} %copy.311), channel_id=8, replica_groups=mesh['seq'=8,'req'=32] {'seq'}, dimensions={0}, use_global_device_ids=true | all-gather | bytes 6912 | tf_op jit(solution)/shard_map/all_gather | solution.py:21
  624.9 15.8 %all-gather.7 = bf16[128,8,3,64]{3,0,2,1:T(8,128)(2,1)S(1)} all-gather(bf16[16,8,3,64]{3,0,2,1:T(8,128)(2,1)S(1)} %fusion.85), channel_id=9, replica_groups=mesh['seq'=8,'req'=32] {'seq'}, dimensions={0}, use_global_device_ids=true | all-gather | bytes 442368 | tf_op jit(solution)/shard_map/all_gather | solution.py:21
  645.0 33.6 %while.85 = (s32[]{:T(128)}, f32[16,8,3]{0,1,2:T(8,128)S(1)}, f32[16,8,3]{0,1,2:T(8,128)S(1)}, f32[16,8,3,64]{3,2,1,0:T(4,128)S(1)}, bf16[8,16,8,3]{1,2,3,0:T(8,...) while((s32[]{:T(128)}, f32[16,8,3]{0,1,2:T(8,128)S(1)}, ...), condition=%wide.region_17.20_spmd, body=%wide.region_16.19_spmd.sunk | while | flops 101381 | bytes 364183 | solution.py:33
  683.3 14.6 %all-gather.1 = bf16[128,8,3]{1,2,0:T(4,128)(2,1)S(1)} all-gather(bf16[16,8,3]{1,2,0:T(4,128)(2,1)S(1)} %copy.285), channel_id=3, replica_groups=mesh['seq'=8,'req'=32] {'seq'}, dimensions={0}, use_global_device_ids=true | all-gather | bytes 6912 | tf_op jit(solution)/shard_map/all_gather | solution.py:21
  700.5 14.6 %all-gather.2 = bf16[128,8,3]{1,2,0:T(4,128)(2,1)S(1)} all-gather(bf16[16,8,3]{1,2,0:T(4,128)(2,1)S(1)} %copy.286), channel_id=4, replica_groups=mesh['seq'=8,'req'=32] {'seq'}, dimensions={0}, use_global_device_ids=true | all-gather | bytes 6912 | tf_op jit(solution)/shard_map/all_gather | solution.py:21
  718.2 15.5 %all-gather.4 = bf16[128,8,3,64]{3,0,2,1:T(8,128)(2,1)S(1)} all-gather(bf16[16,8,3,64]{3,0,2,1:T(8,128)(2,1)S(1)} %fusion.84), channel_id=6, replica_groups=mesh['seq'=8,'req'=32] {'seq'}, dimensions={0}, use_global_device_ids=true | all-gather | bytes 442368 | tf_op jit(solution)/shard_map/all_gather | solution.py:21
  738.0 33.7 %while.84 = (s32[]{:T(128)}, f32[16,8,3]{0,1,2:T(8,128)S(1)}, f32[16,8,3]{0,1,2:T(8,128)S(1)}, f32[16,8,3,64]{3,2,1,0:T(4,128)S(1)}, bf16[8,16,8,3]{1,2,3,0:T(8,...) while((s32[]{:T(128)}, f32[16,8,3]{0,1,2:T(8,128)S(1)}, ...), condition=%wide.region_8.11_spmd, body=%wide.region_7.10_spmd.sunk | while | flops 101381 | bytes 364183 | solution.py:33
  776.5 72.4 %all-reduce.7.cloned.1.call-done = (bf16[16,1536]{1,0:T(8,128)(2,1)}, bf16[16,1536]{1,0:T(8,128)(2,1)}, bf16[16,1536]{1,0:T(8,128)(2,1)}, bf16[16,1536]{1,0:T(8,128)(2,1)}) async-done(((bf16[16,1536]{1,0:T(8,128)(2,1)}, bf16[16,1536]{1,0:T(8,128)(2,1)}, bf16[16,1536]{1,0:T(8,128)(2,1)}, bf16[16,1536]{1,0:T(8,128)(2,1)}), (bf16[16,1536]{1,0:T(8,128)(2,1)}, bf16[16,1536]{1,0:T(8,128)(2,1)}, ...) | async-done | bytes 196624
  853.5 16.4 %all_to_all.46 = bf16[32,1,4,1536]{3,2,1,0:T(4,128)(2,1)S(1)} all-to-all(bf16[32,1,4,1536]{3,2,1,0:T(4,128)(2,1)} %bitcast.395), channel_id=1, replica_groups=mesh['seq'=8,'req'=32] {'req'}, dimensions={0} | all-to-all | bytes 786432 | tf_op jit(solution)/shard_map/all_to_all | solution.py:217
  (528 shorter events, 383.5 us)
Async XLA Ops:
  7.2 862.7 %copy-start = (bf16[1,1536,1024]{2,1,0:T(8,128)(2,1)S(1)}, bf16[1,1536,1024]{2,1,0:T(8,128)(2,1)}, u32[]{:S(2)}) copy-start(bf16[1,1536,1024]{2,1,0:T(8,128)(2,1)} %param.58) | copy-start | bytes 9437188
  7.2 156.3 %copy-start.26 = (bf16[1,2,4,1536]{3,2,1,0:T(4,128)(2,1)S(1)}, bf16[1,2,4,1536]{3,2,1,0:T(4,128)(2,1)}, u32[]{:S(2)}) copy-start(bf16[1,2,4,1536]{3,2,1,0:T(4,128)(2,1)} %param.45) | copy-start | bytes 73732
  29.6 242.2 %all-to-all-start = ((bf16[8,2,256]{2,1,0:T(2,128)(2,1)}), bf16[8,2,256]{2,1,0:T(2,128)(2,1)}, u32[]{:S(2)}, u32[]{:S(2)}) async-start(bf16[8,2,256]{2,1,0:T(2,128)(2,1)} %reshape.1151), calls=%async_computation | async-start | bytes 16384 | tf_op jit(solution)/shard_map/all_to_all | solution.py:193
  38.5 69.6 %copy-start.63 = (pred[2]{0:T(512)(128)(4,1)}, pred[2]{0:T(512)(128)(4,1)S(1)}, u32[]{:S(2)}) copy-start(pred[2]{0:T(512)(128)(4,1)S(1)} %get-tuple-element.1064) | copy-start | bytes 10
  38.5 149.1 %copy-start.61 = (pred[2]{0:T(512)(128)(4,1)}, pred[2]{0:T(512)(128)(4,1)S(1)}, u32[]{:S(2)}) copy-start(pred[2]{0:T(512)(128)(4,1)S(1)} %get-tuple-element.1060) | copy-start | bytes 10
  38.5 149.1 %copy-start.62 = (pred[2]{0:T(512)(128)(4,1)}, pred[2]{0:T(512)(128)(4,1)S(1)}, u32[]{:S(2)}) copy-start(pred[2]{0:T(512)(128)(4,1)S(1)} %get-tuple-element.1062) | copy-start | bytes 10
  38.5 69.5 %copy-start.59 = (s32[1024]{0:T(1024)}, s32[1024]{0:T(1024)S(1)}, u32[]{:S(2)}) copy-start(s32[1024]{0:T(1024)S(1)} %pad_clamp_fusion.3) | copy-start | bytes 12292
  75.9 89.8 %copy-start.27 = (bf16[2,16,512]{2,1,0:T(8,128)(2,1)}, bf16[2,16,512]{2,1,0:T(8,128)(2,1)S(1)}, u32[]{:S(2)}) copy-start(bf16[2,16,512]{2,1,0:T(8,128)(2,1)S(1)} %get-tuple-element.1074) | copy-start | bytes 98308
  92.3 18.7 %copy-start.57 = (s32[1024]{0:T(1024)}, s32[1024]{0:T(1024)S(1)}, u32[]{:S(2)}) copy-start(s32[1024]{0:T(1024)S(1)} %pad_clamp_fusion.2) | copy-start | bytes 12292
  111.2 54.5 %copy-start.29 = (bf16[2,16,512]{2,1,0:T(8,128)(2,1)}, bf16[2,16,512]{2,1,0:T(8,128)(2,1)S(1)}, u32[]{:S(2)}) copy-start(bf16[2,16,512]{2,1,0:T(8,128)(2,1)S(1)} %get-tuple-element.1072) | copy-start | bytes 98308
  127.6 18.7 %copy-start.56 = (s32[1024]{0:T(1024)}, s32[1024]{0:T(1024)S(1)}, u32[]{:S(2)}) copy-start(s32[1024]{0:T(1024)S(1)} %pad_clamp_fusion.1) | copy-start | bytes 12292
  191.2 17.9 %copy-start.31 = (bf16[2,16,512]{2,1,0:T(8,128)(2,1)S(1)}, bf16[2,16,512]{2,1,0:T(8,128)(2,1)}, u32[]{:S(2)}) copy-start(bf16[2,16,512]{2,1,0:T(8,128)(2,1)} %get-tuple-element.1070) | copy-start | bytes 98308
  193.5 34.8 %copy-start.60 = (pred[2]{0:T(512)(128)(4,1)S(1)}, pred[2]{0:T(512)(128)(4,1)}, u32[]{:S(2)}) copy-start(pred[2]{0:T(512)(128)(4,1)} %get-tuple-element.1032) | copy-start | bytes 10
  196.4 68.7 %copy-start.34 = (bf16[2,4,512]{2,1,0:T(4,128)(2,1)}, bf16[2,4,512]{2,1,0:T(4,128)(2,1)S(1)}, u32[]{:S(2)}) copy-start(bf16[2,4,512]{2,1,0:T(4,128)(2,1)S(1)} %broadcast_select_fusion.14) | copy-start | bytes 24580
  198.1 31.0 %copy-start.73 = (s32[2]{0:T(128)S(1)}, s32[2]{0:T(128)}, u32[]{:S(2)}) copy-start(s32[2]{0:T(128)} %iota_add_fusion) | copy-start | bytes 28
  198.8 29.5 %copy-start.58 = (s32[1024]{0:T(1024)}, s32[1024]{0:T(1024)S(1)}, u32[]{:S(2)}) copy-start(s32[1024]{0:T(1024)S(1)} %pad_clamp_fusion) | copy-start | bytes 12292
  228.4 41.4 %copy-start.32 = (bf16[2,16,512]{2,1,0:T(8,128)(2,1)}, bf16[2,16,512]{2,1,0:T(8,128)(2,1)S(1)}, u32[]{:S(2)}) copy-start(bf16[2,16,512]{2,1,0:T(8,128)(2,1)S(1)} %get-tuple-element.1068) | copy-start | bytes 98308
  229.3 30.6 %copy-start.37 = (pred[16,32]{1,0:T(8,128)(4,1)}, pred[16,32]{1,0:T(8,128)(4,1)S(1)}, u32[]{:S(2)}) copy-start(pred[16,32]{1,0:T(8,128)(4,1)S(1)} %iota_compare_fusion.6) | copy-start | bytes 1540
  262.4 117.7 %copy-start.51 = (pred[16,8]{0,1:T(8,128)(4,1)}, pred[16,8]{0,1:T(8,128)(4,1)S(1)}, u32[]{:S(2)}) copy-start(pred[16,8]{0,1:T(8,128)(4,1)S(1)} %get-tuple-element.1085) | copy-start | bytes 388
  265.1 30.3 %copy-start.35 = (bf16[2,4,512]{2,1,0:T(4,128)(2,1)S(1)}, bf16[2,4,512]{2,1,0:T(4,128)(2,1)}, u32[]{:S(2)}) copy-start(bf16[2,4,512]{2,1,0:T(4,128)(2,1)} %copy-done.34) | copy-start | bytes 24580
  265.1 112.8 %copy-start.52 = (pred[16,8]{0,1:T(8,128)(4,1)S(1)}, pred[16,8]{0,1:T(8,128)(4,1)}, u32[]{:S(2)}) copy-start(pred[16,8]{0,1:T(8,128)(4,1)} %get-tuple-element.1083) | copy-start | bytes 388
  265.9 118.1 %copy-start.43 = (f32[16,8,3]{0,2,1:T(4,128)S(1)}, f32[16,8,3]{0,2,1:T(4,128)}, u32[]{:S(2)}) copy-start(f32[16,8,3]{0,2,1:T(4,128)} %get-tuple-element.1088) | copy-start | bytes 4612
  265.9 119.4 %copy-start.45 = (f32[16,8,3]{0,2,1:T(4,128)S(1)}, f32[16,8,3]{0,2,1:T(4,128)}, u32[]{:S(2)}) copy-start(f32[16,8,3]{0,2,1:T(4,128)} %get-tuple-element.1106) | copy-start | bytes 4612
  271.8 22.9 %all-to-all-start.1 = ((bf16[8,2,256]{2,1,0:T(2,128)(2,1)}), bf16[8,2,256]{2,1,0:T(2,128)(2,1)S(1)}, u32[]{:S(2)}, u32[]{:S(2)}) async-start(bf16[8,2,256]{2,1,0:T(2,128)(2,1)} %reshape.1153), calls=%async_computation.1 | async-start | bytes 16384 | tf_op jit(solution)/shard_map/all_to_all | solution.py:194
  276.7 572.2 %all-reduce.7.cloned.1.call-start = ((), (), s32[]{:S(2)}) async-start(), calls=%async_computation.4 | async-start | bytes 393216
  386.6 28.8 %copy-start.25 = (f32[16,8,3]{0,2,1:T(4,128)}, f32[16,8,3]{0,2,1:T(4,128)S(1)}, u32[]{:S(2)}) copy-start(f32[16,8,3]{0,2,1:T(4,128)S(1)} %get-tuple-element.1029) | copy-start | bytes 4612
  392.7 22.7 %copy-start.24 = (f32[16,8,3]{0,2,1:T(4,128)}, f32[16,8,3]{0,2,1:T(4,128)S(1)}, u32[]{:S(2)}) copy-start(f32[16,8,3]{0,2,1:T(4,128)S(1)} %get-tuple-element.1027) | copy-start | bytes 4612
  394.8 20.6 %copy-start.23 = (f32[16,8,3]{0,2,1:T(4,128)}, f32[16,8,3]{0,2,1:T(4,128)S(1)}, u32[]{:S(2)}) copy-start(f32[16,8,3]{0,2,1:T(4,128)S(1)} %get-tuple-element.1025) | copy-start | bytes 4612
  397.8 17.6 %copy-start.14 = (f32[16,8,3,32]{3,0,2,1:T(8,128)S(1)}, f32[16,8,3,32]{3,0,2,1:T(8,128)}, u32[]{:S(2)}) copy-start(f32[16,8,3,32]{3,0,2,1:T(8,128)} %get-tuple-element.1097) | copy-start | bytes 147460
  397.8 17.6 %copy-start.38 = (pred[16,32]{1,0:T(8,128)(4,1)S(1)}, pred[16,32]{1,0:T(8,128)(4,1)}, u32[]{:S(2)}) copy-start(pred[16,32]{1,0:T(8,128)(4,1)} %copy-done.37) | copy-start | bytes 1540
  853.5 17.0 %copy-start.71 = (bf16[1,512,1536]{2,1,0:T(8,128)(2,1)S(1)}, bf16[1,512,1536]{2,1,0:T(8,128)(2,1)}, u32[]{:S(2)}) copy-start(bf16[1,512,1536]{2,1,0:T(8,128)(2,1)} %param.59) | copy-start | bytes 4718596
  871.9 13.6 %all-to-all-start.3 = ((bf16[32,1,4,1536]{3,2,1,0:T(4,128)(2,1)}), bf16[32,1,4,1536]{3,2,1,0:T(4,128)(2,1)S(1)}, u32[]{:S(2)}, u32[]{:S(2)}) async-start(bf16[32,1,4,1536]{3,2,1,0:T(4,128)(2,1)} %copy.366), calls=%async_computation.3 | async-start | bytes 786432 | tf_op jit(solution)/shard_map/all_to_all | solution.py:215
  (46 other events, 224.2 us)
Sparse Core Ops, SparseCore 0:
  775.7 73.1 all-reduce.6
where the time goes:
time: 908 us; the launch traced here: 895 us
  blocking collectives  452 us (50%)
  local copies, waits for them, and re-layouts  168 us (19%)
  other arithmetic  103 us (11%)
  waiting for transfers between devices  76.4 us (8%)
  matrix products  64.6 us (7%)
  between operations  15.8 us (2%)
  starting transfers between devices  14.6 us (2%)
    all_gather x12, blocking collectives, merged(): lax.all_gather(a.astype(kind), axis)  179 us
    unnamed x2, waiting for transfers between devices  72.4 us
    all_gather x4, blocking collectives, local(): lax.all_gather(beam_value_cache, 'seq', axis=0, tiled=True)  65.9 us
    all_gather x4, blocking collectives, local(): lax.all_gather(beam_key_cache, 'seq', axis=0, tiled=True)  63.1 us
    add x28, other arithmetic, join_partials(): first_scale[..., None] * first_part[2]  46.6 us
    all_gather x3, blocking collectives, local(): lax.all_gather(newest_key, 'seq', axis=0, tiled=True)  46 us
    all_gather x3, blocking collectives, local(): lax.all_gather(newest_value, 'seq', axis=0, tiled=True)  43.7 us
    dot_general x12, matrix products, local_partial(): jnp.einsum('bgjd,kgd->bgjk', decode_query_step, shaped_keys, preferred_el...  29.1 us
  transfers between devices with their start and end apart: 4, of which 2 were waited for; matrix products, arithmetic and copies ran while one was open for 10% of the time, Pallas kernels for 0%

commit v1 on v0

v1 whole, which is shorter than its diff:
```python
import functools

import jax
import jax.numpy as jnp
import numpy as np
from jax import lax
from jax.experimental import pallas as pl
from jax.experimental.pallas import tpu as pltpu
from jax.sharding import PartitionSpec as P

HEAD = 64
BLK = 128
EPSILON = 1e-05
ROPE_BASE = 10000.0
FILL = -(2.0**100)
SCALE = 0.125
BF16 = jnp.bfloat16
F32 = jnp.float32


def whole():
    return pl.BlockSpec(memory_space=pltpu.VMEM)


def scalars():
    return pl.BlockSpec(memory_space=pltpu.SMEM)


def params(mib):
    return pltpu.CompilerParams(vmem_limit_bytes=mib << 20)


def dot(a, b):
    return jnp.dot(a, b, preferred_element_type=F32)


def dot_t(a, b):
    return lax.dot_general(a, b, (((1,), (1,)), ((), ())), preferred_element_type=F32)


def lanes(shape):
    return lax.broadcasted_iota(jnp.int32, shape, len(shape) - 1)


def norm(x, gain):
    mean_sq = jnp.mean(x * x, axis=-1, keepdims=True)
    return x * lax.rsqrt(mean_sq + EPSILON) * gain


def norm_kernel(x_ref, gain_ref, own_k_ref, own_v_ref, out_ref, own_ref):
    beams, steps = x_ref.shape[0], x_ref.shape[1]
    for b in range(beams):
        rows = norm(x_ref[b].astype(F32), gain_ref[...])
        out_ref[b * steps : (b + 1) * steps, :] = rows.astype(BF16)
    for d in range(own_ref.shape[0]):
        own_ref[d, 0] = own_k_ref[...]
        own_ref[d, 1] = own_v_ref[...]


def project_kernel(x_ref, wq_ref, wk_ref, wv_ref, cos_ref, sin_ref, out_ref):
    x = x_ref[...]
    rows = x.shape[0]
    q = dot(x, wq_ref[...]) * SCALE
    k = dot(x, wk_ref[...])
    v = dot(x, wv_ref[...])
    y = jnp.concatenate([q, k], axis=1)
    width = y.shape[1]
    half = HEAD // 2
    first = lanes(y.shape) % HEAD < half
    turned = jnp.where(first, pltpu.roll(y, width - half, 1), pltpu.roll(y, half, 1))
    y = (y * cos_ref[...] + turned * sin_ref[...]).astype(BF16)
    out_ref[0:rows, :] = y[:, 0:128]
    out_ref[rows : 2 * rows, :] = y[:, 128:256]
    out_ref[2 * rows : 2 * rows + rows // 2, :] = jnp.concatenate(
        [v[0 : rows // 2], v[rows // 2 :]], axis=1
    ).astype(BF16)


def lookup(parents_ref, step, cur, beams):
    found = jnp.zeros(cur.shape, jnp.int32)
    for b in range(beams):
        found = jnp.where(cur == b, parents_ref[step, b], found)
    return found


def attend_kernel(
    seq_ref,
    parents_ref,
    len_ref,
    qkv_ref,
    k_ref,
    v_ref,
    own_k_ref,
    own_v_ref,
    out_ref,
    fresh_k_ref,
    fresh_v_ref,
    s_ref,
    p_ref,
    bias_ref,
    extra_ref,
):
    steps, beams = parents_ref.shape
    rows = steps * beams
    keys = k_ref.shape[0]
    blocks = keys // BLK
    here = own_k_ref.shape[0]
    tail = own_k_ref.shape[1]
    own_keys = here * tail
    seq = seq_ref[0]
    shape = (rows, 128)
    lane = lanes(shape)
    low = lane < HEAD

    @pl.when(pl.program_id(0) == 0)
    def _():
        spot = lanes((8, BLK))
        for j in range(blocks):
            bias_ref[:, j * BLK : (j + 1) * BLK] = jnp.where(spot < len_ref[0, j], 0.0, FILL)
        row = lax.broadcasted_iota(jnp.int32, shape, 0)
        step = row % steps
        cur = row // steps
        fresh = lane - own_keys
        key_beam = fresh // steps
        key_step = fresh % steps
        live = jnp.zeros(shape, jnp.int32)
        for s in range(steps - 1, -1, -1):
            hit = (key_step == s) & (cur == key_beam) & (step >= s) & (key_beam // here == seq)
            live = live | jnp.where((fresh >= 0) & hit, 1, 0)
            cur = jnp.where(step >= s, lookup(parents_ref, s, cur, beams), cur)
        own_hit = (lane < own_keys) & (cur == seq * here + lane // tail)
        live = live | jnp.where(own_hit, 1, 0)
        extra_ref[...] = jnp.where(live > 0, 0.0, FILL)

    def swap(x):
        return pltpu.roll(x, HEAD, 1)

    parts = []
    fresh_k, fresh_v = [], []
    for c in range(2):
        t0 = qkv_ref[c, 0:rows, :].astype(F32)
        t1 = qkv_ref[c, rows : 2 * rows, :].astype(F32)
        tv = qkv_ref[c, 2 * rows : 2 * rows + rows // 2, :].astype(F32)
        keep = low if c == 0 else ~low
        for tile in (t0, swap(t0), t1) if c == 0 else (swap(t0), t0, swap(t1)):
            parts.append(jnp.where(keep, tile, 0.0).astype(BF16))
        fresh_k.append(t1)
        fresh_v.append(jnp.concatenate([tv, swap(tv)], axis=0))
    q = jnp.concatenate(parts, axis=0)
    new_k = jnp.where(low, swap(fresh_k[0]), fresh_k[1]).astype(BF16)
    new_v = jnp.where(low, fresh_v[0], swap(fresh_v[1])).astype(BF16)
    fill = jnp.zeros((128 - own_keys - rows, 128), BF16)
    extra_k = jnp.concatenate([own_k_ref[...].reshape(own_keys, 128), new_k, fill], axis=0)
    extra_v = jnp.concatenate([own_v_ref[...].reshape(own_keys, 128), new_v, fill], axis=0)

    pick_row = lax.broadcasted_iota(jnp.int32, (here * steps, rows), 0)
    pick_col = lanes((here * steps, rows))
    chosen = jnp.zeros(pick_row.shape, jnp.int32)
    for i in range(here):
        beam = seq * here + i
        for s in range(steps - 1, -1, -1):
            hit = (pick_row == i * steps + s) & (pick_col == beam * steps + s)
            chosen = chosen | jnp.where(hit, 1, 0)
            beam = parents_ref[s, beam]
    chosen = chosen.astype(F32).astype(BF16)
    fresh_k_ref[...] = dot(chosen, new_k).astype(BF16)
    fresh_v_ref[...] = dot(chosen, new_v).astype(BF16)

    s_ref[:, 0:keys] = dot_t(q, k_ref[...])
    s_ref[:, keys : keys + 128] = dot_t(q, extra_k)
    lse, total = [], []
    for i in range(6):
        span = slice(i * rows, (i + 1) * rows)
        s0 = s_ref[span, 0:keys] + bias_ref[0:1, :]
        s1 = s_ref[span, keys : keys + 128] + extra_ref[...]
        top = jnp.maximum(
            jnp.max(s0, axis=-1, keepdims=True), jnp.max(s1, axis=-1, keepdims=True)
        )
        e0 = jnp.exp(s0 - top)
        e1 = jnp.exp(s1 - top)
        p_ref[span, 0:keys] = e0.astype(BF16)
        p_ref[span, keys : keys + 128] = e1.astype(BF16)
        denominator = jnp.sum(e0, axis=-1, keepdims=True) + jnp.sum(e1, axis=-1, keepdims=True)
        total.append(denominator)
        lse.append(top + jnp.log(denominator))
    o = dot(p_ref[:, 0:keys], v_ref[...]) + dot(p_ref[:, keys : keys + 128], extra_v)
    for c in range(2):
        values = []
        stats = jnp.zeros(shape, F32)
        for j in range(3):
            i = 3 * c + j
            values.append(o[i * rows : (i + 1) * rows, :] / total[i])
            rest = lse[i]
            for piece in range(3):
                part = rest.astype(BF16).astype(F32)
                rest = rest - part
                stats = jnp.where(lane == HEAD + 3 * j + piece, part, stats)
        if c == 0:
            a = jnp.where(low, values[0], swap(values[1]))
            b = jnp.where(low, values[2], stats)
        else:
            a = jnp.where(low, swap(values[0]), values[1])
            b = jnp.where(low, swap(values[2]), stats)
        out_ref[c, :, 0:128] = a.astype(BF16)
        out_ref[c, :, 128:256] = b.astype(BF16)


def join_kernel(part_ref, w_ref, out_ref):
    sources, rows = part_ref.shape[0], part_ref.shape[1]
    shape = (rows, 128)
    low = lanes(shape) < HEAD
    b = [part_ref[s, :, 128:256].astype(F32) for s in range(sources)]
    lse = [x + pltpu.roll(x, 127, 1) + pltpu.roll(x, 126, 1) for x in b]
    top = functools.reduce(jnp.maximum, lse)
    weight = [jnp.exp(x - top) for x in lse]
    inverse = 1.0 / functools.reduce(jnp.add, weight)
    first = jnp.zeros(shape, F32)
    second = jnp.zeros(shape, F32)
    for s in range(sources):
        w = weight[s] * inverse
        w0, w1, w2 = (w[:, HEAD + 3 * j : HEAD + 3 * j + 1] for j in range(3))
        first = first + part_ref[s, :, 0:128].astype(F32) * jnp.where(low, w0, w1)
        second = second + b[s] * w2
    first = first.astype(BF16)
    second = second[:, 0:HEAD].astype(BF16)
    out = dot(first, w_ref[0:128, :]) + dot(second, w_ref[128 : 128 + HEAD, :])
    out = out.astype(BF16)
    each = rows // sources
    for s in range(sources):
        out_ref[s] = out[s * each : (s + 1) * each, :]


def dispatch_kernel(
    capacity, x_ref, sums_ref, gain_ref, route_ref, gate_ref, hidden_ref, out_ref, mix_ref
):
    beams, steps = x_ref.shape[0], x_ref.shape[1]
    rows = beams * steps
    total = sums_ref[0].astype(F32)
    for s in range(1, sums_ref.shape[0]):
        total = total + sums_ref[s].astype(F32)
    inputs = jnp.concatenate([x_ref[b].astype(F32) for b in range(beams)], axis=0)
    hidden = inputs + total
    hidden_ref[...] = hidden
    expert_in = norm(hidden, gain_ref[...]).astype(BF16)
    experts = out_ref.shape[0]
    slots = experts * capacity
    slot = lanes((rows, slots))
    routes = jnp.concatenate([route_ref[b] for b in range(beams)], axis=0)
    gates = jnp.concatenate([gate_ref[b] for b in range(beams)], axis=0)
    named = jnp.zeros((rows, slots), F32)
    gate = jnp.zeros((rows, slots), F32)
    for j in range(routes.shape[1]):
        hit = routes[:, j : j + 1] == slot // capacity
        named = jnp.where(hit, 1.0, named)
        gate = jnp.where(hit, gates[:, j : j + 1], gate)
    earlier = jnp.where(
        lanes((rows, rows)) < lax.broadcasted_iota(jnp.int32, (rows, rows), 0), 1.0, 0.0
    )
    rank = dot(earlier.astype(BF16), named.astype(BF16))
    placed = (named > 0.0) & (rank == (slot % capacity).astype(F32))
    mix_ref[...] = jnp.where(placed, gate, 0.0)
    place = jnp.where(placed, 1.0, 0.0).T.astype(BF16)
    buffer = dot(place, expert_in)
    for e in range(experts):
        out_ref[e] = buffer[e * capacity : (e + 1) * capacity, :].astype(BF16)


def expert_kernel(x_ref, w_in_ref, w_out_ref, out_ref, rows_ref):
    sources, capacity = x_ref.shape[0], x_ref.shape[1]
    for s in range(sources):
        rows_ref[s * capacity : (s + 1) * capacity, :] = x_ref[s].astype(F32)
    projected = dot(rows_ref[...].astype(BF16), w_in_ref[0])
    half = projected.shape[1] // 2
    g, u = projected[:, 0:half], projected[:, half:]
    act = (g * jax.nn.sigmoid(g) * u).astype(BF16)
    out = dot(act, w_out_ref[0])
    for s in range(sources):
        out_ref[s] = out[s * capacity : (s + 1) * capacity, :].astype(BF16)


def mix_kernel(hidden_ref, mix_ref, back_ref, out_ref, rows_ref):
    experts, capacity = back_ref.shape[0], back_ref.shape[1]
    for e in range(experts):
        rows_ref[e * capacity : (e + 1) * capacity, :] = back_ref[e].astype(F32)
    returned = rows_ref[...].astype(BF16)
    rest = mix_ref[...]
    total = hidden_ref[...]
    for _ in range(3):
        part = rest.astype(BF16)
        rest = rest - part.astype(F32)
        total = total + dot(part, returned)
    steps = out_ref.shape[1]
    for b in range(out_ref.shape[0]):
        out_ref[b] = total[b * steps : (b + 1) * steps, :].astype(BF16)


def final_kernel(seq_ref, parents_ref, own_ref, fresh_k_ref, fresh_v_ref, k_ref, v_ref):
    steps = parents_ref.shape[0]
    here, tail = own_ref.shape[2], own_ref.shape[3]
    for i in range(here):
        beam = seq_ref[0] * here + i
        for s in range(steps - 1, -1, -1):
            beam = parents_ref[s, beam]
        k_ref[i, 0:tail, :] = own_ref[beam // here, 0, beam % here]
        v_ref[i, 0:tail, :] = own_ref[beam // here, 1, beam % here]
        k_ref[i, tail:, :] = fresh_k_ref[i * steps : (i + 1) * steps, :]
        v_ref[i, tail:, :] = fresh_v_ref[i * steps : (i + 1) * steps, :]


def rotary_tables(rows, steps, start):
    half = HEAD // 2
    frequency = ROPE_BASE ** (-(np.arange(half, dtype=np.float64) * 2.0 / HEAD))
    angles = (np.arange(rows) % steps + start)[:, None] * frequency[None, :]
    cosine = np.tile(np.cos(angles), (1, 8)).astype(np.float32)
    sine = np.sin(angles)
    sine = np.tile(np.concatenate([-sine, sine], axis=1), (1, 4)).astype(np.float32)
    return cosine, sine


def call(kernel, outs, *args, ins=None, scratch=(), mib=48, flops=0, moved=0):
    return pl.pallas_call(
        kernel,
        out_shape=outs,
        in_specs=ins or [whole()] * len(args),
        out_specs=jax.tree.map(lambda _: whole(), outs),
        scratch_shapes=list(scratch),
        compiler_params=params(mib),
        cost_estimate=pl.CostEstimate(
            flops=flops or 1 << 20, bytes_accessed=moved or 1 << 20, transcendentals=0
        ),
    )(*args)


def shaped(shape, dtype=BF16):
    return jax.ShapeDtypeStruct(shape, dtype)


def local(
    inputs,
    parents,
    block_len,
    prompt_key_cache,
    prompt_value_cache,
    generated_key_cache,
    generated_value_cache,
    gain_attn,
    gain_moe,
    w_query,
    key_projection_weight,
    value_projection_weight,
    w_output,
    w_in,
    w_out,
    routes,
    gate_weights,
):
    n_seq = lax.axis_size("seq")
    n_req = lax.axis_size("req")
    seq = lax.axis_index("seq").astype(jnp.int32).reshape(1)
    here, steps, width = inputs.shape[1:]
    local_rows = here * steps
    rows = local_rows * n_seq
    keys, kv_width = prompt_key_cache.shape[1:]
    tail = generated_key_cache.shape[2]
    top = routes.shape[3]
    capacity = 4
    x = inputs[0]
    own_shape = (here, tail, kv_width)

    normed, own = call(
        norm_kernel,
        (shaped((local_rows, width)), shaped((n_seq, 2) + own_shape)),
        x,
        gain_attn.reshape(1, width),
        generated_key_cache[0],
        generated_value_cache[0],
    )
    normed_all = lax.all_gather(normed, "seq", axis=0, tiled=True)
    cosine, sine = rotary_tables(rows, steps, keys * n_seq + tail)
    packed_rows = 2 * rows + rows // 2
    qkv = call(
        project_kernel,
        shaped((packed_rows, 128)),
        normed_all,
        w_query,
        key_projection_weight,
        value_projection_weight,
        cosine,
        sine,
    )
    qkv_all = lax.all_gather(qkv, "seq", axis=0, tiled=False)
    own_all = lax.all_to_all(own, "seq", split_axis=0, concat_axis=0, tiled=True)

    pairs = kv_width // 128
    partial, fresh_k, fresh_v = pl.pallas_call(
        attend_kernel,
        grid=(pairs,),
        out_shape=(
            shaped((n_seq, rows, 256)),
            shaped((local_rows, kv_width)),
            shaped((local_rows, kv_width)),
        ),
        in_specs=[
            scalars(),
            scalars(),
            scalars(),
            pl.BlockSpec((2, packed_rows, 128), lambda p: (p, 0, 0)),
            pl.BlockSpec((keys, 128), lambda p: (0, p)),
            pl.BlockSpec((keys, 128), lambda p: (0, p)),
            pl.BlockSpec((here, tail, 128), lambda p: (0, 0, p)),
            pl.BlockSpec((here, tail, 128), lambda p: (0, 0, p)),
        ],
        out_specs=(
            pl.BlockSpec((2, rows, 256), lambda p: (p, 0, 0)),
            pl.BlockSpec((local_rows, 128), lambda p: (0, p)),
            pl.BlockSpec((local_rows, 128), lambda p: (0, p)),
        ),
        scratch_shapes=[
            pltpu.VMEM((6 * rows, keys + 128), F32),
            pltpu.VMEM((6 * rows, keys + 128), BF16),
            pltpu.VMEM((8, keys), F32),
            pltpu.VMEM((rows, 128), F32),
        ],
        compiler_params=params(48),
        cost_estimate=pl.CostEstimate(
            flops=4 * 24 * rows * keys * HEAD,
            bytes_accessed=4 * keys * kv_width,
            transcendentals=24 * rows * keys,
        ),
    )(
        seq,
        parents[0],
        block_len,
        qkv_all,
        prompt_key_cache[0],
        prompt_value_cache[0],
        generated_key_cache[0],
        generated_value_cache[0],
    )
    parts = lax.all_to_all(partial, "seq", split_axis=0, concat_axis=0, tiled=True)
    sums = call(join_kernel, shaped((n_seq, local_rows, width)), parts, w_output)
    sums = lax.all_to_all(sums, "seq", split_axis=0, concat_axis=0, tiled=True)
    hidden, buffer, mix = call(
        functools.partial(dispatch_kernel, capacity),
        (
            shaped((local_rows, width), F32),
            shaped((n_req, capacity, width)),
            shaped((local_rows, n_req * capacity), F32),
        ),
        x,
        sums,
        gain_moe.reshape(1, width),
        routes[0],
        gate_weights[0],
    )
    buffer = lax.all_to_all(buffer, "req", split_axis=0, concat_axis=0, tiled=True)
    back = call(
        expert_kernel,
        shaped(buffer.shape),
        buffer,
        w_in,
        w_out,
        scratch=[pltpu.VMEM((n_req * capacity, width), F32)],
    )
    back = lax.all_to_all(back, "req", split_axis=0, concat_axis=0, tiled=True)
    mixed = call(
        mix_kernel,
        shaped((here, steps, width)),
        hidden,
        mix,
        back,
        scratch=[pltpu.VMEM((n_req * capacity, width), F32)],
    )
    final_k, final_v = call(
        final_kernel,
        (shaped((here, tail + steps, kv_width)),) * 2,
        seq,
        parents[0],
        own_all,
        fresh_k,
        fresh_v,
        ins=[scalars(), scalars(), whole(), whole(), whole()],
    )
    return (mixed[None], final_k[None], final_v[None])


def solution(mesh):
    placed = (
        P("req", "seq", None, None),
        P("req", None, None),
        P("req", "seq"),
        P("req", "seq", None),
        P("req", "seq", None),
        P("req", "seq", None, None),
        P("req", "seq", None, None),
        P(),
        P(),
        P(None, "seq"),
        P(None, "seq"),
        P(None, "seq"),
        P("seq", None),
        P("req", None, None),
        P("req", None, None),
        P("req", "seq", None, None),
        P("req", "seq", None, None),
    )
    return jax.shard_map(
        local,
        mesh=mesh,
        in_specs=placed,
        out_specs=(P("req", "seq", None, None),) * 3,
        check_vma=False,
    )
```

time: 908 us -> 146 us (0.16); the launches traced: 895 us -> 145 us
  blocking collectives: 452 us -> 66.9 us
  local copies, waits for them, and re-layouts: 168 us -> 15.1 us
  other arithmetic: 103 us -> 0 us
  matrix products: 64.6 us -> 0 us
  waiting for transfers between devices: 76.4 us -> 31.8 us
  Pallas kernels: 0 us -> 17.6 us
  between operations: 15.8 us -> 0.85 us
    all_gather x27 -> x1, blocking collectives: 418 us -> 14.9 us  [local(): qkv_all = lax.all_gather(qkv, 'seq', axis=0, tiled=False)]
    unnamed x2 -> x0, waiting for transfers between devices: 72.4 us -> none
    add x58 -> x0, other arithmetic: 67.5 us -> none  [the longest x28 46.6 us: join_partials(): first_scale[..., None] * first_part[2]]
    dot_general x37 -> x0, matrix products: 64.6 us -> none  [the longest x12 29.1 us: local_partial(): jnp.einsum('bgjd,kgd->bgjk', decode_query_step, shaped_keys, preferred_el...]
    exp x56 -> x0, local copies, waits for them, and re-layouts: 41.8 us -> none  [the longest x28 21 us: join_partials(): second_scale = jnp.exp(second_part[0] - row_max)]
    all_to_all x3, waiting for transfers between devices: 3.92 us -> 31.8 us  [the longest x1 14.7 us: local(): lax.all_to_all(own, 'seq', split_axis=0, concat_axis=0, tiled=True)]
    dynamic_slice x29 -> x0, local copies, waits for them, and re-layouts: 26.3 us -> none  [the longest x28 25.6 us: take(): lax.dynamic_index_in_dim(a, source, 0, False).astype(own.dtype)]
    gather x15 -> x0, local copies, waits for them, and re-layouts: 17.7 us -> none  [the longest x4 5.99 us: local(): beam_key_cache = jnp.take(received[0], chosen_rows, axis=0)]
  transfers between devices with their start and end apart: 4 -> 3, of which waited for: 2 -> 3; matrix products, arithmetic and copies ran while one was open for 10% -> 1% of each run, Pallas kernels for 0% -> 2%
where the time goes in v1:
time: 146 us; the launch traced here: 145 us
  blocking collectives  66.9 us (46%)
  waiting for transfers between devices  31.8 us (22%)
  Pallas kernels  17.6 us (12%)
  local copies, waits for them, and re-layouts  15.1 us (10%)
  starting transfers between devices  12.6 us (9%)
    all_gather x1, blocking collectives, local(): normed_all = lax.all_gather(normed, 'seq', axis=0, tiled=True)  18.2 us
    all_to_all x1, blocking collectives, local(): lax.all_to_all(partial, 'seq', split_axis=0, concat_axis=0, tiled=True)  17.3 us
    all_to_all x1, blocking collectives, local(): lax.all_to_all(buffer, 'req', split_axis=0, concat_axis=0, tiled=True)  16.6 us
    all_gather x1, blocking collectives, local(): qkv_all = lax.all_gather(qkv, 'seq', axis=0, tiled=False)  14.9 us
    all_to_all x1, waiting for transfers between devices, local(): lax.all_to_all(own, 'seq', split_axis=0, concat_axis=0, tiled=True)  14.7 us
    unnamed x55, local copies, waits for them, and re-layouts  14.4 us
    pallas_call x1, Pallas kernels, local(): pl.pallas_call(attend_kernel, grid=(pairs,), out_shape=(shaped((n_seq, ro...  11.4 us
    all_to_all x1, waiting for transfers between devices, local(): sums = lax.all_to_all(sums, 'seq', split_axis=0, concat_axis=0, tiled=True)  10.9 us
  transfers between devices with their start and end apart: 3, of which 3 were waited for; matrix products, arithmetic and copies ran while one was open for 1% of the time, Pallas kernels for 2%

profile of v1, /device:TPU:8, one launch (start us, length us, event | category | flops | bytes accessed | tf_op | source)
XLA Modules:
  0.0 145.0 jit_solution(16858928752409232019)
XLA Ops:
  0.6 0.7 reshape.16.gain_ref
  1.3 0.7 copy-done.4
  2.1 0.8 copy-done.10
  2.8 0.8 copy-done.12
  3.7 0.8 copy-done.3
  4.5 18.2 %all_gather.9.x_ref = bf16[64,1536]{1,0:T(8,128)(2,1)S(1)} all-gather(bf16[8,1536]{1,0:T(8,128)(2,1)S(1)} %get-tuple-element.13), channel_id=1, replica_groups=mesh['seq'=8,'req'=32] {'seq'}, dimensions={0}, use_global_device_ids=true | all-gather | bytes 221184 | tf_op jit(solution)/shard_map/all_gather | solution.py:378
  22.7 1.3 copy.22.wq_ref
  24.1 1.1 copy.23.wk_ref
  25.9 14.9 %all-gather = bf16[1280,128]{1,0:T(8,128)(2,1)S(1)} all-gather(bf16[160,128]{1,0:T(8,128)(2,1)S(1)} %shard_map.203), channel_id=2, replica_groups=mesh['seq'=8,'req'=32] {'seq'}, dimensions={0}, use_global_device_ids=true | all-gather | bytes 368640 | tf_op jit(solution)/shard_map/all_gather | solution.py:391
  40.8 1.6 %copy-done.20 = bf16[1,2048,512]{2,1,0:T(8,128)(2,1)S(1)} copy-done((bf16[1,2048,512]{2,1,0:T(8,128)(2,1)S(1)}, bf16[1,2048,512]{2,1,0:T(8,128)(2,1)}, u32[]{:S(2)}) %copy-start.20) | copy-done | bytes 2097176
  42.4 1.6 %copy-done.21 = bf16[1,2048,512]{2,1,0:T(8,128)(2,1)S(1)} copy-done((bf16[1,2048,512]{2,1,0:T(8,128)(2,1)S(1)}, bf16[1,2048,512]{2,1,0:T(8,128)(2,1)}, u32[]{:S(2)}) %copy-start.21) | copy-done | bytes 2097176
  44.0 11.4 %shard_map.204 = (bf16[8,64,256]{2,1,0:T(8,128)(2,1)S(1)}, bf16[8,512]{1,0:T(8,128)(2,1)S(1)}, bf16[8,512]{1,0:T(8,128)(2,1)S(1)}) custom-call(s32[1]{0:T(128)} %bitcast.1.seq_ref, s32[4,16]{1,0:T(4,128)S(1)} %bitcast.24, s32[1,16]{1,0:T(1,128)S(1)} %copy-done.22, bf16[8,160,128]{2,1,0:T(8,128)(2,1)S(1)} %bitcast.13, bf16[2048,512]{1,0:T(8,128)(2,1)S(1)} %bitcast.26, ...), custom_call_target="tpu_custom_call" | custom-call | flops 805306368 | bytes 4194304 | tf_op jit(solution)/shard_map/pallas_call | solution.py:395
  55.5 17.3 %all_to_all.25.part_ref = bf16[8,64,256]{2,1,0:T(8,128)(2,1)S(1)} all-to-all(bf16[8,64,256]{2,1,0:T(8,128)(2,1)S(1)} %get-tuple-element.14), channel_id=1, replica_groups=mesh['seq'=8,'req'=32] {'seq'}, dimensions={0} | all-to-all | bytes 524288 | tf_op jit(solution)/shard_map/all_to_all | solution.py:440
  72.7 1.4 shard_map.205
  74.1 3.4 %all-to-all-start.1 = ((bf16[8,8,1536]{2,1,0:T(8,128)(2,1)}), bf16[8,8,1536]{2,1,0:T(8,128)(2,1)S(1)}, u32[]{:S(2)}, u32[]{:S(2)}) async-start(bf16[8,8,1536]{2,1,0:T(8,128)(2,1)} %shard_map.205), calls=%async_computation.1 | async-start | bytes 393216 | tf_op jit(solution)/shard_map/all_to_all | solution.py:442
  77.6 10.9 %all-to-all-done.1.sums_ref = bf16[8,8,1536]{2,1,0:T(8,128)(2,1)S(1)} async-done(((bf16[8,8,1536]{2,1,0:T(8,128)(2,1)}), bf16[8,8,1536]{2,1,0:T(8,128)(2,1)S(1)}, u32[]{:S(2)}, u32[]{:S(2)}) %all-to-all-start.1) | async-done | bytes 196640 | tf_op jit(solution)/shard_map/all_to_all | solution.py:442
  88.5 0.5 shard_map.206
  89.0 0.6 copy-done.16
  89.6 16.6 %all_to_all.26.x_ref = bf16[32,4,1536]{2,1,0:T(4,128)(2,1)S(1)} all-to-all(bf16[32,4,1536]{2,1,0:T(4,128)(2,1)S(1)} %get-tuple-element.17), channel_id=1, replica_groups=mesh['seq'=8,'req'=32] {'req'}, dimensions={0} | all-to-all | bytes 786432 | tf_op jit(solution)/shard_map/all_to_all | solution.py:456
  106.2 4.1 %all-to-all-start.4 = ((bf16[8,2,2,16,512]{4,3,2,1,0:T(8,128)(2,1)}), bf16[8,2,2,16,512]{4,3,2,1,0:T(8,128)(2,1)}, u32[]{:S(2)}, u32[]{:S(2)}) async-start(bf16[8,2,2,16,512]{4,3,2,1,0:T(8,128)(2,1)} %copy-done.3), calls=%async_computation.4 | async-start | bytes 1048576 | tf_op jit(solution)/shard_map/all_to_all | solution.py:392
  110.3 1.4 copy-done.1
  111.7 1.7 %shard_map.207 = bf16[32,4,1536]{2,1,0:T(4,128)(2,1)} custom-call(bf16[32,4,1536]{2,1,0:T(4,128)(2,1)S(1)} %all_to_all.26.x_ref, bf16[1,1536,1024]{2,1,0:T(8,128)(2,1)S(1)} %copy-done, bf16[1,512,1536]{2,1,0:T(8,128)(2,1)S(1)} %copy-done.1), custom_call_target="tpu_custom_call" | custom-call | flops 1048576 | bytes 1048576 | tf_op jit(solution)/shard_map/pallas_call | solution.py:321
  113.4 14.7 %all-to-all-done.4.own_ref = bf16[8,2,2,16,512]{4,3,2,1,0:T(8,128)(2,1)} async-done(((bf16[8,2,2,16,512]{4,3,2,1,0:T(8,128)(2,1)}), bf16[8,2,2,16,512]{4,3,2,1,0:T(8,128)(2,1)}, u32[]{:S(2)}, u32[]{:S(2)}) %all-to-all-start.4) | async-done | bytes 524320 | tf_op jit(solution)/shard_map/all_to_all | solution.py:392
  128.1 5.1 %all-to-all-start.3 = ((bf16[32,4,1536]{2,1,0:T(4,128)(2,1)}), bf16[32,4,1536]{2,1,0:T(4,128)(2,1)S(1)}, u32[]{:S(2)}, u32[]{:S(2)}) async-start(bf16[32,4,1536]{2,1,0:T(4,128)(2,1)} %shard_map.207), calls=%async_computation.3 | async-start | bytes 786432 | tf_op jit(solution)/shard_map/all_to_all | solution.py:465
  133.2 0.7 copy-done.19
  133.9 1.1 shard_map.209
  135.0 0.6 copy.25
  135.6 0.6 copy.26
  136.3 6.2 %all-to-all-done.3.back_ref = bf16[32,4,1536]{2,1,0:T(4,128)(2,1)S(1)} async-done(((bf16[32,4,1536]{2,1,0:T(4,128)(2,1)}), bf16[32,4,1536]{2,1,0:T(4,128)(2,1)S(1)}, u32[]{:S(2)}, u32[]{:S(2)}) %all-to-all-start.3) | async-done | bytes 393248 | tf_op jit(solution)/shard_map/all_to_all | solution.py:465
  142.5 0.8 copy-done.9
  143.3 0.7 copy-done.17
  144.0 1.0 shard_map.208
  (43 shorter events, 0.9 us)
Async XLA Ops:
  1.3 0.7 copy-start.4
  2.1 0.8 copy-start.10
  2.8 0.8 copy-start.12
  3.6 21.6 %copy-start.23 = (bf16[1536,64]{0,1:T(8,128)(2,1)S(1)}, bf16[1536,64]{0,1:T(8,128)(2,1)}, u32[]{:S(2)}) copy-start(bf16[1536,64]{0,1:T(8,128)(2,1)} %param.30) | copy-start | bytes 589828
  3.6 21.9 %copy-start.6 = (f32[64,256]{1,0:T(8,128)S(1)}, f32[64,256]{1,0:T(8,128)}, u32[]{:S(2)}) copy-start(f32[64,256]{1,0:T(8,128)} %constant.10.clone.cos_ref) | copy-start | bytes 196612
  3.6 21.9 %copy-start.7 = (f32[64,256]{1,0:T(8,128)S(1)}, f32[64,256]{1,0:T(8,128)}, u32[]{:S(2)}) copy-start(f32[64,256]{1,0:T(8,128)} %constant.11.clone.sin_ref) | copy-start | bytes 196612
  3.7 0.8 copy-start.3
  22.7 18.1 %copy-start.11 = (bf16[1,2,16,512]{3,2,1,0:T(8,128)(2,1)S(1)}, bf16[1,2,16,512]{3,2,1,0:T(8,128)(2,1)}, u32[]{:S(2)}) copy-start(bf16[1,2,16,512]{3,2,1,0:T(8,128)(2,1)} %param.24) | copy-start | bytes 98308
  22.7 18.1 %copy-start.13 = (bf16[1,2,16,512]{3,2,1,0:T(8,128)(2,1)S(1)}, bf16[1,2,16,512]{3,2,1,0:T(8,128)(2,1)}, u32[]{:S(2)}) copy-start(bf16[1,2,16,512]{3,2,1,0:T(8,128)(2,1)} %param.25) | copy-start | bytes 98308
  22.7 18.1 %copy-start.18 = (s32[1,4,16]{2,1,0:T(4,128)S(1)}, s32[1,4,16]{2,1,0:T(4,128)}, u32[]{:S(2)}) copy-start(s32[1,4,16]{2,1,0:T(4,128)} %param.20) | copy-start | bytes 772
  22.7 18.1 %copy-start.22 = (s32[1,16]{1,0:T(1,128)S(1)}, s32[1,16]{1,0:T(1,128)}, u32[]{:S(2)}) copy-start(s32[1,16]{1,0:T(1,128)} %len_ref.1) | copy-start | bytes 196
  40.8 1.6 %copy-start.20 = (bf16[1,2048,512]{2,1,0:T(8,128)(2,1)S(1)}, bf16[1,2048,512]{2,1,0:T(8,128)(2,1)}, u32[]{:S(2)}) copy-start(bf16[1,2048,512]{2,1,0:T(8,128)(2,1)} %param.22) | copy-start | bytes 6291460
  42.4 1.6 %copy-start.21 = (bf16[1,2048,512]{2,1,0:T(8,128)(2,1)S(1)}, bf16[1,2048,512]{2,1,0:T(8,128)(2,1)}, u32[]{:S(2)}) copy-start(bf16[1,2048,512]{2,1,0:T(8,128)(2,1)} %param.23) | copy-start | bytes 6291460
  44.0 28.7 %copy-start.2 = (bf16[192,1536]{1,0:T(8,128)(2,1)S(1)}, bf16[192,1536]{1,0:T(8,128)(2,1)}, u32[]{:S(2)}) copy-start(bf16[192,1536]{1,0:T(8,128)(2,1)} %w_ref.1) | copy-start | bytes 1769476
  44.0 33.5 %copy-start.24 = (f32[1536]{0:T(1024)S(1)}, f32[1536]{0:T(1024)}, u32[]{:S(2)}) copy-start(f32[1536]{0:T(1024)} %param.27) | copy-start | bytes 18436
  44.0 44.5 %copy-start.5 = (bf16[1,2,4,1536]{3,2,1,0:T(4,128)(2,1)S(1)}, bf16[1,2,4,1536]{3,2,1,0:T(4,128)(2,1)}, u32[]{:S(2)}) copy-start(bf16[1,2,4,1536]{3,2,1,0:T(4,128)(2,1)} %param.19) | copy-start | bytes 73732
  44.0 44.5 %copy-start.14 = (s32[1,2,4,8]{3,2,1,0:T(4,128)S(1)}, s32[1,2,4,8]{3,2,1,0:T(4,128)}, u32[]{:S(2)}) copy-start(s32[1,2,4,8]{3,2,1,0:T(4,128)} %param.34) | copy-start | bytes 772
  44.0 44.5 %copy-start.15 = (f32[1,2,4,8]{3,2,1,0:T(4,128)S(1)}, f32[1,2,4,8]{3,2,1,0:T(4,128)}, u32[]{:S(2)}) copy-start(f32[1,2,4,8]{3,2,1,0:T(4,128)} %param.35) | copy-start | bytes 772
  55.5 54.9 %copy-start = (bf16[1,1536,1024]{2,1,0:T(8,128)(2,1)S(1)}, bf16[1,1536,1024]{2,1,0:T(8,128)(2,1)}, u32[]{:S(2)}) copy-start(bf16[1,1536,1024]{2,1,0:T(8,128)(2,1)} %w_in_ref.1) | copy-start | bytes 9437188
  74.1 14.3 %all-to-all-start.1 = ((bf16[8,8,1536]{2,1,0:T(8,128)(2,1)}), bf16[8,8,1536]{2,1,0:T(8,128)(2,1)S(1)}, u32[]{:S(2)}, u32[]{:S(2)}) async-start(bf16[8,8,1536]{2,1,0:T(8,128)(2,1)} %shard_map.205), calls=%async_computation.1 | async-start | bytes 393216 | tf_op jit(solution)/shard_map/all_to_all | solution.py:442
  89.0 0.6 copy-start.16
  89.6 16.6 %copy-start.8 = (f32[8,1536]{1,0:T(8,128)}, f32[8,1536]{1,0:T(8,128)S(1)}, u32[]{:S(2)}) copy-start(f32[8,1536]{1,0:T(8,128)S(1)} %get-tuple-element.15.hidden_ref) | copy-start | bytes 147460
  106.2 21.9 %all-to-all-start.4 = ((bf16[8,2,2,16,512]{4,3,2,1,0:T(8,128)(2,1)}), bf16[8,2,2,16,512]{4,3,2,1,0:T(8,128)(2,1)}, u32[]{:S(2)}, u32[]{:S(2)}) async-start(bf16[8,2,2,16,512]{4,3,2,1,0:T(8,128)(2,1)} %copy-done.3), calls=%async_computation.4 | async-start | bytes 1048576 | tf_op jit(solution)/shard_map/all_to_all | solution.py:392
  110.3 1.4 copy-start.1
  128.1 14.4 %all-to-all-start.3 = ((bf16[32,4,1536]{2,1,0:T(4,128)(2,1)}), bf16[32,4,1536]{2,1,0:T(4,128)(2,1)S(1)}, u32[]{:S(2)}, u32[]{:S(2)}) async-start(bf16[32,4,1536]{2,1,0:T(4,128)(2,1)} %shard_map.207), calls=%async_computation.3 | async-start | bytes 786432 | tf_op jit(solution)/shard_map/all_to_all | solution.py:465
  133.2 0.7 copy-start.19
  142.5 0.8 copy-start.9
  143.3 0.7 copy-start.17

commit v2 on v1

--- a/solution.py
+++ b/solution.py
@@ -47,33 +47,37 @@
     return x * lax.rsqrt(mean_sq + EPSILON) * gain
 
 
-def norm_kernel(x_ref, gain_ref, own_k_ref, own_v_ref, out_ref, own_ref):
+def norm_kernel(x_ref, gain_ref, out_ref):
     beams, steps = x_ref.shape[0], x_ref.shape[1]
-    for b in range(beams):
-        rows = norm(x_ref[b].astype(F32), gain_ref[...])
-        out_ref[b * steps : (b + 1) * steps, :] = rows.astype(BF16)
-    for d in range(own_ref.shape[0]):
-        own_ref[d, 0] = own_k_ref[...]
-        own_ref[d, 1] = own_v_ref[...]
+    gain = gain_ref[...].reshape(1, -1)
+    rows = [norm(x_ref[b].astype(F32), gain) for b in range(beams)]
+    rows = jnp.concatenate(rows, axis=0).astype(BF16)
+    for d in range(out_ref.shape[0]):
+        out_ref[d] = rows
+
+
+def pack_kernel(order_ref, own_k_ref, own_v_ref, out_ref):
+    out_ref[0] = own_k_ref[...]
+    out_ref[1] = own_v_ref[...]
 
 
 def project_kernel(x_ref, wq_ref, wk_ref, wv_ref, cos_ref, sin_ref, out_ref):
-    x = x_ref[...]
-    rows = x.shape[0]
-    q = dot(x, wq_ref[...]) * SCALE
-    k = dot(x, wk_ref[...])
-    v = dot(x, wv_ref[...])
+    rows = x_ref.shape[0] * x_ref.shape[1]
+    x = x_ref[...].reshape(rows, x_ref.shape[2])
+    q = dot_t(x, wq_ref[...]) * SCALE
+    k = dot_t(x, wk_ref[...])
+    v = dot_t(x, wv_ref[...])
     y = jnp.concatenate([q, k], axis=1)
     width = y.shape[1]
     half = HEAD // 2
     first = lanes(y.shape) % HEAD < half
     turned = jnp.where(first, pltpu.roll(y, width - half, 1), pltpu.roll(y, half, 1))
     y = (y * cos_ref[...] + turned * sin_ref[...]).astype(BF16)
-    out_ref[0:rows, :] = y[:, 0:128]
-    out_ref[rows : 2 * rows, :] = y[:, 128:256]
-    out_ref[2 * rows : 2 * rows + rows // 2, :] = jnp.concatenate(
-        [v[0 : rows // 2], v[rows // 2 :]], axis=1
-    ).astype(BF16)
+    v = jnp.concatenate([v[0 : rows // 2], v[rows // 2 :]], axis=1).astype(BF16)
+    for d in range(out_ref.shape[0]):
+        out_ref[d, 0:rows, :] = y[:, 0:128]
+        out_ref[d, rows : 2 * rows, :] = y[:, 128:256]
+        out_ref[d, 2 * rows : 2 * rows + rows // 2, :] = v
 
 
 def lookup(parents_ref, step, cur, beams):
@@ -83,10 +87,36 @@
     return found
 
 
+def mask_kernel(tail, here, order_ref, seq_ref, parents_ref, len_ref, bias_ref, extra_ref):
+    steps, beams = parents_ref.shape
+    own_keys = here * tail
+    seq = seq_ref[0]
+    shape = extra_ref.shape
+    lane = lanes(shape)
+    spot = lanes((bias_ref.shape[0], BLK))
+    for j in range(bias_ref.shape[1] // BLK):
+        bias_ref[:, j * BLK : (j + 1) * BLK] = jnp.where(spot < len_ref[0, j], 0.0, FILL)
+    row = lax.broadcasted_iota(jnp.int32, shape, 0)
+    step = row % steps
+    cur = row // steps
+    fresh = lane - own_keys
+    key_beam = fresh // steps
+    key_step = fresh % steps
+    live = jnp.zeros(shape, jnp.int32)
+    for s in range(steps - 1, -1, -1):
+        hit = (key_step == s) & (cur == key_beam) & (step >= s) & (key_beam // here == seq)
+        live = live | jnp.where((fresh >= 0) & hit, 1, 0)
+        cur = jnp.where(step >= s, lookup(parents_ref, s, cur, beams), cur)
+    own_hit = (lane < own_keys) & (cur == seq * here + lane // tail)
+    live = live | jnp.where(own_hit, 1, 0)
+    extra_ref[...] = jnp.where(live > 0, 0.0, FILL)
+
+
 def attend_kernel(
     seq_ref,
     parents_ref,
-    len_ref,
+    bias_ref,
+    extra_ref,
     qkv_ref,
     k_ref,
     v_ref,
@@ -97,13 +127,10 @@
     fresh_v_ref,
     s_ref,
     p_ref,
-    bias_ref,
-    extra_ref,
 ):
     steps, beams = parents_ref.shape
     rows = steps * beams
     keys = k_ref.shape[0]
-    blocks = keys // BLK
     here = own_k_ref.shape[0]
     tail = own_k_ref.shape[1]
     own_keys = here * tail
@@ -111,26 +138,6 @@
     shape = (rows, 128)
     lane = lanes(shape)
     low = lane < HEAD
-
-    @pl.when(pl.program_id(0) == 0)
-    def _():
-        spot = lanes((8, BLK))
-        for j in range(blocks):
-            bias_ref[:, j * BLK : (j + 1) * BLK] = jnp.where(spot < len_ref[0, j], 0.0, FILL)
-        row = lax.broadcasted_iota(jnp.int32, shape, 0)
-        step = row % steps
-        cur = row // steps
-        fresh = lane - own_keys
-        key_beam = fresh // steps
-        key_step = fresh % steps
-        live = jnp.zeros(shape, jnp.int32)
-        for s in range(steps - 1, -1, -1):
-            hit = (key_step == s) & (cur == key_beam) & (step >= s) & (key_beam // here == seq)
-            live = live | jnp.where((fresh >= 0) & hit, 1, 0)
-            cur = jnp.where(step >= s, lookup(parents_ref, s, cur, beams), cur)
-        own_hit = (lane < own_keys) & (cur == seq * here + lane // tail)
-        live = live | jnp.where(own_hit, 1, 0)
-        extra_ref[...] = jnp.where(live > 0, 0.0, FILL)
 
     def swap(x):
         return pltpu.roll(x, HEAD, 1)
@@ -230,20 +237,10 @@
         out_ref[s] = out[s * each : (s + 1) * each, :]
 
 
-def dispatch_kernel(
-    capacity, x_ref, sums_ref, gain_ref, route_ref, gate_ref, hidden_ref, out_ref, mix_ref
-):
-    beams, steps = x_ref.shape[0], x_ref.shape[1]
+def route_kernel(capacity, order_ref, route_ref, gate_ref, place_ref, mix_ref):
+    beams, steps = route_ref.shape[0], route_ref.shape[1]
     rows = beams * steps
-    total = sums_ref[0].astype(F32)
-    for s in range(1, sums_ref.shape[0]):
-        total = total + sums_ref[s].astype(F32)
-    inputs = jnp.concatenate([x_ref[b].astype(F32) for b in range(beams)], axis=0)
-    hidden = inputs + total
-    hidden_ref[...] = hidden
-    expert_in = norm(hidden, gain_ref[...]).astype(BF16)
-    experts = out_ref.shape[0]
-    slots = experts * capacity
+    slots = place_ref.shape[0]
     slot = lanes((rows, slots))
     routes = jnp.concatenate([route_ref[b] for b in range(beams)], axis=0)
     gates = jnp.concatenate([gate_ref[b] for b in range(beams)], axis=0)
@@ -259,8 +256,20 @@
     rank = dot(earlier.astype(BF16), named.astype(BF16))
     placed = (named > 0.0) & (rank == (slot % capacity).astype(F32))
     mix_ref[...] = jnp.where(placed, gate, 0.0)
-    place = jnp.where(placed, 1.0, 0.0).T.astype(BF16)
-    buffer = dot(place, expert_in)
+    place_ref[...] = jnp.where(placed, 1.0, 0.0).T.astype(BF16)
+
+
+def dispatch_kernel(x_ref, sums_ref, gain_ref, place_ref, hidden_ref, out_ref):
+    beams = x_ref.shape[0]
+    total = sums_ref[0].astype(F32)
+    for s in range(1, sums_ref.shape[0]):
+        total = total + sums_ref[s].astype(F32)
+    inputs = jnp.concatenate([x_ref[b].astype(F32) for b in range(beams)], axis=0)
+    hidden = inputs + total
+    hidden_ref[...] = hidden
+    expert_in = norm(hidden, gain_ref[...].reshape(1, -1)).astype(BF16)
+    buffer = dot(place_ref[...], expert_in)
+    experts, capacity = out_ref.shape[0], out_ref.shape[1]
     for e in range(experts):
         out_ref[e] = buffer[e * capacity : (e + 1) * capacity, :].astype(BF16)
 
@@ -294,17 +303,25 @@
         out_ref[b] = total[b * steps : (b + 1) * steps, :].astype(BF16)
 
 
-def final_kernel(seq_ref, parents_ref, own_ref, fresh_k_ref, fresh_v_ref, k_ref, v_ref):
+def final_kernel(seq_ref, parents_ref, fresh_k_ref, fresh_v_ref, *refs):
+    own_refs, (k_ref, v_ref) = refs[:-2], refs[-2:]
     steps = parents_ref.shape[0]
-    here, tail = own_ref.shape[2], own_ref.shape[3]
+    here, tail = own_refs[0].shape[1], own_refs[0].shape[2]
+    seq = seq_ref[0]
     for i in range(here):
-        beam = seq_ref[0] * here + i
+        beam = seq * here + i
         for s in range(steps - 1, -1, -1):
             beam = parents_ref[s, beam]
-        k_ref[i, 0:tail, :] = own_ref[beam // here, 0, beam % here]
-        v_ref[i, 0:tail, :] = own_ref[beam // here, 1, beam % here]
-        k_ref[i, tail:, :] = fresh_k_ref[i * steps : (i + 1) * steps, :]
-        v_ref[i, tail:, :] = fresh_v_ref[i * steps : (i + 1) * steps, :]
+        apart = lax.bitwise_xor(beam // here, seq)
+        for j, own_ref in enumerate(own_refs):
+
+            @pl.when(apart == j)
+            def _():
+                k_ref[0:tail, i, :] = own_ref[0, beam % here]
+                v_ref[0:tail, i, :] = own_ref[1, beam % here]
+
+        k_ref[tail:, i, :] = fresh_k_ref[i * steps : (i + 1) * steps, :]
+        v_ref[tail:, i, :] = fresh_v_ref[i * steps : (i + 1) * steps, :]
 
 
 def rotary_tables(rows, steps, start):
@@ -317,9 +334,10 @@
     return cosine, sine
 
 
-def call(kernel, outs, *args, ins=None, scratch=(), mib=48, flops=0, moved=0):
+def call(kernel, outs, *args, ins=None, scratch=(), mib=48, flops=0, moved=0, grid=()):
     return pl.pallas_call(
         kernel,
+        grid=grid,
         out_shape=outs,
         in_specs=ins or [whole()] * len(args),
         out_specs=jax.tree.map(lambda _: whole(), outs),
@@ -365,31 +383,51 @@
     top = routes.shape[3]
     capacity = 4
     x = inputs[0]
-    own_shape = (here, tail, kv_width)
-
-    normed, own = call(
+    anywhere = pl.BlockSpec(memory_space=pl.ANY)
+
+    def exchange(a, axis):
+        return lax.all_to_all(a, axis, split_axis=0, concat_axis=0, tiled=True)
+
+    def apart(a, distance):
+        return lax.ppermute(a, "seq", [(i, i ^ distance) for i in range(n_seq)])
+
+    normed = call(
         norm_kernel,
-        (shaped((local_rows, width)), shaped((n_seq, 2) + own_shape)),
+        shaped((n_seq, local_rows, width)),
         x,
-        gain_attn.reshape(1, width),
-        generated_key_cache[0],
-        generated_value_cache[0],
-    )
-    normed_all = lax.all_gather(normed, "seq", axis=0, tiled=True)
+        gain_attn,
+        grid=(1,),
+        ins=[
+            pl.BlockSpec((here, steps, width), lambda i: (0, 0, 0)),
+            pl.BlockSpec((width,), lambda i: (0,)),
+        ],
+        mib=60,
+    )
+    normed_all = exchange(normed, "seq")
+    bias, extra = call(
+        functools.partial(mask_kernel, tail, here),
+        (shaped((8, keys), F32), shaped((rows, 128), F32)),
+        normed,
+        seq,
+        parents[0],
+        block_len,
+        ins=[anywhere, scalars(), scalars(), scalars()],
+        mib=8,
+    )
     cosine, sine = rotary_tables(rows, steps, keys * n_seq + tail)
     packed_rows = 2 * rows + rows // 2
     qkv = call(
         project_kernel,
-        shaped((packed_rows, 128)),
+        shaped((n_seq, packed_rows, 128)),
         normed_all,
-        w_query,
-        key_projection_weight,
-        value_projection_weight,
+        w_query.T,
+        key_projection_weight.T,
+        value_projection_weight.T,
         cosine,
         sine,
-    )
-    qkv_all = lax.all_gather(qkv, "seq", axis=0, tiled=False)
-    own_all = lax.all_to_all(own, "seq", split_axis=0, concat_axis=0, tiled=True)
+        mib=16,
+    )
+    qkv_all = exchange(qkv, "seq")
 
     pairs = kv_width // 128
     partial, fresh_k, fresh_v = pl.pallas_call(
@@ -403,7 +441,8 @@
         in_specs=[
             scalars(),
             scalars(),
-            scalars(),
+            whole(),
+            whole(),
             pl.BlockSpec((2, packed_rows, 128), lambda p: (p, 0, 0)),
             pl.BlockSpec((keys, 128), lambda p: (0, p)),
             pl.BlockSpec((keys, 128), lambda p: (0, p)),
@@ -418,10 +457,8 @@
         scratch_shapes=[
             pltpu.VMEM((6 * rows, keys + 128), F32),
             pltpu.VMEM((6 * rows, keys + 128), BF16),
-            pltpu.VMEM((8, keys), F32),
-            pltpu.VMEM((rows, 128), F32),
         ],
-        compiler_params=params(48),
+        compiler_params=params(60),
         cost_estimate=pl.CostEstimate(
             flops=4 * 24 * rows * keys * HEAD,
             bytes_accessed=4 * keys * kv_width,
@@ -430,58 +467,84 @@
     )(
         seq,
         parents[0],
-        block_len,
+        bias,
+        extra,
         qkv_all,
         prompt_key_cache[0],
         prompt_value_cache[0],
         generated_key_cache[0],
         generated_value_cache[0],
     )
-    parts = lax.all_to_all(partial, "seq", split_axis=0, concat_axis=0, tiled=True)
-    sums = call(join_kernel, shaped((n_seq, local_rows, width)), parts, w_output)
-    sums = lax.all_to_all(sums, "seq", split_axis=0, concat_axis=0, tiled=True)
-    hidden, buffer, mix = call(
-        functools.partial(dispatch_kernel, capacity),
-        (
-            shaped((local_rows, width), F32),
-            shaped((n_req, capacity, width)),
-            shaped((local_rows, n_req * capacity), F32),
-        ),
+    parts = exchange(partial, "seq")
+    sums = call(join_kernel, shaped((n_seq, local_rows, width)), parts, w_output, mib=16)
+    slots = n_req * capacity
+    place, mix = call(
+        functools.partial(route_kernel, capacity),
+        (shaped((slots, local_rows)), shaped((local_rows, slots), F32)),
+        sums,
+        routes[0],
+        gate_weights[0],
+        ins=[anywhere, whole(), whole()],
+        mib=8,
+    )
+    sums = exchange(sums, "seq")
+    hidden, buffer = call(
+        dispatch_kernel,
+        (shaped((local_rows, width), F32), shaped((n_req, capacity, width))),
         x,
         sums,
-        gain_moe.reshape(1, width),
-        routes[0],
-        gate_weights[0],
-    )
-    buffer = lax.all_to_all(buffer, "req", split_axis=0, concat_axis=0, tiled=True)
+        gain_moe,
+        place,
+        mib=16,
+    )
+    own = call(
+        pack_kernel,
+        shaped((2, here, tail, kv_width)),
+        buffer,
+        generated_key_cache[0],
+        generated_value_cache[0],
+        ins=[anywhere, whole(), whole()],
+        mib=8,
+    )
+    even = [own] + [apart(own, k) for k in range(2, n_seq, 2)]
+    odd = [apart(a, 1) for a in even]
+    owns = [a for pair in zip(even, odd) for a in pair]
+    buffer = exchange(buffer, "req")
     back = call(
         expert_kernel,
         shaped(buffer.shape),
         buffer,
         w_in,
         w_out,
-        scratch=[pltpu.VMEM((n_req * capacity, width), F32)],
-    )
-    back = lax.all_to_all(back, "req", split_axis=0, concat_axis=0, tiled=True)
+        scratch=[pltpu.VMEM((slots, width), F32)],
+        mib=16,
+    )
+    back = exchange(back, "req")
     mixed = call(
         mix_kernel,
         shaped((here, steps, width)),
         hidden,
         mix,
         back,
-        scratch=[pltpu.VMEM((n_req * capacity, width), F32)],
+        scratch=[pltpu.VMEM((slots, width), F32)],
+        mib=16,
     )
     final_k, final_v = call(
         final_kernel,
-        (shaped((here, tail + steps, kv_width)),) * 2,
+        (shaped((tail + steps, here, kv_width)),) * 2,
         seq,
         parents[0],
-        own_all,
         fresh_k,
         fresh_v,
-        ins=[scalars(), scalars(), whole(), whole(), whole()],
-    )
-    return (mixed[None], final_k[None], final_v[None])
+        *owns,
+        ins=[scalars(), scalars()] + [whole()] * (2 + n_seq),
+        mib=16,
+    )
+    return (
+        mixed[None],
+        final_k.transpose(1, 0, 2)[None],
+        final_v.transpose(1, 0, 2)[None],
+    )
 
 
 def solution(mesh):

time: 146 us -> 139 us (0.952)
  blocking collectives: 66.9 us -> 52.2 us
  waiting for transfers between devices: 31.8 us -> 25.4 us
  starting transfers between devices: 12.6 us -> 18.9 us
  Pallas kernels: 17.6 us -> 21 us
  local copies, waits for them, and re-layouts: 15.1 us -> 18.4 us
    all_gather x2 -> x0, blocking collectives: 33.1 us -> none  [the longest x1 18.2 us: local(): normed_all = lax.all_gather(normed, 'seq', axis=0, tiled=True)]
    all_to_all x2 -> x3, blocking collectives: 33.8 us -> 52.2 us  [exchange(): return lax.all_to_all(a, axis, split_axis=0, concat_axis=0, tiled=True)]
    all_to_all x3, waiting for transfers between devices: 31.8 us -> 21.2 us  [exchange(): return lax.all_to_all(a, axis, split_axis=0, concat_axis=0, tiled=True)]
    ppermute x0 -> x7, starting transfers between devices: none -> 7.23 us  [apart(): return lax.ppermute(a, 'seq', [(i, i ^ distance) for i in range(n_seq)])]
    ppermute x0 -> x7, waiting for transfers between devices: none -> 4.26 us  [apart(): return lax.ppermute(a, 'seq', [(i, i ^ distance) for i in range(n_seq)])]
    unnamed x55 -> x64, local copies, waits for them, and re-layouts: 14.4 us -> 18.4 us
    pallas_call x7 -> x10, Pallas kernels: 6.19 us -> 8.84 us  [call(): pl.pallas_call(kernel, grid=grid, out_shape=outs, in_specs=ins or [whole(...]
  transfers between devices with their start and end apart: 3 -> 10, of which waited for: 3 -> 6; matrix products, arithmetic and copies ran while one was open for 1% -> 0% of each run, Pallas kernels for 2% -> 2%
where the time goes in v2:
time: 139 us; the launch traced here: 137 us
  blocking collectives  52.2 us (38%)
  waiting for transfers between devices  25.4 us (18%)
  Pallas kernels  21 us (15%)
  starting transfers between devices  18.9 us (14%)
  local copies, waits for them, and re-layouts  18.4 us (13%)
    all_to_all x3, blocking collectives, exchange(): return lax.all_to_all(a, axis, split_axis=0, concat_axis=0, tiled=True)  52.2 us
    all_to_all x3, waiting for transfers between devices, exchange(): return lax.all_to_all(a, axis, split_axis=0, concat_axis=0, tiled=True)  21.2 us
    unnamed x64, local copies, waits for them, and re-layouts  18.4 us
    pallas_call x1, Pallas kernels, local(): pl.pallas_call(attend_kernel, grid=(pairs,), out_shape=(shaped((n_seq, ro...  12.2 us
    all_to_all x3, starting transfers between devices, exchange(): return lax.all_to_all(a, axis, split_axis=0, concat_axis=0, tiled=True)  11.6 us
    pallas_call x10, Pallas kernels, call(): pl.pallas_call(kernel, grid=grid, out_shape=outs, in_specs=ins or [whole(...  8.84 us
    ppermute x7, starting transfers between devices, apart(): return lax.ppermute(a, 'seq', [(i, i ^ distance) for i in range(n_seq)])  7.23 us
    ppermute x7, waiting for transfers between devices, apart(): return lax.ppermute(a, 'seq', [(i, i ^ distance) for i in range(n_seq)])  4.26 us
  transfers between devices with their start and end apart: 10, of which 6 were waited for; matrix products, arithmetic and copies ran while one was open for 0% of the time, Pallas kernels for 2%

profile of v2, /device:TPU:8, one launch (start us, length us, event | category | flops | bytes accessed | tf_op | source)
XLA Modules:
  0.0 136.8 jit_solution(10667454709459927297)
XLA Ops:
  0.7 1.5 %shard_map.202.order_ref = bf16[8,8,1536]{2,1,0:T(8,128)(2,1)} custom-call(bf16[2,4,1536]{2,1,0:T(4,128)(2,1)} %bitcast.22, f32[1536]{0:T(1024)} %gain_ref.2), custom_call_target="tpu_custom_call" | custom-call | flops 1048576 | bytes 1048576 | tf_op jit(solution)/shard_map/pallas_call | solution.py:338
  2.2 19.6 %all_to_all.30.x_ref = bf16[8,8,1536]{2,1,0:T(8,128)(2,1)S(1)} all-to-all(bf16[8,8,1536]{2,1,0:T(8,128)(2,1)} %shard_map.202.order_ref), channel_id=1, replica_groups=mesh['seq'=8,'req'=32] {'seq'}, dimensions={0} | all-to-all | bytes 393216 | tf_op jit(solution)/shard_map/all_to_all | solution.py:389
  21.8 1.1 copy-done.6
  22.9 0.9 copy-done.8
  23.8 0.9 copy-done.9
  24.8 0.8 copy-done.11
  25.6 0.8 copy-done.12
  26.4 1.2 shard_map.204
  27.7 3.4 %all-to-all-start.1 = ((bf16[8,160,128]{2,1,0:T(8,128)(2,1)}), bf16[8,160,128]{2,1,0:T(8,128)(2,1)S(1)}, u32[]{:S(2)}, u32[]{:S(2)}) async-start(bf16[8,160,128]{2,1,0:T(8,128)(2,1)} %shard_map.204), calls=%async_computation.1 | async-start | bytes 655360 | tf_op jit(solution)/shard_map/all_to_all | solution.py:389
  31.1 0.8 shard_map.203
  33.1 11.7 %all-to-all-done.1.qkv_ref = bf16[8,160,128]{2,1,0:T(8,128)(2,1)S(1)} async-done(((bf16[8,160,128]{2,1,0:T(8,128)(2,1)}), bf16[8,160,128]{2,1,0:T(8,128)(2,1)S(1)}, u32[]{:S(2)}, u32[]{:S(2)}) %all-to-all-start.1) | async-done | bytes 327712 | tf_op jit(solution)/shard_map/all_to_all | solution.py:389
  45.6 12.2 %shard_map.205 = (bf16[8,64,256]{2,1,0:T(8,128)(2,1)}, bf16[8,512]{1,0:T(8,128)(2,1)}, bf16[8,512]{1,0:T(8,128)(2,1)}) custom-call(s32[1]{0:T(128)} %bitcast.1.seq_ref, s32[4,16]{1,0:T(4,128)} %bitcast.28, f32[8,2048]{1,0:T(8,128)} %copy-done.29, f32[64,128]{1,0:T(8,128)} %copy-done.30, bf16[8,160,128]{2,1,0:T(8,128)(2,1)} %copy-done.31, ...), custom_call_target="tpu_custom_call" | custom-call | flops 805306368 | bytes 4194304 | tf_op jit(solution)/shard_map/pallas_call | solution.py:433
  57.8 16.0 %all_to_all.31.part_ref = bf16[8,64,256]{2,1,0:T(8,128)(2,1)S(1)} all-to-all(bf16[8,64,256]{2,1,0:T(8,128)(2,1)} %get-tuple-element.16), channel_id=1, replica_groups=mesh['seq'=8,'req'=32] {'seq'}, dimensions={0} | all-to-all | bytes 524288 | tf_op jit(solution)/shard_map/all_to_all | solution.py:389
  73.9 1.1 copy-done.7
  74.9 1.4 %shard_map.206.order_ref = bf16[8,8,1536]{2,1,0:T(8,128)(2,1)} custom-call(bf16[8,64,256]{2,1,0:T(8,128)(2,1)S(1)} %all_to_all.31.part_ref, bf16[192,1536]{1,0:T(8,128)(2,1)S(1)} %copy-done.7), custom_call_target="tpu_custom_call" | custom-call | flops 1048576 | bytes 1048576 | tf_op jit(solution)/shard_map/pallas_call | solution.py:338
  76.3 3.4 %all-to-all-start.3 = ((bf16[8,8,1536]{2,1,0:T(8,128)(2,1)}), bf16[8,8,1536]{2,1,0:T(8,128)(2,1)S(1)}, u32[]{:S(2)}, u32[]{:S(2)}) async-start(bf16[8,8,1536]{2,1,0:T(8,128)(2,1)} %shard_map.206.order_ref), calls=%async_computation.3 | async-start | bytes 393216 | tf_op jit(solution)/shard_map/all_to_all | solution.py:389
  81.2 9.4 %all-to-all-done.3.sums_ref = bf16[8,8,1536]{2,1,0:T(8,128)(2,1)S(1)} async-done(((bf16[8,8,1536]{2,1,0:T(8,128)(2,1)}), bf16[8,8,1536]{2,1,0:T(8,128)(2,1)S(1)}, u32[]{:S(2)}, u32[]{:S(2)}) %all-to-all-start.3) | async-done | bytes 196640 | tf_op jit(solution)/shard_map/all_to_all | solution.py:389
  91.3 0.9 copy-done.5
  92.3 0.7 copy-done.10
  93.0 0.8 copy-done.18
  94.7 16.6 %all_to_all.32.x_ref = bf16[32,4,1536]{2,1,0:T(4,128)(2,1)S(1)} all-to-all(bf16[32,4,1536]{2,1,0:T(4,128)(2,1)S(1)} %get-tuple-element.20.order_ref), channel_id=1, replica_groups=mesh['seq'=8,'req'=32] {'req'}, dimensions={0} | all-to-all | bytes 786432 | tf_op jit(solution)/shard_map/all_to_all | solution.py:389
  111.3 1.4 %copy-done.2 = bf16[1,512,1536]{2,1,0:T(8,128)(2,1)S(1)} copy-done((bf16[1,512,1536]{2,1,0:T(8,128)(2,1)S(1)}, bf16[1,512,1536]{2,1,0:T(8,128)(2,1)}, u32[]{:S(2)}) %copy-start.2) | copy-done | bytes 1572888
  112.7 0.9 shard_map.209
  114.4 4.8 %all-to-all-start.5 = ((bf16[32,4,1536]{2,1,0:T(4,128)(2,1)}), bf16[32,4,1536]{2,1,0:T(4,128)(2,1)S(1)}, u32[]{:S(2)}, u32[]{:S(2)}) async-start(bf16[32,4,1536]{2,1,0:T(4,128)(2,1)} %copy-done.3), calls=%async_computation.5 | async-start | bytes 786432 | tf_op jit(solution)/shard_map/all_to_all | solution.py:389
  119.2 0.7 copy-done.15
  120.0 0.8 copy-done.16
  121.4 2.3 %collective-permute-start.3 = (bf16[2,2,16,512]{3,2,1,0:T(8,128)(2,1)S(1)}, bf16[2,2,16,512]{3,2,1,0:T(8,128)(2,1)S(1)}, u32[]{:S(2)}, u32[]{:S(2)}) collective-permute-start(bf16[2,2,16,512]{3,2,1,0:T(8,128)(2,1)S(1)} %shard_map.211.refs_0_), channel_id=1, source_target_pairs={{0,128},{32,160},{64,192},{96,224},{128,0},{160,32},{192,64},{224,... | collective-permute-start | bytes 196616 | tf_op jit(solution)/shard_map/ppermute | solution.py:392
  123.7 3.5 %collective-permute-start.5 = (bf16[2,2,16,512]{3,2,1,0:T(8,128)(2,1)S(1)}, bf16[2,2,16,512]{3,2,1,0:T(8,128)(2,1)S(1)}, u32[]{:S(2)}, u32[]{:S(2)}) collective-permute-start(bf16[2,2,16,512]{3,2,1,0:T(8,128)(2,1)S(1)} %shard_map.211.refs_0_), channel_id=1, source_target_pairs={{0,192},{32,224},{64,128},{96,160},{128,64},{160,96},{192,0},{224,... | collective-permute-start | bytes 196616 | tf_op jit(solution)/shard_map/ppermute | solution.py:392
  127.7 2.9 %collective-permute-done.3.refs_4_ = bf16[2,2,16,512]{3,2,1,0:T(8,128)(2,1)S(1)} collective-permute-done((bf16[2,2,16,512]{3,2,1,0:T(8,128)(2,1)S(1)}, bf16[2,2,16,512]{3,2,1,0:T(8,128)(2,1)S(1)}, u32[]{:S(2)}, u32[]{:S(2)}) %collective-permute-start.3) | collective-permute-done | bytes 65568 | tf_op jit(solution)/shard_map/ppermute | solution.py:392
  132.9 1.4 %shard_map.212 = (bf16[20,2,512]{2,1,0:T(2,128)(2,1)}, bf16[20,2,512]{2,1,0:T(2,128)(2,1)}) custom-call(s32[1]{0:T(128)} %bitcast.1.seq_ref, s32[4,16]{1,0:T(4,128)S(1)} %bitcast.30, bf16[8,512]{1,0:T(8,128)(2,1)S(1)} %copy-done.19, bf16[8,512]{1,0:T(8,128)(2,1)S(1)} %copy-done.20, bf16[2,2,16,512]{3,2,1,0:T(8,128)(2,1)S(1)} %shard_map.211.refs_0_, ...), custom_call_target="tpu_custom_call" | custom-call | flops 1048576 | bytes 1048576 | tf_op jit(solution)/shard_map/pallas_call | solution.py:338
  134.3 0.8 copy-done.14
  135.8 1.0 shard_map.210
  (66 shorter events, 10.0 us)
Async XLA Ops:
  0.6 30.5 %copy-start.21 = (s32[1,4,16]{2,1,0:T(4,128)S(1)}, s32[1,4,16]{2,1,0:T(4,128)}, u32[]{:S(2)}) copy-start(s32[1,4,16]{2,1,0:T(4,128)} %param.20) | copy-start | bytes 772
  0.6 30.5 %copy-start.28 = (s32[1,16]{1,0:T(1,128)S(1)}, s32[1,16]{1,0:T(1,128)}, u32[]{:S(2)}) copy-start(s32[1,16]{1,0:T(1,128)} %len_ref.1) | copy-start | bytes 196
  2.2 28.9 %copy-start.1 = (bf16[8,8,1536]{2,1,0:T(8,128)(2,1)S(1)}, bf16[8,8,1536]{2,1,0:T(8,128)(2,1)}, u32[]{:S(2)}) copy-start(bf16[8,8,1536]{2,1,0:T(8,128)(2,1)} %shard_map.202.order_ref) | copy-start | bytes 589828
  21.8 1.1 copy-start.6
  22.9 0.9 copy-start.8
  23.8 0.9 copy-start.9
  24.8 0.8 copy-start.11
  25.6 0.8 copy-start.12
  27.7 17.2 %all-to-all-start.1 = ((bf16[8,160,128]{2,1,0:T(8,128)(2,1)}), bf16[8,160,128]{2,1,0:T(8,128)(2,1)S(1)}, u32[]{:S(2)}, u32[]{:S(2)}) async-start(bf16[8,160,128]{2,1,0:T(8,128)(2,1)} %shard_map.204), calls=%async_computation.1 | async-start | bytes 655360 | tf_op jit(solution)/shard_map/all_to_all | solution.py:389
  45.6 34.1 %copy-start.26 = (s32[1,2,4,8]{3,2,1,0:T(4,128)S(1)}, s32[1,2,4,8]{3,2,1,0:T(4,128)}, u32[]{:S(2)}) copy-start(s32[1,2,4,8]{3,2,1,0:T(4,128)} %param.34) | copy-start | bytes 772
  45.6 34.1 %copy-start.27 = (f32[1,2,4,8]{3,2,1,0:T(4,128)S(1)}, f32[1,2,4,8]{3,2,1,0:T(4,128)}, u32[]{:S(2)}) copy-start(f32[1,2,4,8]{3,2,1,0:T(4,128)} %param.35) | copy-start | bytes 772
  45.6 45.7 %copy-start.23 = (f32[1536]{0:T(1024)S(1)}, f32[1536]{0:T(1024)}, u32[]{:S(2)}) copy-start(f32[1536]{0:T(1024)} %gain_ref.3) | copy-start | bytes 18436
  57.8 53.5 %copy-start = (bf16[1,1536,1024]{2,1,0:T(8,128)(2,1)S(1)}, bf16[1,1536,1024]{2,1,0:T(8,128)(2,1)}, u32[]{:S(2)}) copy-start(bf16[1,1536,1024]{2,1,0:T(8,128)(2,1)} %w_in_ref.1) | copy-start | bytes 9437188
  73.8 1.1 copy-start.7
  76.3 14.4 %all-to-all-start.3 = ((bf16[8,8,1536]{2,1,0:T(8,128)(2,1)}), bf16[8,8,1536]{2,1,0:T(8,128)(2,1)S(1)}, u32[]{:S(2)}, u32[]{:S(2)}) async-start(bf16[8,8,1536]{2,1,0:T(8,128)(2,1)} %shard_map.206.order_ref), calls=%async_computation.3 | async-start | bytes 393216 | tf_op jit(solution)/shard_map/all_to_all | solution.py:389
  91.3 0.9 copy-start.5
  92.3 0.7 copy-start.10
  93.0 0.8 copy-start.18
  111.3 1.4 %copy-start.2 = (bf16[1,512,1536]{2,1,0:T(8,128)(2,1)S(1)}, bf16[1,512,1536]{2,1,0:T(8,128)(2,1)}, u32[]{:S(2)}) copy-start(bf16[1,512,1536]{2,1,0:T(8,128)(2,1)} %w_out_ref.1) | copy-start | bytes 4718596
  112.7 19.5 %copy-start.19 = (bf16[8,512]{1,0:T(8,128)(2,1)S(1)}, bf16[8,512]{1,0:T(8,128)(2,1)}, u32[]{:S(2)}) copy-start(bf16[8,512]{1,0:T(8,128)(2,1)} %get-tuple-element.21.fresh_k_ref) | copy-start | bytes 24580
  112.7 19.5 %copy-start.20 = (bf16[8,512]{1,0:T(8,128)(2,1)S(1)}, bf16[8,512]{1,0:T(8,128)(2,1)}, u32[]{:S(2)}) copy-start(bf16[8,512]{1,0:T(8,128)(2,1)} %get-tuple-element.22.fresh_v_ref) | copy-start | bytes 24580
  114.4 19.9 %all-to-all-start.5 = ((bf16[32,4,1536]{2,1,0:T(4,128)(2,1)}), bf16[32,4,1536]{2,1,0:T(4,128)(2,1)S(1)}, u32[]{:S(2)}, u32[]{:S(2)}) async-start(bf16[32,4,1536]{2,1,0:T(4,128)(2,1)} %copy-done.3), calls=%async_computation.5 | async-start | bytes 786432 | tf_op jit(solution)/shard_map/all_to_all | solution.py:389
  119.2 0.8 copy-start.15
  120.0 0.8 copy-start.16
  120.7 6.5 %collective-permute-start.1 = (bf16[2,2,16,512]{3,2,1,0:T(8,128)(2,1)S(1)}, bf16[2,2,16,512]{3,2,1,0:T(8,128)(2,1)S(1)}, u32[]{:S(2)}, u32[]{:S(2)}) collective-permute-start(bf16[2,2,16,512]{3,2,1,0:T(8,128)(2,1)S(1)} %shard_map.211.refs_0_), channel_id=1, source_target_pairs={{0,64},{32,96},{64,0},{96,32},{128,192},{160,224},{192,128},{224,1... | collective-permute-start | bytes 196616 | tf_op jit(solution)/shard_map/ppermute | solution.py:392
  121.4 9.2 %collective-permute-start.3 = (bf16[2,2,16,512]{3,2,1,0:T(8,128)(2,1)S(1)}, bf16[2,2,16,512]{3,2,1,0:T(8,128)(2,1)S(1)}, u32[]{:S(2)}, u32[]{:S(2)}) collective-permute-start(bf16[2,2,16,512]{3,2,1,0:T(8,128)(2,1)S(1)} %shard_map.211.refs_0_), channel_id=1, source_target_pairs={{0,128},{32,160},{64,192},{96,224},{128,0},{160,32},{192,64},{224,... | collective-permute-start | bytes 196616 | tf_op jit(solution)/shard_map/ppermute | solution.py:392
  123.7 7.2 %collective-permute-start.5 = (bf16[2,2,16,512]{3,2,1,0:T(8,128)(2,1)S(1)}, bf16[2,2,16,512]{3,2,1,0:T(8,128)(2,1)S(1)}, u32[]{:S(2)}, u32[]{:S(2)}) collective-permute-start(bf16[2,2,16,512]{3,2,1,0:T(8,128)(2,1)S(1)} %shard_map.211.refs_0_), channel_id=1, source_target_pairs={{0,192},{32,224},{64,128},{96,160},{128,64},{160,96},{192,0},{224,... | collective-permute-start | bytes 196616 | tf_op jit(solution)/shard_map/ppermute | solution.py:392
  127.2 4.0 %collective-permute-start = (bf16[2,2,16,512]{3,2,1,0:T(8,128)(2,1)S(1)}, bf16[2,2,16,512]{3,2,1,0:T(8,128)(2,1)S(1)}, u32[]{:S(2)}, u32[]{:S(2)}) collective-permute-start(bf16[2,2,16,512]{3,2,1,0:T(8,128)(2,1)S(1)} %shard_map.211.refs_0_), channel_id=1, source_target_pairs={{0,32},{32,0},{64,96},{96,64},{128,160},{160,128},{192,224},{224,1... | collective-permute-start | bytes 196616 | tf_op jit(solution)/shard_map/ppermute | solution.py:392
  127.2 4.0 %collective-permute-start.2 = (bf16[2,2,16,512]{3,2,1,0:T(8,128)(2,1)S(1)}, bf16[2,2,16,512]{3,2,1,0:T(8,128)(2,1)S(1)}, u32[]{:S(2)}, u32[]{:S(2)}) collective-permute-start(bf16[2,2,16,512]{3,2,1,0:T(8,128)(2,1)S(1)} %collective-permute-done.1.refs_2_), channel_id=1, source_target_pairs={{0,32},{32,0},{64,96},{96,64},{128,160},{160,128},{192,224},{224,1... | collective-permute-start | bytes 196616 | tf_op jit(solution)/shard_map/ppermute | solution.py:392
  130.7 1.3 collective-permute-start.4
  131.0 1.3 collective-permute-start.6
  134.3 0.8 copy-start.14
  (10 other events, 6.5 us)

commit v3 on v2

--- a/solution.py
+++ b/solution.py
@@ -16,10 +16,6 @@
 SCALE = 0.125
 BF16 = jnp.bfloat16
 F32 = jnp.float32
-
-
-def whole():
-    return pl.BlockSpec(memory_space=pltpu.VMEM)
 
 
 def scalars():
@@ -334,17 +330,22 @@
     return cosine, sine
 
 
-def call(kernel, outs, *args, ins=None, scratch=(), mib=48, flops=0, moved=0, grid=()):
+def block(shape):
+    return pl.BlockSpec(shape, lambda i: (0,) * len(shape))
+
+
+def call(kernel, outs, *args, ins=(), scratch=(), mib=48):
+    specs = list(ins) + [block(a.shape) for a in args[len(ins) :]]
     return pl.pallas_call(
         kernel,
-        grid=grid,
+        grid=(1,),
         out_shape=outs,
-        in_specs=ins or [whole()] * len(args),
-        out_specs=jax.tree.map(lambda _: whole(), outs),
+        in_specs=specs,
+        out_specs=jax.tree.map(lambda o: block(o.shape), outs),
         scratch_shapes=list(scratch),
         compiler_params=params(mib),
         cost_estimate=pl.CostEstimate(
-            flops=flops or 1 << 20, bytes_accessed=moved or 1 << 20, transcendentals=0
+            flops=1 << 20, bytes_accessed=1 << 20, transcendentals=0
         ),
     )(*args)
 
@@ -372,6 +373,9 @@
     routes,
     gate_weights,
 ):
+    def stay(a):
+        return pltpu.with_memory_space_constraint(a, pltpu.MemorySpace.HBM)
+
     n_seq = lax.axis_size("seq")
     n_req = lax.axis_size("req")
     seq = lax.axis_index("seq").astype(jnp.int32).reshape(1)
@@ -382,7 +386,7 @@
     tail = generated_key_cache.shape[2]
     top = routes.shape[3]
     capacity = 4
-    x = inputs[0]
+    x = stay(inputs[0])
     anywhere = pl.BlockSpec(memory_space=pl.ANY)
 
     def exchange(a, axis):
@@ -395,13 +399,7 @@
         norm_kernel,
         shaped((n_seq, local_rows, width)),
         x,
-        gain_attn,
-        grid=(1,),
-        ins=[
-            pl.BlockSpec((here, steps, width), lambda i: (0, 0, 0)),
-            pl.BlockSpec((width,), lambda i: (0,)),
-        ],
-        mib=60,
+        stay(gain_attn),
     )
     normed_all = exchange(normed, "seq")
     bias, extra = call(
@@ -412,20 +410,18 @@
         parents[0],
         block_len,
         ins=[anywhere, scalars(), scalars(), scalars()],
-        mib=8,
-    )
-    cosine, sine = rotary_tables(rows, steps, keys * n_seq + tail)
+    )
+    cosine, sine = map(jnp.asarray, rotary_tables(rows, steps, keys * n_seq + tail))
     packed_rows = 2 * rows + rows // 2
     qkv = call(
         project_kernel,
         shaped((n_seq, packed_rows, 128)),
         normed_all,
-        w_query.T,
-        key_projection_weight.T,
-        value_projection_weight.T,
-        cosine,
-        sine,
-        mib=16,
+        stay(w_query.T),
+        stay(key_projection_weight.T),
+        stay(value_projection_weight.T),
+        stay(cosine),
+        stay(sine),
     )
     qkv_all = exchange(qkv, "seq")
 
@@ -441,8 +437,8 @@
         in_specs=[
             scalars(),
             scalars(),
-            whole(),
-            whole(),
+            pl.BlockSpec((8, keys), lambda p: (0, 0)),
+            pl.BlockSpec((rows, 128), lambda p: (0, 0)),
             pl.BlockSpec((2, packed_rows, 128), lambda p: (p, 0, 0)),
             pl.BlockSpec((keys, 128), lambda p: (0, p)),
             pl.BlockSpec((keys, 128), lambda p: (0, p)),
@@ -458,7 +454,7 @@
             pltpu.VMEM((6 * rows, keys + 128), F32),
             pltpu.VMEM((6 * rows, keys + 128), BF16),
         ],
-        compiler_params=params(60),
+        compiler_params=params(48),
         cost_estimate=pl.CostEstimate(
             flops=4 * 24 * rows * keys * HEAD,
             bytes_accessed=4 * keys * kv_width,
@@ -470,22 +466,21 @@
         bias,
         extra,
         qkv_all,
-        prompt_key_cache[0],
-        prompt_value_cache[0],
-        generated_key_cache[0],
-        generated_value_cache[0],
+        stay(prompt_key_cache[0]),
+        stay(prompt_value_cache[0]),
+        stay(generated_key_cache[0]),
+        stay(generated_value_cache[0]),
     )
     parts = exchange(partial, "seq")
-    sums = call(join_kernel, shaped((n_seq, local_rows, width)), parts, w_output, mib=16)
+    sums = call(join_kernel, shaped((n_seq, local_rows, width)), parts, stay(w_output))
     slots = n_req * capacity
     place, mix = call(
         functools.partial(route_kernel, capacity),
         (shaped((slots, local_rows)), shaped((local_rows, slots), F32)),
         sums,
-        routes[0],
-        gate_weights[0],
-        ins=[anywhere, whole(), whole()],
-        mib=8,
+        stay(routes[0]),
+        stay(gate_weights[0]),
+        ins=[anywhere],
     )
     sums = exchange(sums, "seq")
     hidden, buffer = call(
@@ -493,18 +488,16 @@
         (shaped((local_rows, width), F32), shaped((n_req, capacity, width))),
         x,
         sums,
-        gain_moe,
+        stay(gain_moe),
         place,
-        mib=16,
     )
     own = call(
         pack_kernel,
         shaped((2, here, tail, kv_width)),
         buffer,
-        generated_key_cache[0],
-        generated_value_cache[0],
-        ins=[anywhere, whole(), whole()],
-        mib=8,
+        stay(generated_key_cache[0]),
+        stay(generated_value_cache[0]),
+        ins=[anywhere],
     )
     even = [own] + [apart(own, k) for k in range(2, n_seq, 2)]
     odd = [apart(a, 1) for a in even]
@@ -515,9 +508,8 @@
         shaped(buffer.shape),
         buffer,
         w_in,
-        w_out,
+        stay(w_out),
         scratch=[pltpu.VMEM((slots, width), F32)],
-        mib=16,
     )
     back = exchange(back, "req")
     mixed = call(
@@ -527,7 +519,6 @@
         mix,
         back,
         scratch=[pltpu.VMEM((slots, width), F32)],
-        mib=16,
     )
     final_k, final_v = call(
         final_kernel,
@@ -537,8 +528,7 @@
         fresh_k,
         fresh_v,
         *owns,
-        ins=[scalars(), scalars()] + [whole()] * (2 + n_seq),
-        mib=16,
+        ins=[scalars(), scalars()],
     )
     return (
         mixed[None],

time: 139 us -> 131 us (0.942)
  local copies, waits for them, and re-layouts: 18.4 us -> 7.11 us
  Pallas kernels: 21 us -> 25.4 us
    unnamed x64 -> x26, local copies, waits for them, and re-layouts: 18.4 us -> 7.11 us
    pallas_call x10, Pallas kernels: 8.84 us -> 14.1 us  [call(): pl.pallas_call(kernel, grid=(1,), out_shape=outs, in_specs=specs, out_spe...]
  transfers between devices with their start and end apart: 10 -> 10, of which waited for: 6 -> 6; matrix products, arithmetic and copies ran while one was open for 0% -> 0% of each run, Pallas kernels for 2% -> 3%
where the time goes in v3:
time: 131 us; the launch traced here: 129 us
  blocking collectives  51 us (39%)
  waiting for transfers between devices  26.2 us (20%)
  Pallas kernels  25.4 us (19%)
  starting transfers between devices  18.6 us (14%)
  local copies, waits for them, and re-layouts  7.11 us (5%)
    all_to_all x3, blocking collectives, exchange(): return lax.all_to_all(a, axis, split_axis=0, concat_axis=0, tiled=True)  51 us
    all_to_all x3, waiting for transfers between devices, exchange(): return lax.all_to_all(a, axis, split_axis=0, concat_axis=0, tiled=True)  21.7 us
    pallas_call x10, Pallas kernels, call(): pl.pallas_call(kernel, grid=(1,), out_shape=outs, in_specs=specs, out_spe...  14.1 us
    all_to_all x3, starting transfers between devices, exchange(): return lax.all_to_all(a, axis, split_axis=0, concat_axis=0, tiled=True)  11.6 us
    pallas_call x1, Pallas kernels, local(): pl.pallas_call(attend_kernel, grid=(pairs,), out_shape=(shaped((n_seq, ro...  11.3 us
    unnamed x26, local copies, waits for them, and re-layouts  7.11 us
    ppermute x7, starting transfers between devices, apart(): return lax.ppermute(a, 'seq', [(i, i ^ distance) for i in range(n_seq)])  7.01 us
    ppermute x7, waiting for transfers between devices, apart(): return lax.ppermute(a, 'seq', [(i, i ^ distance) for i in range(n_seq)])  4.47 us
  transfers between devices with their start and end apart: 10, of which 6 were waited for; matrix products, arithmetic and copies ran while one was open for 0% of the time, Pallas kernels for 3%

profile of v3, /device:TPU:8, one launch (start us, length us, event | category | flops | bytes accessed | tf_op | source)
XLA Modules:
  0.0 129.1 jit_solution(7742420650486901749)
XLA Ops:
  0.7 0.9 shard_map.202.order_ref
  1.5 19.3 %all_to_all.30.x_ref = bf16[8,8,1536]{2,1,0:T(8,128)(2,1)S(1)} all-to-all(bf16[8,8,1536]{2,1,0:T(8,128)(2,1)S(1)} %shard_map.202.order_ref), channel_id=1, replica_groups=mesh['seq'=8,'req'=32] {'seq'}, dimensions={0} | all-to-all | bytes 393216 | tf_op jit(solution)/shard_map/all_to_all | solution.py:393
  20.8 2.5 %shard_map.204 = bf16[8,160,128]{2,1,0:T(8,128)(2,1)} custom-call(bf16[8,8,1536]{2,1,0:T(8,128)(2,1)S(1)} %all_to_all.30.x_ref, bf16[192,1536]{1,0:T(8,128)(2,1)} %bitcast.22, bf16[64,1536]{1,0:T(8,128)(2,1)} %bitcast.23, bf16[64,1536]{1,0:T(8,128)(2,1)} %bitcast.24, f32[64,256]{1,0:T(8,128)} %constant.10.clone.cos_ref, f32[64,256]{1,0:T(8,128)} %constant.11.clone.sin_ref), custom_call_target="tpu_custom_call" | custom-call | flops 1048576 | bytes 1048576 | tf_op jit(solution)/shard_map/pallas_call | solution.py:339
  23.3 3.4 %all-to-all-start.1 = ((bf16[8,160,128]{2,1,0:T(8,128)(2,1)}), bf16[8,160,128]{2,1,0:T(8,128)(2,1)S(1)}, u32[]{:S(2)}, u32[]{:S(2)}) async-start(bf16[8,160,128]{2,1,0:T(8,128)(2,1)} %shard_map.204), calls=%async_computation.1 | async-start | bytes 655360 | tf_op jit(solution)/shard_map/all_to_all | solution.py:393
  26.8 0.8 shard_map.203
  27.5 13.0 %all-to-all-done.1.qkv_ref = bf16[8,160,128]{2,1,0:T(8,128)(2,1)S(1)} async-done(((bf16[8,160,128]{2,1,0:T(8,128)(2,1)}), bf16[8,160,128]{2,1,0:T(8,128)(2,1)S(1)}, u32[]{:S(2)}, u32[]{:S(2)}) %all-to-all-start.1) | async-done | bytes 327712 | tf_op jit(solution)/shard_map/all_to_all | solution.py:393
  40.5 11.3 %shard_map.205 = (bf16[8,64,256]{2,1,0:T(8,128)(2,1)S(1)}, bf16[8,512]{1,0:T(8,128)(2,1)S(1)}, bf16[8,512]{1,0:T(8,128)(2,1)S(1)}) custom-call(s32[1]{0:T(128)} %bitcast.1.seq_ref, s32[4,16]{1,0:T(4,128)S(1)} %bitcast.20, f32[8,2048]{1,0:T(8,128)S(1)} %get-tuple-element.14.bias_ref, f32[64,128]{1,0:T(8,128)S(1)} %get-tuple-element.15.extra_ref, ...), custom_call_target="tpu_custom_call" | custom-call | flops 805306368 | bytes 4194304 | tf_op jit(solution)/shard_map/pallas_call | solution.py:429
  51.8 15.1 %all_to_all.31.part_ref = bf16[8,64,256]{2,1,0:T(8,128)(2,1)S(1)} all-to-all(bf16[8,64,256]{2,1,0:T(8,128)(2,1)S(1)} %get-tuple-element.16), channel_id=1, replica_groups=mesh['seq'=8,'req'=32] {'seq'}, dimensions={0} | all-to-all | bytes 524288 | tf_op jit(solution)/shard_map/all_to_all | solution.py:393
  66.9 2.4 %shard_map.206.order_ref = bf16[8,8,1536]{2,1,0:T(8,128)(2,1)} custom-call(bf16[8,64,256]{2,1,0:T(8,128)(2,1)S(1)} %all_to_all.31.part_ref, bf16[192,1536]{1,0:T(8,128)(2,1)} %w_ref.1), custom_call_target="tpu_custom_call" | custom-call | flops 1048576 | bytes 1048576 | tf_op jit(solution)/shard_map/pallas_call | solution.py:339
  69.4 3.4 %all-to-all-start.3 = ((bf16[8,8,1536]{2,1,0:T(8,128)(2,1)}), bf16[8,8,1536]{2,1,0:T(8,128)(2,1)S(1)}, u32[]{:S(2)}, u32[]{:S(2)}) async-start(bf16[8,8,1536]{2,1,0:T(8,128)(2,1)} %shard_map.206.order_ref), calls=%async_computation.3 | async-start | bytes 393216 | tf_op jit(solution)/shard_map/all_to_all | solution.py:393
  72.8 1.0 shard_map.207
  75.0 8.7 %all-to-all-done.3.sums_ref = bf16[8,8,1536]{2,1,0:T(8,128)(2,1)S(1)} async-done(((bf16[8,8,1536]{2,1,0:T(8,128)(2,1)}), bf16[8,8,1536]{2,1,0:T(8,128)(2,1)S(1)}, u32[]{:S(2)}, u32[]{:S(2)}) %all-to-all-start.3) | async-done | bytes 196640 | tf_op jit(solution)/shard_map/all_to_all | solution.py:393
  83.7 0.7 copy-done.2
  84.4 0.9 copy-done.3
  85.3 0.8 copy-done.7
  86.1 1.1 shard_map.208
  87.8 16.6 %all_to_all.32.x_ref = bf16[32,4,1536]{2,1,0:T(4,128)(2,1)S(1)} all-to-all(bf16[32,4,1536]{2,1,0:T(4,128)(2,1)S(1)} %get-tuple-element.20.order_ref), channel_id=1, replica_groups=mesh['seq'=8,'req'=32] {'req'}, dimensions={0} | all-to-all | bytes 786432 | tf_op jit(solution)/shard_map/all_to_all | solution.py:393
  104.4 2.3 %shard_map.209 = bf16[32,4,1536]{2,1,0:T(4,128)(2,1)S(1)} custom-call(bf16[32,4,1536]{2,1,0:T(4,128)(2,1)S(1)} %all_to_all.32.x_ref, bf16[1,1536,1024]{2,1,0:T(8,128)(2,1)S(1)} %copy-done, bf16[1,512,1536]{2,1,0:T(8,128)(2,1)} %w_out_ref.1), custom_call_target="tpu_custom_call" | custom-call | flops 1048576 | bytes 1048576 | tf_op jit(solution)/shard_map/pallas_call | solution.py:339
  106.7 0.8 copy-done.1
  107.5 4.8 %all-to-all-start.5 = ((bf16[32,4,1536]{2,1,0:T(4,128)(2,1)}), bf16[32,4,1536]{2,1,0:T(4,128)(2,1)S(1)}, u32[]{:S(2)}, u32[]{:S(2)}) async-start(bf16[32,4,1536]{2,1,0:T(4,128)(2,1)} %copy-done.1), calls=%async_computation.5 | async-start | bytes 786432 | tf_op jit(solution)/shard_map/all_to_all | solution.py:393
  112.3 0.8 shard_map.211.refs_0_
  113.1 0.7 collective-permute-start.1
  113.8 2.3 %collective-permute-start.3 = (bf16[2,2,16,512]{3,2,1,0:T(8,128)(2,1)S(1)}, bf16[2,2,16,512]{3,2,1,0:T(8,128)(2,1)S(1)}, u32[]{:S(2)}, u32[]{:S(2)}) collective-permute-start(bf16[2,2,16,512]{3,2,1,0:T(8,128)(2,1)S(1)} %shard_map.211.refs_0_), channel_id=1, source_target_pairs={{0,128},{32,160},{64,192},{96,224},{128,0},{160,32},{192,64},{224,... | collective-permute-start | bytes 196616 | tf_op jit(solution)/shard_map/ppermute | solution.py:396
  116.1 3.5 %collective-permute-start.5 = (bf16[2,2,16,512]{3,2,1,0:T(8,128)(2,1)S(1)}, bf16[2,2,16,512]{3,2,1,0:T(8,128)(2,1)S(1)}, u32[]{:S(2)}, u32[]{:S(2)}) collective-permute-start(bf16[2,2,16,512]{3,2,1,0:T(8,128)(2,1)S(1)} %shard_map.211.refs_0_), channel_id=1, source_target_pairs={{0,192},{32,224},{64,128},{96,160},{128,64},{160,96},{192,0},{224,... | collective-permute-start | bytes 196616 | tf_op jit(solution)/shard_map/ppermute | solution.py:396
  120.1 2.6 %collective-permute-done.3.refs_4_ = bf16[2,2,16,512]{3,2,1,0:T(8,128)(2,1)S(1)} collective-permute-done((bf16[2,2,16,512]{3,2,1,0:T(8,128)(2,1)S(1)}, bf16[2,2,16,512]{3,2,1,0:T(8,128)(2,1)S(1)}, u32[]{:S(2)}, u32[]{:S(2)}) %collective-permute-start.3) | collective-permute-done | bytes 65568 | tf_op jit(solution)/shard_map/ppermute | solution.py:396
  123.3 0.6 collective-permute-done.4.refs_5_
  124.0 0.6 collective-permute-done.6.refs_7_
  124.6 0.7 copy-done.9
  125.2 1.4 %shard_map.212 = (bf16[20,2,512]{2,1,0:T(2,128)(2,1)}, bf16[20,2,512]{2,1,0:T(2,128)(2,1)}) custom-call(s32[1]{0:T(128)} %bitcast.1.seq_ref, s32[4,16]{1,0:T(4,128)S(1)} %bitcast.21, bf16[8,512]{1,0:T(8,128)(2,1)S(1)} %get-tuple-element.21.fresh_k_ref, bf16[8,512]{1,0:T(8,128)(2,1)S(1)} %get-tuple-element.22.fresh_v_ref, ...), custom_call_target="tpu_custom_call" | custom-call | flops 1048576 | bytes 1048576 | tf_op jit(solution)/shard_map/pallas_call | solution.py:339
  126.6 0.8 copy-done.5
  127.4 0.7 copy-done.11
  128.1 1.0 shard_map.210
  (28 shorter events, 3.0 us)
Async XLA Ops:
  0.6 26.1 %copy-start.8 = (s32[1,4,16]{2,1,0:T(4,128)S(1)}, s32[1,4,16]{2,1,0:T(4,128)}, u32[]{:S(2)}) copy-start(s32[1,4,16]{2,1,0:T(4,128)} %param.20) | copy-start | bytes 772
  0.6 26.1 %copy-start.12 = (s32[1,16]{1,0:T(1,128)S(1)}, s32[1,16]{1,0:T(1,128)}, u32[]{:S(2)}) copy-start(s32[1,16]{1,0:T(1,128)} %len_ref.1) | copy-start | bytes 196
  23.3 17.2 %all-to-all-start.1 = ((bf16[8,160,128]{2,1,0:T(8,128)(2,1)}), bf16[8,160,128]{2,1,0:T(8,128)(2,1)S(1)}, u32[]{:S(2)}, u32[]{:S(2)}) async-start(bf16[8,160,128]{2,1,0:T(8,128)(2,1)} %shard_map.204), calls=%async_computation.1 | async-start | bytes 655360 | tf_op jit(solution)/shard_map/all_to_all | solution.py:393
  51.8 52.6 %copy-start = (bf16[1,1536,1024]{2,1,0:T(8,128)(2,1)S(1)}, bf16[1,1536,1024]{2,1,0:T(8,128)(2,1)}, u32[]{:S(2)}) copy-start(bf16[1,1536,1024]{2,1,0:T(8,128)(2,1)} %w_in_ref.1) | copy-start | bytes 9437188
  69.4 14.4 %all-to-all-start.3 = ((bf16[8,8,1536]{2,1,0:T(8,128)(2,1)}), bf16[8,8,1536]{2,1,0:T(8,128)(2,1)S(1)}, u32[]{:S(2)}, u32[]{:S(2)}) async-start(bf16[8,8,1536]{2,1,0:T(8,128)(2,1)} %shard_map.206.order_ref), calls=%async_computation.3 | async-start | bytes 393216 | tf_op jit(solution)/shard_map/all_to_all | solution.py:393
  73.8 0.6 copy-start.6
  74.4 0.6 copy-start.10
  83.7 0.7 copy-start.2
  84.4 0.9 copy-start.3
  85.3 0.8 copy-start.7
  87.2 0.6 copy-start.4
  106.7 0.8 copy-start.1
  107.5 19.2 %all-to-all-start.5 = ((bf16[32,4,1536]{2,1,0:T(4,128)(2,1)}), bf16[32,4,1536]{2,1,0:T(4,128)(2,1)S(1)}, u32[]{:S(2)}, u32[]{:S(2)}) async-start(bf16[32,4,1536]{2,1,0:T(4,128)(2,1)} %copy-done.1), calls=%async_computation.5 | async-start | bytes 786432 | tf_op jit(solution)/shard_map/all_to_all | solution.py:393
  113.1 6.5 %collective-permute-start.1 = (bf16[2,2,16,512]{3,2,1,0:T(8,128)(2,1)S(1)}, bf16[2,2,16,512]{3,2,1,0:T(8,128)(2,1)S(1)}, u32[]{:S(2)}, u32[]{:S(2)}) collective-permute-start(bf16[2,2,16,512]{3,2,1,0:T(8,128)(2,1)S(1)} %shard_map.211.refs_0_), channel_id=1, source_target_pairs={{0,64},{32,96},{64,0},{96,32},{128,192},{160,224},{192,128},{224,1... | collective-permute-start | bytes 196616 | tf_op jit(solution)/shard_map/ppermute | solution.py:396
  113.8 8.9 %collective-permute-start.3 = (bf16[2,2,16,512]{3,2,1,0:T(8,128)(2,1)S(1)}, bf16[2,2,16,512]{3,2,1,0:T(8,128)(2,1)S(1)}, u32[]{:S(2)}, u32[]{:S(2)}) collective-permute-start(bf16[2,2,16,512]{3,2,1,0:T(8,128)(2,1)S(1)} %shard_map.211.refs_0_), channel_id=1, source_target_pairs={{0,128},{32,160},{64,192},{96,224},{128,0},{160,32},{192,64},{224,... | collective-permute-start | bytes 196616 | tf_op jit(solution)/shard_map/ppermute | solution.py:396
  116.1 7.2 %collective-permute-start.5 = (bf16[2,2,16,512]{3,2,1,0:T(8,128)(2,1)S(1)}, bf16[2,2,16,512]{3,2,1,0:T(8,128)(2,1)S(1)}, u32[]{:S(2)}, u32[]{:S(2)}) collective-permute-start(bf16[2,2,16,512]{3,2,1,0:T(8,128)(2,1)S(1)} %shard_map.211.refs_0_), channel_id=1, source_target_pairs={{0,192},{32,224},{64,128},{96,160},{128,64},{160,96},{192,0},{224,... | collective-permute-start | bytes 196616 | tf_op jit(solution)/shard_map/ppermute | solution.py:396
  119.6 3.7 %collective-permute-start = (bf16[2,2,16,512]{3,2,1,0:T(8,128)(2,1)S(1)}, bf16[2,2,16,512]{3,2,1,0:T(8,128)(2,1)S(1)}, u32[]{:S(2)}, u32[]{:S(2)}) collective-permute-start(bf16[2,2,16,512]{3,2,1,0:T(8,128)(2,1)S(1)} %shard_map.211.refs_0_), channel_id=1, source_target_pairs={{0,32},{32,0},{64,96},{96,64},{128,160},{160,128},{192,224},{224,1... | collective-permute-start | bytes 196616 | tf_op jit(solution)/shard_map/ppermute | solution.py:396
  119.6 3.7 %collective-permute-start.2 = (bf16[2,2,16,512]{3,2,1,0:T(8,128)(2,1)S(1)}, bf16[2,2,16,512]{3,2,1,0:T(8,128)(2,1)S(1)}, u32[]{:S(2)}, u32[]{:S(2)}) collective-permute-start(bf16[2,2,16,512]{3,2,1,0:T(8,128)(2,1)S(1)} %collective-permute-done.1.refs_2_), channel_id=1, source_target_pairs={{0,32},{32,0},{64,96},{96,64},{128,160},{160,128},{192,224},{224,1... | collective-permute-start | bytes 196616 | tf_op jit(solution)/shard_map/ppermute | solution.py:396
  122.7 1.3 collective-permute-start.4
  123.3 1.3 collective-permute-start.6
  124.6 0.7 copy-start.9
  126.6 0.8 copy-start.5
  127.4 0.7 copy-start.11

commit v4 on v3

v4 whole, which is shorter than its diff:
```python
import functools

import jax
import jax.numpy as jnp
import numpy as np
from jax import lax
from jax.experimental import pallas as pl
from jax.experimental.pallas import tpu as pltpu
from jax.sharding import PartitionSpec as P

HEAD = 64
BLK = 128
EPSILON = 1e-05
ROPE_BASE = 10000.0
FILL = -(2.0**100)
SCALE = 0.125
BF16 = jnp.bfloat16
F32 = jnp.float32


def scalars():
    return pl.BlockSpec(memory_space=pltpu.SMEM)


def params(mib):
    return pltpu.CompilerParams(vmem_limit_bytes=mib << 20)


def dot(a, b):
    return jnp.dot(a, b, preferred_element_type=F32)


def dot_t(a, b):
    return lax.dot_general(a, b, (((1,), (1,)), ((), ())), preferred_element_type=F32)


def lanes(shape):
    return lax.broadcasted_iota(jnp.int32, shape, len(shape) - 1)


def norm(x, gain):
    mean_sq = jnp.mean(x * x, axis=-1, keepdims=True)
    return x * lax.rsqrt(mean_sq + EPSILON) * gain


def norm_kernel(x_ref, gain_ref, out_ref):
    beams, steps = x_ref.shape[0], x_ref.shape[1]
    gain = gain_ref[...].reshape(1, -1)
    rows = [norm(x_ref[b].astype(F32), gain) for b in range(beams)]
    rows = jnp.concatenate(rows, axis=0).astype(BF16)
    for d in range(out_ref.shape[0]):
        out_ref[d] = rows


def pack_kernel(order_ref, own_k_ref, own_v_ref, out_ref):
    out_ref[0] = own_k_ref[...]
    out_ref[1] = own_v_ref[...]


def swap(x):
    return pltpu.roll(x, HEAD, 1)


def even_odd(own, other, core):
    return jnp.where(core == 0, own, other), jnp.where(core == 0, other, own)


def project_kernel(
    x_ref,
    seq_ref,
    wq_ref,
    wk_ref,
    wv_ref,
    other_wq_ref,
    other_wk_ref,
    other_wv_ref,
    cos_ref,
    sin_ref,
    q_ref,
    kv_ref,
):
    core = seq_ref[0] % 2
    rows = x_ref.shape[0] * x_ref.shape[1]
    x = x_ref[...].reshape(rows, x_ref.shape[2])
    half = HEAD // 2

    def turned(wq, wk):
        y = jnp.concatenate([dot_t(x, wq) * SCALE, dot_t(x, wk)], axis=1)
        first = lanes(y.shape) % HEAD < half
        width = y.shape[1]
        turn = jnp.where(first, pltpu.roll(y, width - half, 1), pltpu.roll(y, half, 1))
        return y * cos_ref[...] + turn * sin_ref[...]

    y = turned(wq_ref[...], wk_ref[...])
    z = turned(other_wq_ref[...], other_wk_ref[...])
    even, odd = even_odd(y, z, core)
    v_even, v_odd = even_odd(dot_t(x, wv_ref[...]), dot_t(x, other_wv_ref[...]), core)
    low = lanes((rows, 128)) < HEAD
    e0, e1, o0, o1 = even[:, 0:128], even[:, 128:256], odd[:, 0:128], odd[:, 128:256]
    tiles = [
        jnp.where(low, e0, swap(o0)),
        jnp.where(low, swap(e0), o0),
        jnp.where(low, e1, swap(o1)),
    ]
    q = jnp.concatenate(tiles, axis=0).astype(BF16)
    for d in range(q_ref.shape[0]):
        q_ref[d] = q
    kv_ref[0] = jnp.where(low, swap(e1), o1).astype(BF16)
    kv_ref[1] = jnp.concatenate([v_even, v_odd], axis=1).astype(BF16)


def lookup(parents_ref, step, cur, beams):
    found = jnp.zeros(cur.shape, jnp.int32)
    for b in range(beams):
        found = jnp.where(cur == b, parents_ref[step, b], found)
    return found


def mask_kernel(
    tail,
    here,
    order_ref,
    seq_ref,
    parents_ref,
    len_ref,
    other_len_ref,
    bias_ref,
    extra_ref,
    fresh_ref,
    final_ref,
):
    steps, beams = parents_ref.shape
    seq = seq_ref[0]
    core = seq % 2
    other = seq + 1 - 2 * core
    shape = extra_ref.shape
    rows = shape[0]
    lane = lanes(shape)
    spot = lanes((bias_ref.shape[0], BLK))
    half = bias_ref.shape[1] // 2
    for source, start in ((len_ref, 0), (other_len_ref, half)):
        for j in range(half // BLK):
            at = start + j * BLK
            bias_ref[:, at : at + BLK] = jnp.where(spot < source[0, j], 0.0, FILL)
    row = lax.broadcasted_iota(jnp.int32, shape, 0)

    def beam_of(place, parity):
        return (place // (here * steps)) * 2 * here + parity * here + place // steps % here

    step = row % steps
    key = lane % rows
    key_beam = beam_of(key, jnp.where(lane < rows, core, 1 - core))
    key_step = key % steps
    real = lane < 2 * rows
    cur = beam_of(row, core)
    end = cur
    live = jnp.zeros(shape, jnp.int32)
    chosen = jnp.zeros(shape, jnp.int32)
    for s in range(steps - 1, -1, -1):
        here_now = real & (key_step == s)
        live = live | jnp.where(here_now & (cur == key_beam) & (step >= s), 1, 0)
        chosen = chosen | jnp.where(here_now & (end == key_beam) & (step == s), 1, 0)
        cur = jnp.where(step >= s, lookup(parents_ref, s, cur, beams), cur)
        end = jnp.where(step < s, lookup(parents_ref, s, end, beams), end)
    fresh_ref[...] = jnp.where(live > 0, 0.0, FILL)
    final_ref[...] = jnp.where(chosen > 0, 1.0, 0.0).astype(BF16)
    own_keys = here * tail
    holder = jnp.where(lane < own_keys, seq, other)
    own_beam = holder * here + lane % own_keys // tail
    extra_ref[...] = jnp.where((lane < 2 * own_keys) & (cur == own_beam), 0.0, FILL)


def split_heads(q_ref, rows):
    low = lanes((3 * rows, 128)) < HEAD
    q = q_ref[...].reshape(3 * rows, 128).astype(F32)
    both = [jnp.where(low, q, 0.0), jnp.where(low, 0.0, q)]
    return jnp.concatenate(both, axis=0).astype(BF16)


def pack_partial(o, total, lse, rows, store):
    lane = lanes((rows, 128))
    low = lane < HEAD
    stats = jnp.zeros((rows, 128), F32)
    for i in range(6):
        rest = lse[i]
        for piece in range(3):
            part = rest.astype(BF16).astype(F32)
            rest = rest - part
            stats = jnp.where(lane == 3 * i + piece, part, stats)
    for j in range(3):
        even = o[j * rows : (j + 1) * rows, :] / total[j]
        odd = o[(3 + j) * rows : (4 + j) * rows, :] / total[3 + j]
        store(j, jnp.where(low, even, odd).astype(BF16))
    store(3, stats.astype(BF16))


def fresh_kernel(q_ref, kv_ref, other_ref, bias_ref, final_ref, out_ref, pick_ref):
    rows = kv_ref.shape[1]
    q = split_heads(q_ref.at[0], rows)
    fill = jnp.zeros((128 - 2 * rows, 128), BF16)
    k = jnp.concatenate([kv_ref[0], other_ref[0], fill], axis=0)
    v = jnp.concatenate([kv_ref[1], other_ref[1], fill], axis=0)
    s = dot_t(q, k)
    probs, total, lse = [], [], []
    for i in range(6):
        piece = s[i * rows : (i + 1) * rows, :] + bias_ref[...]
        top = jnp.max(piece, axis=-1, keepdims=True)
        e = jnp.exp(piece - top)
        total.append(jnp.sum(e, axis=-1, keepdims=True))
        lse.append(top + jnp.log(total[i]))
        probs.append(e.astype(BF16))
    o = dot(jnp.concatenate(probs, axis=0), v)

    def store(j, tile):
        out_ref[:, j * 128 : (j + 1) * 128] = tile

    pack_partial(o, total, lse, rows, store)
    pick_k = dot(final_ref[...], k).astype(BF16)
    pick_v = dot(final_ref[...], v).astype(BF16)
    each = pick_ref.shape[1]
    for d in range(pick_ref.shape[0]):
        pick_ref[d, :, 0:128] = pick_k[d * each : (d + 1) * each, :]
        pick_ref[d, :, 128:256] = pick_v[d * each : (d + 1) * each, :]
        pick_ref[d, :, 256:512] = jnp.zeros((each, 256), BF16)


def attend_kernel(
    bias_ref,
    extra_ref,
    q_ref,
    k_ref,
    v_ref,
    other_k_ref,
    other_v_ref,
    own_ref,
    other_own_ref,
    pick_ref,
    out_ref,
    s_ref,
    p_ref,
):
    rows = extra_ref.shape[0]
    half = k_ref.shape[0]
    keys = 2 * half
    own_keys = own_ref.shape[1] * own_ref.shape[2]
    q = split_heads(q_ref.at[0], rows)
    fill = jnp.zeros((128 - 2 * own_keys, 128), BF16)
    extra = [
        jnp.concatenate(
            [
                own_ref[i].reshape(own_keys, 128),
                other_own_ref[i].reshape(own_keys, 128),
                fill,
            ],
            axis=0,
        )
        for i in range(2)
    ]
    s_ref[:, 0:half] = dot_t(q, k_ref[...])
    s_ref[:, half:keys] = dot_t(q, other_k_ref[...])
    s_ref[:, keys : keys + 128] = dot_t(q, extra[0])
    lse, total = [], []
    for i in range(6):
        span = slice(i * rows, (i + 1) * rows)
        s0 = s_ref[span, 0:keys] + bias_ref[0:1, :]
        s1 = s_ref[span, keys : keys + 128] + extra_ref[...]
        top = jnp.maximum(
            jnp.max(s0, axis=-1, keepdims=True), jnp.max(s1, axis=-1, keepdims=True)
        )
        e0 = jnp.exp(s0 - top)
        e1 = jnp.exp(s1 - top)
        p_ref[span, 0:keys] = e0.astype(BF16)
        p_ref[span, keys : keys + 128] = e1.astype(BF16)
        denominator = jnp.sum(e0, axis=-1, keepdims=True) + jnp.sum(e1, axis=-1, keepdims=True)
        total.append(denominator)
        lse.append(top + jnp.log(denominator))
    o = dot(p_ref[:, 0:half], v_ref[...]) + dot(p_ref[:, half:keys], other_v_ref[...])
    o = o + dot(p_ref[:, keys : keys + 128], extra[1])

    def store(j, tile):
        out_ref[0, 0:rows, j * 128 : (j + 1) * 128] = tile

    pack_partial(o, total, lse, rows, store)
    out_ref[0, rows:, :] = pick_ref[0]


def join_kernel(part_ref, fresh_ref, seq_ref, w_ref, other_w_ref, out_ref):
    sources, rows = part_ref.shape[0], fresh_ref.shape[0]
    core = seq_ref[0] % 2
    low = lanes((rows, 128)) < HEAD

    def tile(s, j):
        span = slice(j * 128, (j + 1) * 128)
        source = fresh_ref[:, span] if s == sources else part_ref[s, 0:rows, span]
        return source.astype(F32)

    stats = [tile(s, 3) for s in range(sources + 1)]
    lse = [x + pltpu.roll(x, 127, 1) + pltpu.roll(x, 126, 1) for x in stats]
    top = functools.reduce(jnp.maximum, lse)
    weight = [jnp.exp(x - top) for x in lse]
    inverse = 1.0 / functools.reduce(jnp.add, weight)
    out = jnp.zeros((rows, w_ref.shape[1]), F32)
    for j in range(3):
        total = jnp.zeros((rows, 128), F32)
        for s in range(sources + 1):
            w = weight[s] * inverse
            even, odd = w[:, 3 * j : 3 * j + 1], w[:, 9 + 3 * j : 10 + 3 * j]
            total = total + tile(s, j) * jnp.where(low, even, odd)
        total = jnp.where(core == 0, total, swap(total)).astype(BF16)
        span = slice(j * HEAD, (j + 1) * HEAD)
        out = out + dot(total, jnp.concatenate([w_ref[span, :], other_w_ref[span, :]], axis=0))
    out = out.astype(BF16)
    each = rows // sources
    for s in range(sources):
        out_ref[s] = out[s * each : (s + 1) * each, :]


def route_kernel(capacity, order_ref, route_ref, gate_ref, place_ref, mix_ref):
    beams, steps = route_ref.shape[0], route_ref.shape[1]
    rows = beams * steps
    slots = place_ref.shape[0]
    slot = lanes((rows, slots))
    routes = jnp.concatenate([route_ref[b] for b in range(beams)], axis=0)
    gates = jnp.concatenate([gate_ref[b] for b in range(beams)], axis=0)
    named = jnp.zeros((rows, slots), F32)
    gate = jnp.zeros((rows, slots), F32)
    for j in range(routes.shape[1]):
        hit = routes[:, j : j + 1] == slot // capacity
        named = jnp.where(hit, 1.0, named)
        gate = jnp.where(hit, gates[:, j : j + 1], gate)
    earlier = jnp.where(
        lanes((rows, rows)) < lax.broadcasted_iota(jnp.int32, (rows, rows), 0), 1.0, 0.0
    )
    rank = dot(earlier.astype(BF16), named.astype(BF16))
    placed = (named > 0.0) & (rank == (slot % capacity).astype(F32))
    mix_ref[...] = jnp.where(placed, gate, 0.0)
    place_ref[...] = jnp.where(placed, 1.0, 0.0).T.astype(BF16)


def dispatch_kernel(x_ref, sums_ref, gain_ref, place_ref, hidden_ref, out_ref):
    beams = x_ref.shape[0]
    total = sums_ref[0].astype(F32)
    for s in range(1, sums_ref.shape[0]):
        total = total + sums_ref[s].astype(F32)
    inputs = jnp.concatenate([x_ref[b].astype(F32) for b in range(beams)], axis=0)
    hidden = inputs + total
    hidden_ref[...] = hidden
    expert_in = norm(hidden, gain_ref[...].reshape(1, -1)).astype(BF16)
    buffer = dot(place_ref[...], expert_in)
    experts, capacity = out_ref.shape[0], out_ref.shape[1]
    for e in range(experts):
        out_ref[e] = buffer[e * capacity : (e + 1) * capacity, :].astype(BF16)


def expert_kernel(x_ref, w_in_ref, w_out_ref, out_ref, rows_ref):
    sources, capacity = x_ref.shape[0], x_ref.shape[1]
    for s in range(sources):
        rows_ref[s * capacity : (s + 1) * capacity, :] = x_ref[s].astype(F32)
    projected = dot(rows_ref[...].astype(BF16), w_in_ref[0])
    half = projected.shape[1] // 2
    g, u = projected[:, 0:half], projected[:, half:]
    act = (g * jax.nn.sigmoid(g) * u).astype(BF16)
    out = dot(act, w_out_ref[0])
    for s in range(sources):
        out_ref[s] = out[s * capacity : (s + 1) * capacity, :].astype(BF16)


def mix_kernel(hidden_ref, mix_ref, back_ref, out_ref, rows_ref):
    experts, capacity = back_ref.shape[0], back_ref.shape[1]
    for e in range(experts):
        rows_ref[e * capacity : (e + 1) * capacity, :] = back_ref[e].astype(F32)
    returned = rows_ref[...].astype(BF16)
    rest = mix_ref[...]
    total = hidden_ref[...]
    for _ in range(3):
        part = rest.astype(BF16)
        rest = rest - part.astype(F32)
        total = total + dot(part, returned)
    steps = out_ref.shape[1]
    for b in range(out_ref.shape[0]):
        out_ref[b] = total[b * steps : (b + 1) * steps, :].astype(BF16)


def final_kernel(seq_ref, parents_ref, part_ref, *refs):
    own_refs, (k_ref, v_ref) = refs[:-2], refs[-2:]
    steps = parents_ref.shape[0]
    here, tail = own_refs[0].shape[1], own_refs[0].shape[2]
    start = part_ref.shape[1] - here * steps
    seq = seq_ref[0]
    for i in range(here):
        beam = seq * here + i
        for s in range(steps - 1, -1, -1):
            beam = parents_ref[s, beam]
        apart = lax.bitwise_xor(beam // here, seq)
        for j, own_ref in enumerate(own_refs):

            @pl.when(apart == j)
            def _():
                k_ref[0:tail, i, :] = own_ref[0, beam % here]
                v_ref[0:tail, i, :] = own_ref[1, beam % here]

        span = slice(start + i * steps, start + (i + 1) * steps)
        for p in range(part_ref.shape[0]):
            k_ref[tail:, i, p * 128 : (p + 1) * 128] = part_ref[p, span, 0:128]
            v_ref[tail:, i, p * 128 : (p + 1) * 128] = part_ref[p, span, 128:256]


def rotary_tables(rows, steps, start):
    half = HEAD // 2
    frequency = ROPE_BASE ** (-(np.arange(half, dtype=np.float64) * 2.0 / HEAD))
    angles = (np.arange(rows) % steps + start)[:, None] * frequency[None, :]
    cosine = np.tile(np.cos(angles), (1, 8)).astype(np.float32)
    sine = np.sin(angles)
    sine = np.tile(np.concatenate([-sine, sine], axis=1), (1, 4)).astype(np.float32)
    return cosine, sine


def block(shape):
    return pl.BlockSpec(shape, lambda i: (0,) * len(shape))


def call(kernel, outs, *args, ins=(), scratch=(), mib=48):
    specs = list(ins) + [block(a.shape) for a in args[len(ins) :]]
    return pl.pallas_call(
        kernel,
        grid=(1,),
        out_shape=outs,
        in_specs=specs,
        out_specs=jax.tree.map(lambda o: block(o.shape), outs),
        scratch_shapes=list(scratch),
        compiler_params=params(mib),
        cost_estimate=pl.CostEstimate(
            flops=1 << 20, bytes_accessed=1 << 20, transcendentals=0
        ),
    )(*args)


def shaped(shape, dtype=BF16):
    return jax.ShapeDtypeStruct(shape, dtype)


def local(
    inputs,
    parents,
    block_len,
    prompt_key_cache,
    prompt_value_cache,
    generated_key_cache,
    generated_value_cache,
    gain_attn,
    gain_moe,
    w_query,
    key_projection_weight,
    value_projection_weight,
    w_output,
    w_in,
    w_out,
    routes,
    gate_weights,
):
    def stay(a):
        return pltpu.with_memory_space_constraint(a, pltpu.MemorySpace.HBM)

    n_seq = lax.axis_size("seq")
    n_req = lax.axis_size("req")
    n_chips = n_seq // 2
    seq = lax.axis_index("seq").astype(jnp.int32).reshape(1)
    here, steps, width = inputs.shape[1:]
    local_rows = here * steps
    rows = local_rows * n_chips
    keys, kv_width = prompt_key_cache.shape[1:]
    tail = generated_key_cache.shape[2]
    capacity = 4
    x = stay(inputs[0])
    anywhere = pl.BlockSpec(memory_space=pl.ANY)
    same_core = [[2 * z + core for z in range(n_chips)] for core in range(2)]

    def exchange(a, axis):
        return lax.all_to_all(a, axis, split_axis=0, concat_axis=0, tiled=True)

    def exchange_chips(a):
        return lax.all_to_all(
            a, "seq", split_axis=0, concat_axis=0, tiled=True, axis_index_groups=same_core
        )

    def apart(a, distance):
        return lax.ppermute(a, "seq", [(i, i ^ distance) for i in range(n_seq)])

    def of_other_core(a):
        return apart(a, 1)

    normed = call(norm_kernel, shaped((n_chips, local_rows, width)), x, stay(gain_attn))
    normed_all = exchange_chips(normed)
    weights = [w_query.T, key_projection_weight.T, value_projection_weight.T]
    other_weights = [of_other_core(w) for w in weights]
    prompt = [prompt_key_cache[0], prompt_value_cache[0]]
    other_prompt = [of_other_core(a) for a in prompt]
    other_w_output = of_other_core(w_output)
    own = call(
        pack_kernel,
        shaped((2, here, tail, kv_width)),
        normed,
        stay(generated_key_cache[0]),
        stay(generated_value_cache[0]),
        ins=[anywhere],
    )
    other_own = apart(own, 1)
    bias, extra, fresh_bias, final = call(
        functools.partial(mask_kernel, tail, here),
        (
            shaped((8, 2 * keys), F32),
            shaped((rows, 128), F32),
            shaped((rows, 128), F32),
            shaped((rows, 128)),
        ),
        normed,
        seq,
        parents[0],
        block_len,
        apart(block_len, 1),
        ins=[anywhere, scalars(), scalars(), scalars(), scalars()],
    )
    cosine, sine = map(jnp.asarray, rotary_tables(rows, steps, keys * n_seq + tail))
    q, kv = call(
        project_kernel,
        (shaped((n_chips, 3 * rows, 128)), shaped((2, rows, 128))),
        normed_all,
        seq,
        *[stay(w) for w in weights],
        *other_weights,
        stay(cosine),
        stay(sine),
        ins=[block(normed_all.shape), scalars()],
    )
    q_all = exchange_chips(q)
    fresh, pick = call(
        fresh_kernel,
        (shaped((rows, 512)), shaped((n_chips, local_rows, 512))),
        q,
        kv,
        apart(kv, 1),
        fresh_bias,
        final,
    )

    held = pl.BlockSpec((keys, 128), lambda p: (0, p))
    held_own = pl.BlockSpec((2, here, tail, 128), lambda p: (0, 0, 0, p))
    partial = pl.pallas_call(
        attend_kernel,
        grid=(kv_width // 128,),
        out_shape=shaped((n_chips, rows + local_rows, 512)),
        in_specs=[
            pl.BlockSpec((8, 2 * keys), lambda p: (0, 0)),
            pl.BlockSpec((rows, 128), lambda p: (0, 0)),
            pl.BlockSpec((1, 3 * rows, 128), lambda p: (p, 0, 0)),
            held,
            held,
            held,
            held,
            held_own,
            held_own,
            pl.BlockSpec((1, local_rows, 512), lambda p: (p, 0, 0)),
        ],
        out_specs=pl.BlockSpec((1, rows + local_rows, 512), lambda p: (p, 0, 0)),
        scratch_shapes=[
            pltpu.VMEM((6 * rows, 2 * keys + 128), F32),
            pltpu.VMEM((6 * rows, 2 * keys + 128), BF16),
        ],
        compiler_params=params(48),
        cost_estimate=pl.CostEstimate(
            flops=4 * 24 * rows * 2 * keys * HEAD,
            bytes_accessed=8 * keys * kv_width,
            transcendentals=24 * rows * 2 * keys,
        ),
    )(bias, extra, q_all, *map(stay, prompt), *other_prompt, own, other_own, pick)
    parts = exchange_chips(partial)
    sums = call(
        join_kernel,
        shaped((n_chips, local_rows, width)),
        parts,
        fresh,
        seq,
        stay(w_output),
        other_w_output,
        ins=[block(parts.shape), block(fresh.shape), scalars()],
    )
    slots = n_req * capacity
    place, mix = call(
        functools.partial(route_kernel, capacity),
        (shaped((slots, local_rows)), shaped((local_rows, slots), F32)),
        sums,
        stay(routes[0]),
        stay(gate_weights[0]),
        ins=[anywhere],
    )
    sums = exchange_chips(sums)
    hidden, buffer = call(
        dispatch_kernel,
        (shaped((local_rows, width), F32), shaped((n_req, capacity, width))),
        x,
        sums,
        stay(gain_moe),
        place,
    )
    own, buffer = lax.optimization_barrier((own, buffer))
    even = [own] + [apart(own, k) for k in range(2, n_seq, 2)]
    buffer = exchange(buffer, "req")
    back = call(
        expert_kernel,
        shaped(buffer.shape),
        buffer,
        stay(w_in),
        stay(w_out),
        scratch=[pltpu.VMEM((slots, width), F32)],
    )
    back, *even = lax.optimization_barrier((back, *even))
    odd = [other_own] + [apart(a, 1) for a in even[1:]]
    owns = [a for pair in zip(even, odd) for a in pair]
    back = exchange(back, "req")
    mixed = call(
        mix_kernel,
        shaped((here, steps, width)),
        hidden,
        mix,
        back,
        scratch=[pltpu.VMEM((slots, width), F32)],
    )
    final_k, final_v = call(
        final_kernel,
        (shaped((tail + steps, here, kv_width)),) * 2,
        seq,
        parents[0],
        parts,
        *owns,
        ins=[scalars(), scalars()],
    )
    return (
        mixed[None],
        final_k.transpose(1, 0, 2)[None],
        final_v.transpose(1, 0, 2)[None],
    )


def solution(mesh):
    placed = (
        P("req", "seq", None, None),
        P("req", None, None),
        P("req", "seq"),
        P("req", "seq", None),
        P("req", "seq", None),
        P("req", "seq", None, None),
        P("req", "seq", None, None),
        P(),
        P(),
        P(None, "seq"),
        P(None, "seq"),
        P(None, "seq"),
        P("seq", None),
        P("req", None, None),
        P("req", None, None),
        P("req", "seq", None, None),
        P("req", "seq", None, None),
    )
    return jax.shard_map(
        local,
        mesh=mesh,
        in_specs=placed,
        out_specs=(P("req", "seq", None, None),) * 3,
        check_vma=False,
    )
```

time: 131 us -> 112 us (0.85)
  blocking collectives: 51 us -> 0 us
  starting transfers between devices: 18.6 us -> 40.5 us
  waiting for transfers between devices: 26.2 us -> 39.8 us
  local copies, waits for them, and re-layouts: 7.11 us -> 1.61 us
  Pallas kernels: 25.4 us -> 28.2 us
    all_to_all x3 -> x0, blocking collectives: 51 us -> none  [exchange(): return lax.all_to_all(a, axis, split_axis=0, concat_axis=0, tiled=True)]
    all_to_all x0 -> x4, waiting for transfers between devices: none -> 28.7 us  [exchange_chips(): lax.all_to_all(a, 'seq', split_axis=0, concat_axis=0, tiled=True, axis_in...]
    all_to_all x0 -> x4, starting transfers between devices: none -> 18.4 us  [exchange_chips(): lax.all_to_all(a, 'seq', split_axis=0, concat_axis=0, tiled=True, axis_in...]
    all_to_all x3 -> x2, waiting for transfers between devices: 21.7 us -> 9.05 us  [exchange(): return lax.all_to_all(a, axis, split_axis=0, concat_axis=0, tiled=True)]
    unnamed x26 -> x8, local copies, waits for them, and re-layouts: 7.11 us -> 1.61 us
    pallas_call x10 -> x11, Pallas kernels: 14.1 us -> 18.6 us  [call(): pl.pallas_call(kernel, grid=(1,), out_shape=outs, in_specs=specs, out_spe...]
    ppermute x7 -> x15, starting transfers between devices: 7.01 us -> 9.43 us  [apart(): return lax.ppermute(a, 'seq', [(i, i ^ distance) for i in range(n_seq)])]
    ppermute x7 -> x15, waiting for transfers between devices: 4.47 us -> 2.11 us  [apart(): return lax.ppermute(a, 'seq', [(i, i ^ distance) for i in range(n_seq)])]
  transfers between devices with their start and end apart: 10 -> 21, of which waited for: 6 -> 11; matrix products, arithmetic and copies ran while one was open for 0% -> 0% of each run, Pallas kernels for 3% -> 21%
where the time goes in v4:
time: 112 us; the launch traced here: 111 us
  starting transfers between devices  40.5 us (36%)
  waiting for transfers between devices  39.8 us (36%)
  Pallas kernels  28.2 us (25%)
  local copies, waits for them, and re-layouts  1.61 us (1%)
    all_to_all x4, waiting for transfers between devices, exchange_chips(): lax.all_to_all(a, 'seq', split_axis=0, concat_axis=0, tiled=True, axis_in...  28.7 us
    pallas_call x11, Pallas kernels, call(): pl.pallas_call(kernel, grid=(1,), out_shape=outs, in_specs=specs, out_spe...  18.6 us
    all_to_all x4, starting transfers between devices, exchange_chips(): lax.all_to_all(a, 'seq', split_axis=0, concat_axis=0, tiled=True, axis_in...  18.4 us
    all_to_all x2, starting transfers between devices, exchange(): return lax.all_to_all(a, axis, split_axis=0, concat_axis=0, tiled=True)  12.6 us
    pallas_call x1, Pallas kernels, local(): pl.pallas_call(attend_kernel, grid=(kv_width // 128,), out_shape=shaped((...  9.64 us
    ppermute x15, starting transfers between devices, apart(): return lax.ppermute(a, 'seq', [(i, i ^ distance) for i in range(n_seq)])  9.43 us
    all_to_all x2, waiting for transfers between devices, exchange(): return lax.all_to_all(a, axis, split_axis=0, concat_axis=0, tiled=True)  9.05 us
  transfers between devices with their start and end apart: 21, of which 11 were waited for; matrix products, arithmetic and copies ran while one was open for 0% of the time, Pallas kernels for 21%

profile of v4, /device:TPU:8, one launch (start us, length us, event | category | flops | bytes accessed | tf_op | source)
XLA Modules:
  0.0 110.9 jit_solution(4095168107429141692)
XLA Ops:
  1.9 1.5 %shard_map.202.order_ref = bf16[4,8,1536]{2,1,0:T(8,128)(2,1)} custom-call(bf16[2,4,1536]{2,1,0:T(4,128)(2,1)} %bitcast.31, f32[1536]{0:T(1024)} %gain_ref.2), custom_call_target="tpu_custom_call" | custom-call | flops 1048576 | bytes 1048576 | tf_op jit(solution)/shard_map/pallas_call | solution.py:424
  3.4 8.5 %all-to-all-start = ((bf16[4,8,1536]{2,1,0:T(8,128)(2,1)}), bf16[4,8,1536]{2,1,0:T(8,128)(2,1)S(1)}, u32[]{:S(2)}, u32[]{:S(2)}) async-start(bf16[4,8,1536]{2,1,0:T(8,128)(2,1)} %shard_map.202.order_ref), calls=%async_computation | async-start | bytes 196608 | tf_op jit(solution)/shard_map/all_to_all | solution.py:482
  11.8 0.7 copy-done
  12.6 8.1 %all-to-all-done.x_ref = bf16[4,8,1536]{2,1,0:T(8,128)(2,1)S(1)} async-done(((bf16[4,8,1536]{2,1,0:T(8,128)(2,1)}), bf16[4,8,1536]{2,1,0:T(8,128)(2,1)S(1)}, u32[]{:S(2)}, u32[]{:S(2)}) %all-to-all-start) | async-done | bytes 98336 | tf_op jit(solution)/shard_map/all_to_all | solution.py:482
  20.8 0.9 copy-done.1
  21.7 2.7 %shard_map.204 = (bf16[4,96,128]{2,1,0:T(8,128)(2,1)}, bf16[2,32,128]{2,1,0:T(8,128)(2,1)S(1)}) custom-call(bf16[4,8,1536]{2,1,0:T(8,128)(2,1)S(1)} %all-to-all-done.x_ref, s32[1]{0:T(128)} %bitcast.1.seq_ref, bf16[192,1536]{1,0:T(8,128)(2,1)} %bitcast.26, bf16[64,1536]{1,0:T(8,128)(2,1)} %bitcast.28, bf16[64,1536]{1,0:T(8,128)(2,1)} %bitcast.30, ...), custom_call_target="tpu_custom_call" | custom-call | flops 1048576 | bytes 1048576 | tf_op jit(solution)/shard_map/pallas_call | solution.py:424
  24.4 3.3 %all-to-all-start.1 = ((bf16[4,96,128]{2,1,0:T(8,128)(2,1)}), bf16[4,96,128]{2,1,0:T(8,128)(2,1)S(1)}, u32[]{:S(2)}, u32[]{:S(2)}) async-start(bf16[4,96,128]{2,1,0:T(8,128)(2,1)} %get-tuple-element.26.q_ref), calls=%async_computation.1 | async-start | bytes 196608 | tf_op jit(solution)/shard_map/all_to_all | solution.py:482
  27.7 0.8 shard_map.205.own_ref.refs_0_
  28.5 0.5 collective-permute-start
  29.0 0.8 collective-permute-done.other_len_ref
  30.2 0.8 shard_map.203
  31.0 1.3 %shard_map.206 = (bf16[32,512]{1,0:T(8,128)(2,1)S(1)}, bf16[4,8,512]{2,1,0:T(8,128)(2,1)S(1)}) custom-call(bf16[4,96,128]{2,1,0:T(8,128)(2,1)} %get-tuple-element.26.q_ref, bf16[2,32,128]{2,1,0:T(8,128)(2,1)S(1)} %get-tuple-element.27.kv_ref, bf16[2,32,128]{2,1,0:T(8,128)(2,1)S(1)} %collective-permute-done.7.other_ref, ...), custom_call_target="tpu_custom_call" | custom-call | flops 1048576 | bytes 1048576 | tf_op jit(solution)/shard_map/pallas_call | solution.py:424
  32.3 3.9 %all-to-all-done.1.q_ref = bf16[4,96,128]{2,1,0:T(8,128)(2,1)S(1)} async-done(((bf16[4,96,128]{2,1,0:T(8,128)(2,1)}), bf16[4,96,128]{2,1,0:T(8,128)(2,1)S(1)}, u32[]{:S(2)}, u32[]{:S(2)}) %all-to-all-start.1) | async-done | bytes 98336 | tf_op jit(solution)/shard_map/all_to_all | solution.py:482
  36.2 9.6 %shard_map.207 = bf16[4,40,512]{2,1,0:T(8,128)(2,1)} custom-call(f32[8,4096]{1,0:T(8,128)S(1)} %get-tuple-element.24.bias_ref, f32[32,128]{1,0:T(8,128)S(1)} %get-tuple-element.25.extra_ref, bf16[4,96,128]{2,1,0:T(8,128)(2,1)S(1)} %all-to-all-done.1.q_ref, bf16[2048,512]{1,0:T(8,128)(2,1)} %bitcast.22, bf16[2048,512]{1,0:T(8,128)(2,1)} %bitcast.24, ...), custom_call_target="tpu_custom_call" | custom-call | flops 805306368 | bytes 8388608 | tf_op jit(solution)/shard_map/pallas_call | solution.py:548
  45.8 3.3 %all-to-all-start.2 = ((bf16[4,40,512]{2,1,0:T(8,128)(2,1)}), bf16[4,40,512]{2,1,0:T(8,128)(2,1)S(1)}, u32[]{:S(2)}, u32[]{:S(2)}) async-start(bf16[4,40,512]{2,1,0:T(8,128)(2,1)} %shard_map.207), calls=%async_computation.2 | async-start | bytes 327680 | tf_op jit(solution)/shard_map/all_to_all | solution.py:482
  49.2 9.2 %all-to-all-done.2.part_ref = bf16[4,40,512]{2,1,0:T(8,128)(2,1)S(1)} async-done(((bf16[4,40,512]{2,1,0:T(8,128)(2,1)}), bf16[4,40,512]{2,1,0:T(8,128)(2,1)S(1)}, u32[]{:S(2)}, u32[]{:S(2)}) %all-to-all-start.2) | async-done | bytes 163872 | tf_op jit(solution)/shard_map/all_to_all | solution.py:482
  58.4 2.4 %shard_map.208.order_ref = bf16[4,8,1536]{2,1,0:T(8,128)(2,1)} custom-call(bf16[4,40,512]{2,1,0:T(8,128)(2,1)S(1)} %all-to-all-done.2.part_ref, bf16[32,512]{1,0:T(8,128)(2,1)S(1)} %get-tuple-element.31.fresh_ref, s32[1]{0:T(128)} %bitcast.1.seq_ref, bf16[192,1536]{1,0:T(8,128)(2,1)} %w_ref.1, bf16[192,1536]{1,0:T(8,128)(2,1)S(1)} %collective-permute-done.8.other_w_ref), custom_call_target="tpu_custom_call" | custom-call | flops 1048576 | bytes 1048576 | tf_op jit(solution)/shard_map/pallas_call | solution.py:424
  60.8 3.3 %all-to-all-start.3 = ((bf16[4,8,1536]{2,1,0:T(8,128)(2,1)}), bf16[4,8,1536]{2,1,0:T(8,128)(2,1)S(1)}, u32[]{:S(2)}, u32[]{:S(2)}) async-start(bf16[4,8,1536]{2,1,0:T(8,128)(2,1)} %shard_map.208.order_ref), calls=%async_computation.3 | async-start | bytes 196608 | tf_op jit(solution)/shard_map/all_to_all | solution.py:482
  64.1 1.0 shard_map.209
  65.1 7.4 %all-to-all-done.3.sums_ref = bf16[4,8,1536]{2,1,0:T(8,128)(2,1)S(1)} async-done(((bf16[4,8,1536]{2,1,0:T(8,128)(2,1)}), bf16[4,8,1536]{2,1,0:T(8,128)(2,1)S(1)}, u32[]{:S(2)}, u32[]{:S(2)}) %all-to-all-start.3) | async-done | bytes 98336 | tf_op jit(solution)/shard_map/all_to_all | solution.py:482
  72.5 1.8 %shard_map.210 = (f32[8,1536]{1,0:T(8,128)S(1)}, bf16[32,4,1536]{2,1,0:T(4,128)(2,1)}) custom-call(bf16[2,4,1536]{2,1,0:T(4,128)(2,1)} %bitcast.32, bf16[4,8,1536]{2,1,0:T(8,128)(2,1)S(1)} %all-to-all-done.3.sums_ref, f32[1536]{0:T(1024)} %gain_ref.3, bf16[128,8]{1,0:T(8,128)(2,1)S(1)} %get-tuple-element.32.place_ref), custom_call_target="tpu_custom_call" | custom-call | flops 1048576 | bytes 1048576 | tf_op jit(solution)/shard_map/pallas_call | solution.py:424
  74.3 7.8 %all-to-all-start.4 = ((bf16[32,4,1536]{2,1,0:T(4,128)(2,1)}), bf16[32,4,1536]{2,1,0:T(4,128)(2,1)S(1)}, u32[]{:S(2)}, u32[]{:S(2)}) async-start(bf16[32,4,1536]{2,1,0:T(4,128)(2,1)} %get-tuple-element.36), calls=%async_computation.4 | async-start | bytes 786432 | tf_op jit(solution)/shard_map/all_to_all | solution.py:479
  82.1 1.3 %collective-permute-start.10 = (bf16[2,2,16,512]{3,2,1,0:T(8,128)(2,1)S(1)}, bf16[2,2,16,512]{3,2,1,0:T(8,128)(2,1)S(1)}, u32[]{:S(2)}, u32[]{:S(2)}) collective-permute-start(bf16[2,2,16,512]{3,2,1,0:T(8,128)(2,1)S(1)} %shard_map.205.own_ref.refs_0_), channel_id=1, source_target_pairs={{0,128},{32,160},{64,192},{96,224},{128,0},{160,32},{192,64},{224,... | collective-permute-start | bytes 196616 | tf_op jit(solution)/shard_map/ppermute | solution.py:487
  83.4 3.2 %collective-permute-start.11 = (bf16[2,2,16,512]{3,2,1,0:T(8,128)(2,1)S(1)}, bf16[2,2,16,512]{3,2,1,0:T(8,128)(2,1)S(1)}, u32[]{:S(2)}, u32[]{:S(2)}) collective-permute-start(bf16[2,2,16,512]{3,2,1,0:T(8,128)(2,1)S(1)} %shard_map.205.own_ref.refs_0_), channel_id=1, source_target_pairs={{0,192},{32,224},{64,128},{96,160},{128,64},{160,96},{192,0},{224,... | collective-permute-start | bytes 196616 | tf_op jit(solution)/shard_map/ppermute | solution.py:487
  86.6 2.1 %collective-permute-start.9 = (bf16[2,2,16,512]{3,2,1,0:T(8,128)(2,1)S(1)}, bf16[2,2,16,512]{3,2,1,0:T(8,128)(2,1)S(1)}, u32[]{:S(2)}, u32[]{:S(2)}) collective-permute-start(bf16[2,2,16,512]{3,2,1,0:T(8,128)(2,1)S(1)} %shard_map.205.own_ref.refs_0_), channel_id=1, source_target_pairs={{0,64},{32,96},{64,0},{96,32},{128,192},{160,224},{192,128},{224,1... | collective-permute-start | bytes 196616 | tf_op jit(solution)/shard_map/ppermute | solution.py:487
  88.7 3.5 %all-to-all-done.4.x_ref = bf16[32,4,1536]{2,1,0:T(4,128)(2,1)S(1)} async-done(((bf16[32,4,1536]{2,1,0:T(4,128)(2,1)}), bf16[32,4,1536]{2,1,0:T(4,128)(2,1)S(1)}, u32[]{:S(2)}, u32[]{:S(2)}) %all-to-all-start.4) | async-done | bytes 393248 | tf_op jit(solution)/shard_map/all_to_all | solution.py:479
  92.2 4.0 %shard_map.211 = bf16[32,4,1536]{2,1,0:T(4,128)(2,1)} custom-call(bf16[32,4,1536]{2,1,0:T(4,128)(2,1)S(1)} %all-to-all-done.4.x_ref, bf16[1,1536,1024]{2,1,0:T(8,128)(2,1)} %w_in_ref.1, bf16[1,512,1536]{2,1,0:T(8,128)(2,1)} %w_out_ref.1), custom_call_target="tpu_custom_call" | custom-call | flops 1048576 | bytes 1048576 | tf_op jit(solution)/shard_map/pallas_call | solution.py:424
  96.2 4.9 %all-to-all-start.5 = ((bf16[32,4,1536]{2,1,0:T(4,128)(2,1)}), bf16[32,4,1536]{2,1,0:T(4,128)(2,1)S(1)}, u32[]{:S(2)}, u32[]{:S(2)}) async-start(bf16[32,4,1536]{2,1,0:T(4,128)(2,1)} %shard_map.211), calls=%async_computation.5 | async-start | bytes 786432 | tf_op jit(solution)/shard_map/all_to_all | solution.py:479
  101.8 0.6 collective-permute-done.12.refs_3_
  102.9 1.4 %shard_map.213 = (bf16[20,2,512]{2,1,0:T(2,128)(2,1)}, bf16[20,2,512]{2,1,0:T(2,128)(2,1)}) custom-call(s32[1]{0:T(128)} %bitcast.1.seq_ref, s32[4,16]{1,0:T(4,128)S(1)} %bitcast.20, bf16[4,40,512]{2,1,0:T(8,128)(2,1)S(1)} %all-to-all-done.2.part_ref, bf16[2,2,16,512]{3,2,1,0:T(8,128)(2,1)S(1)} %shard_map.205.own_ref.refs_0_, ...), custom_call_target="tpu_custom_call" | custom-call | flops 1048576 | bytes 1048576 | tf_op jit(solution)/shard_map/pallas_call | solution.py:424
  104.3 5.6 %all-to-all-done.5.back_ref = bf16[32,4,1536]{2,1,0:T(4,128)(2,1)S(1)} async-done(((bf16[32,4,1536]{2,1,0:T(4,128)(2,1)}), bf16[32,4,1536]{2,1,0:T(4,128)(2,1)S(1)}, u32[]{:S(2)}, u32[]{:S(2)}) %all-to-all-start.5) | async-done | bytes 393248 | tf_op jit(solution)/shard_map/all_to_all | solution.py:479
  109.9 1.0 shard_map.212
  (30 shorter events, 3.0 us)
Async XLA Ops:
  0.6 27.9 %copy-start.3 = (s32[1,16]{1,0:T(1,128)S(1)}, s32[1,16]{1,0:T(1,128)}, u32[]{:S(2)}) copy-start(s32[1,16]{1,0:T(1,128)} %len_ref.1) | copy-start | bytes 196
  0.6 29.5 %copy-start.2 = (s32[1,4,16]{2,1,0:T(4,128)S(1)}, s32[1,4,16]{2,1,0:T(4,128)}, u32[]{:S(2)}) copy-start(s32[1,4,16]{2,1,0:T(4,128)} %param.20) | copy-start | bytes 772
  0.7 35.5 %collective-permute-start.4 = (bf16[2048,512]{1,0:T(8,128)(2,1)}, bf16[2048,512]{1,0:T(8,128)(2,1)S(1)}, u32[]{:S(2)}, u32[]{:S(2)}) collective-permute-start(bf16[2048,512]{1,0:T(8,128)(2,1)} %bitcast.21), channel_id=1, source_target_pairs={{0,32},{32,0},{64,96},{96,64},{128,160},{160,128},{192,224},{224,1... | collective-permute-start | bytes 6291464 | tf_op jit(solution)/shard_map/ppermute | solution.py:487
  0.8 35.4 %collective-permute-start.5 = (bf16[2048,512]{1,0:T(8,128)(2,1)}, bf16[2048,512]{1,0:T(8,128)(2,1)}, u32[]{:S(2)}, u32[]{:S(2)}) collective-permute-start(bf16[2048,512]{1,0:T(8,128)(2,1)} %bitcast.23), channel_id=1, source_target_pairs={{0,32},{32,0},{64,96},{96,64},{128,160},{160,128},{192,224},{224,1... | collective-permute-start | bytes 6291464 | tf_op jit(solution)/shard_map/ppermute | solution.py:487
  1.2 19.5 %collective-permute-start.1 = (bf16[192,1536]{1,0:T(8,128)(2,1)}, bf16[192,1536]{1,0:T(8,128)(2,1)S(1)}, u32[]{:S(2)}, u32[]{:S(2)}) collective-permute-start(bf16[192,1536]{1,0:T(8,128)(2,1)} %bitcast.25), channel_id=1, source_target_pairs={{0,32},{32,0},{64,96},{96,64},{128,160},{160,128},{192,224},{224,1... | collective-permute-start | bytes 1769480 | tf_op jit(solution)/shard_map/ppermute | solution.py:487
  1.4 10.5 %collective-permute-start.2 = (bf16[64,1536]{1,0:T(8,128)(2,1)}, bf16[64,1536]{1,0:T(8,128)(2,1)S(1)}, u32[]{:S(2)}, u32[]{:S(2)}) collective-permute-start(bf16[64,1536]{1,0:T(8,128)(2,1)} %bitcast.27), channel_id=1, source_target_pairs={{0,32},{32,0},{64,96},{96,64},{128,160},{160,128},{192,224},{224,1... | collective-permute-start | bytes 589832 | tf_op jit(solution)/shard_map/ppermute | solution.py:487
  1.8 19.0 %collective-permute-start.3 = (bf16[64,1536]{1,0:T(8,128)(2,1)}, bf16[64,1536]{1,0:T(8,128)(2,1)}, u32[]{:S(2)}, u32[]{:S(2)}) collective-permute-start(bf16[64,1536]{1,0:T(8,128)(2,1)} %bitcast.29), channel_id=1, source_target_pairs={{0,32},{32,0},{64,96},{96,64},{128,160},{160,128},{192,224},{224,1... | collective-permute-start | bytes 589832 | tf_op jit(solution)/shard_map/ppermute | solution.py:487
  3.4 17.4 %all-to-all-start = ((bf16[4,8,1536]{2,1,0:T(8,128)(2,1)}), bf16[4,8,1536]{2,1,0:T(8,128)(2,1)S(1)}, u32[]{:S(2)}, u32[]{:S(2)}) async-start(bf16[4,8,1536]{2,1,0:T(8,128)(2,1)} %shard_map.202.order_ref), calls=%async_computation | async-start | bytes 196608 | tf_op jit(solution)/shard_map/all_to_all | solution.py:482
  11.8 0.7 copy-start
  12.5 36.7 %collective-permute-start.8 = (bf16[192,1536]{1,0:T(8,128)(2,1)}, bf16[192,1536]{1,0:T(8,128)(2,1)S(1)}, u32[]{:S(2)}, u32[]{:S(2)}) collective-permute-start(bf16[192,1536]{1,0:T(8,128)(2,1)} %w_ref.1), channel_id=1, source_target_pairs={{0,32},{32,0},{64,96},{96,64},{128,160},{160,128},{192,224},{224,1... | collective-permute-start | bytes 1769480 | tf_op jit(solution)/shard_map/ppermute | solution.py:487
  20.8 0.9 copy-start.1
  24.4 11.7 %all-to-all-start.1 = ((bf16[4,96,128]{2,1,0:T(8,128)(2,1)}), bf16[4,96,128]{2,1,0:T(8,128)(2,1)S(1)}, u32[]{:S(2)}, u32[]{:S(2)}) async-start(bf16[4,96,128]{2,1,0:T(8,128)(2,1)} %get-tuple-element.26.q_ref), calls=%async_computation.1 | async-start | bytes 196608 | tf_op jit(solution)/shard_map/all_to_all | solution.py:482
  28.5 3.8 %collective-permute-start.6 = (bf16[2,2,16,512]{3,2,1,0:T(8,128)(2,1)S(1)}, bf16[2,2,16,512]{3,2,1,0:T(8,128)(2,1)S(1)}, u32[]{:S(2)}, u32[]{:S(2)}) collective-permute-start(bf16[2,2,16,512]{3,2,1,0:T(8,128)(2,1)S(1)} %shard_map.205.own_ref.refs_0_), channel_id=1, source_target_pairs={{0,32},{32,0},{64,96},{96,64},{128,160},{160,128},{192,224},{224,1... | collective-permute-start | bytes 196616 | tf_op jit(solution)/shard_map/ppermute | solution.py:487
  28.5 1.3 %collective-permute-start = (s32[1,16]{1,0:T(1,128)S(1)}, s32[1,16]{1,0:T(1,128)S(1)}, u32[]{:S(2)}, u32[]{:S(2)}) collective-permute-start(s32[1,16]{1,0:T(1,128)S(1)} %copy-done.3), channel_id=1, source_target_pairs={{0,32},{32,0},{64,96},{96,64},{128,160},{160,128},{192,224},{224,1... | collective-permute-start | bytes 200 | tf_op jit(solution)/shard_map/ppermute | solution.py:487
  29.9 1.2 %collective-permute-start.7 = (bf16[2,32,128]{2,1,0:T(8,128)(2,1)S(1)}, bf16[2,32,128]{2,1,0:T(8,128)(2,1)S(1)}, u32[]{:S(2)}, u32[]{:S(2)}) collective-permute-start(bf16[2,32,128]{2,1,0:T(8,128)(2,1)S(1)} %get-tuple-element.27.kv_ref), channel_id=1, source_target_pairs={{0,32},{32,0},{64,96},{96,64},{128,160},{160,128},{192,224},{224,1... | collective-permute-start | bytes 49160 | tf_op jit(solution)/shard_map/ppermute | solution.py:487
  45.8 12.6 %all-to-all-start.2 = ((bf16[4,40,512]{2,1,0:T(8,128)(2,1)}), bf16[4,40,512]{2,1,0:T(8,128)(2,1)S(1)}, u32[]{:S(2)}, u32[]{:S(2)}) async-start(bf16[4,40,512]{2,1,0:T(8,128)(2,1)} %shard_map.207), calls=%async_computation.2 | async-start | bytes 327680 | tf_op jit(solution)/shard_map/all_to_all | solution.py:482
  60.8 11.7 %all-to-all-start.3 = ((bf16[4,8,1536]{2,1,0:T(8,128)(2,1)}), bf16[4,8,1536]{2,1,0:T(8,128)(2,1)S(1)}, u32[]{:S(2)}, u32[]{:S(2)}) async-start(bf16[4,8,1536]{2,1,0:T(8,128)(2,1)} %shard_map.208.order_ref), calls=%async_computation.3 | async-start | bytes 196608 | tf_op jit(solution)/shard_map/all_to_all | solution.py:482
  74.3 17.8 %all-to-all-start.4 = ((bf16[32,4,1536]{2,1,0:T(4,128)(2,1)}), bf16[32,4,1536]{2,1,0:T(4,128)(2,1)S(1)}, u32[]{:S(2)}, u32[]{:S(2)}) async-start(bf16[32,4,1536]{2,1,0:T(4,128)(2,1)} %get-tuple-element.36), calls=%async_computation.4 | async-start | bytes 786432 | tf_op jit(solution)/shard_map/all_to_all | solution.py:479
  82.1 14.1 %collective-permute-start.10 = (bf16[2,2,16,512]{3,2,1,0:T(8,128)(2,1)S(1)}, bf16[2,2,16,512]{3,2,1,0:T(8,128)(2,1)S(1)}, u32[]{:S(2)}, u32[]{:S(2)}) collective-permute-start(bf16[2,2,16,512]{3,2,1,0:T(8,128)(2,1)S(1)} %shard_map.205.own_ref.refs_0_), channel_id=1, source_target_pairs={{0,128},{32,160},{64,192},{96,224},{128,0},{160,32},{192,64},{224,... | collective-permute-start | bytes 196616 | tf_op jit(solution)/shard_map/ppermute | solution.py:487
  83.4 12.8 %collective-permute-start.11 = (bf16[2,2,16,512]{3,2,1,0:T(8,128)(2,1)S(1)}, bf16[2,2,16,512]{3,2,1,0:T(8,128)(2,1)S(1)}, u32[]{:S(2)}, u32[]{:S(2)}) collective-permute-start(bf16[2,2,16,512]{3,2,1,0:T(8,128)(2,1)S(1)} %shard_map.205.own_ref.refs_0_), channel_id=1, source_target_pairs={{0,192},{32,224},{64,128},{96,160},{128,64},{160,96},{192,0},{224,... | collective-permute-start | bytes 196616 | tf_op jit(solution)/shard_map/ppermute | solution.py:487
  86.6 9.6 %collective-permute-start.9 = (bf16[2,2,16,512]{3,2,1,0:T(8,128)(2,1)S(1)}, bf16[2,2,16,512]{3,2,1,0:T(8,128)(2,1)S(1)}, u32[]{:S(2)}, u32[]{:S(2)}) collective-permute-start(bf16[2,2,16,512]{3,2,1,0:T(8,128)(2,1)S(1)} %shard_map.205.own_ref.refs_0_), channel_id=1, source_target_pairs={{0,64},{32,96},{64,0},{96,32},{128,192},{160,224},{192,128},{224,1... | collective-permute-start | bytes 196616 | tf_op jit(solution)/shard_map/ppermute | solution.py:487
  96.2 13.7 %all-to-all-start.5 = ((bf16[32,4,1536]{2,1,0:T(4,128)(2,1)}), bf16[32,4,1536]{2,1,0:T(4,128)(2,1)S(1)}, u32[]{:S(2)}, u32[]{:S(2)}) async-start(bf16[32,4,1536]{2,1,0:T(4,128)(2,1)} %shard_map.211), calls=%async_computation.5 | async-start | bytes 786432 | tf_op jit(solution)/shard_map/all_to_all | solution.py:479
  101.1 1.3 %collective-permute-start.12 = (bf16[2,2,16,512]{3,2,1,0:T(8,128)(2,1)S(1)}, bf16[2,2,16,512]{3,2,1,0:T(8,128)(2,1)S(1)}, u32[]{:S(2)}, u32[]{:S(2)}) collective-permute-start(bf16[2,2,16,512]{3,2,1,0:T(8,128)(2,1)S(1)} %collective-permute-done.9.refs_2_), channel_id=1, source_target_pairs={{0,32},{32,0},{64,96},{96,64},{128,160},{160,128},{192,224},{224,1... | collective-permute-start | bytes 196616 | tf_op jit(solution)/shard_map/ppermute | solution.py:487
  101.2 1.4 %collective-permute-start.13 = (bf16[2,2,16,512]{3,2,1,0:T(8,128)(2,1)S(1)}, bf16[2,2,16,512]{3,2,1,0:T(8,128)(2,1)S(1)}, u32[]{:S(2)}, u32[]{:S(2)}) collective-permute-start(bf16[2,2,16,512]{3,2,1,0:T(8,128)(2,1)S(1)} %collective-permute-done.10.refs_4_), channel_id=1, source_target_pairs={{0,32},{32,0},{64,96},{96,64},{128,160},{160,128},{192,224},{224,1... | collective-permute-start | bytes 196616 | tf_op jit(solution)/shard_map/ppermute | solution.py:487
  101.7 1.3 %collective-permute-start.14 = (bf16[2,2,16,512]{3,2,1,0:T(8,128)(2,1)S(1)}, bf16[2,2,16,512]{3,2,1,0:T(8,128)(2,1)S(1)}, u32[]{:S(2)}, u32[]{:S(2)}) collective-permute-start(bf16[2,2,16,512]{3,2,1,0:T(8,128)(2,1)S(1)} %collective-permute-done.11.refs_6_), channel_id=1, source_target_pairs={{0,32},{32,0},{64,96},{96,64},{128,160},{160,128},{192,224},{224,1... | collective-permute-start | bytes 196616 | tf_op jit(solution)/shard_map/ppermute | solution.py:487

commit v5 on v4

--- a/solution.py
+++ b/solution.py
@@ -228,60 +228,106 @@
     bias_ref,
     extra_ref,
     q_ref,
-    k_ref,
-    v_ref,
-    other_k_ref,
-    other_v_ref,
     own_ref,
     other_own_ref,
     pick_ref,
-    out_ref,
-    s_ref,
-    p_ref,
+    *refs,
 ):
+    sources, out_ref, held = refs[0:4], refs[4], refs[5:9]
+    score_refs, prob_refs, top_ref, sem = refs[9:11], refs[11:13], refs[13], refs[14]
+    k_ref, v_ref, other_k_ref, other_v_ref = held
     rows = extra_ref.shape[0]
     half = k_ref.shape[0]
     keys = 2 * half
     own_keys = own_ref.shape[1] * own_ref.shape[2]
-    q = split_heads(q_ref.at[0], rows)
+    pairs = q_ref.shape[0]
+    chunk = 512
+    chunks = keys // chunk
     fill = jnp.zeros((128 - 2 * own_keys, 128), BF16)
-    extra = [
-        jnp.concatenate(
-            [
-                own_ref[i].reshape(own_keys, 128),
-                other_own_ref[i].reshape(own_keys, 128),
-                fill,
-            ],
-            axis=0,
-        )
-        for i in range(2)
-    ]
-    s_ref[:, 0:half] = dot_t(q, k_ref[...])
-    s_ref[:, half:keys] = dot_t(q, other_k_ref[...])
-    s_ref[:, keys : keys + 128] = dot_t(q, extra[0])
-    lse, total = [], []
-    for i in range(6):
+
+    def lane_span(pair):
+        return slice(pair * 128, (pair + 1) * 128)
+
+    copies = {}
+    for pair in range(pairs):
+        for i in (0, 2, 1, 3):
+            copies[pair, i] = pltpu.make_async_copy(
+                sources[i].at[:, lane_span(pair)], held[i].at[:, lane_span(pair)], sem.at[pair, i]
+            )
+            copies[pair, i].start()
+
+    def extra(pair, i):
+        both = [r[i, :, :, lane_span(pair)].reshape(own_keys, 128) for r in (own_ref, other_own_ref)]
+        return jnp.concatenate([*both, fill], axis=0)
+
+    def fold(x):
+        tiles = [x[:, at : at + 128] for at in range(0, x.shape[1], 128)]
+        return functools.reduce(jnp.maximum, tiles)
+
+    queries = {}
+
+    def score(pair, i):
+        s_ref = score_refs[pair % 2]
+        if i == 0:
+            copies[pair, 0].wait()
+            queries[pair] = split_heads(q_ref.at[pair], rows)
+            s = dot_t(queries[pair], extra(pair, 0))
+            s = s + jnp.concatenate([extra_ref[...]] * 6, axis=0)
+            s_ref[:, keys:] = s
+            top = s
+        else:
+            top = top_ref[...]
+        at = i * chunk
+        source, start = (k_ref, at) if at < half else (other_k_ref, at - half)
+        if at == half:
+            copies[pair, 2].wait()
+        s = dot_t(queries[pair], source[start : start + chunk, lane_span(pair)])
+        s = s + bias_ref[0:1, at : at + chunk]
+        s_ref[:, at : at + chunk] = s
+        top_ref[...] = jnp.maximum(top, fold(s))
+
+    tops, totals = {}, {}
+
+    def soften(pair, i):
+        s_ref, p_ref = score_refs[pair % 2], prob_refs[pair % 2]
         span = slice(i * rows, (i + 1) * rows)
-        s0 = s_ref[span, 0:keys] + bias_ref[0:1, :]
-        s1 = s_ref[span, keys : keys + 128] + extra_ref[...]
-        top = jnp.maximum(
-            jnp.max(s0, axis=-1, keepdims=True), jnp.max(s1, axis=-1, keepdims=True)
-        )
-        e0 = jnp.exp(s0 - top)
-        e1 = jnp.exp(s1 - top)
-        p_ref[span, 0:keys] = e0.astype(BF16)
-        p_ref[span, keys : keys + 128] = e1.astype(BF16)
-        denominator = jnp.sum(e0, axis=-1, keepdims=True) + jnp.sum(e1, axis=-1, keepdims=True)
-        total.append(denominator)
-        lse.append(top + jnp.log(denominator))
-    o = dot(p_ref[:, 0:half], v_ref[...]) + dot(p_ref[:, half:keys], other_v_ref[...])
-    o = o + dot(p_ref[:, keys : keys + 128], extra[1])
-
-    def store(j, tile):
-        out_ref[0, 0:rows, j * 128 : (j + 1) * 128] = tile
-
-    pack_partial(o, total, lse, rows, store)
-    out_ref[0, rows:, :] = pick_ref[0]
+        top = tops[pair][span, :]
+        total = jnp.zeros((rows, 128), F32)
+        for at in range(0, keys + 128, 128):
+            e = jnp.exp(s_ref[span, at : at + 128] - top)
+            total = total + e
+            p_ref[span, at : at + 128] = e.astype(BF16)
+        totals[pair, i] = jnp.sum(total, axis=-1, keepdims=True)
+
+    summed = {}
+
+    def weigh(pair, part):
+        p_ref = prob_refs[pair % 2]
+        copies[pair, 1 + 2 * part].wait()
+        if part == 0:
+            summed[pair] = dot(p_ref[:, 0:half], v_ref[:, lane_span(pair)])
+            return
+        o = summed[pair] + dot(p_ref[:, half:keys], other_v_ref[:, lane_span(pair)])
+        o = o + dot(p_ref[:, keys:], extra(pair, 1))
+        total = [totals[pair, i] for i in range(6)]
+        lse = [tops[pair][i * rows : (i + 1) * rows, :] + jnp.log(total[i]) for i in range(6)]
+
+        def store(j, tile):
+            out_ref[pair, 0:rows, lane_span(j)] = tile
+
+        pack_partial(o, total, lse, rows, store)
+        out_ref[pair, rows:, :] = pick_ref[pair]
+
+    for turn in range(pairs + 2):
+        for i in range(chunks):
+            if turn < pairs:
+                score(turn, i)
+            if 0 <= turn - 1 < pairs and i < 6:
+                soften(turn - 1, i)
+            if turn >= 2 and i in (3, 6):
+                weigh(turn - 2, 0 if i == 3 else 1)
+        if turn < pairs:
+            tops[turn] = jnp.max(top_ref[...], axis=-1, keepdims=True)
 
 
 def join_kernel(part_ref, fresh_ref, seq_ref, w_ref, other_w_ref, out_ref):
@@ -352,14 +398,22 @@
         out_ref[e] = buffer[e * capacity : (e + 1) * capacity, :].astype(BF16)
 
 
-def expert_kernel(x_ref, w_in_ref, w_out_ref, out_ref, rows_ref):
+def expert_kernel(x_hbm, w_in_hbm, w_out_hbm, out_ref, x_ref, w_in_ref, w_out_ref, rows_ref, sem):
+    pairs = ((x_hbm, x_ref), (w_in_hbm, w_in_ref), (w_out_hbm, w_out_ref))
+    copies = [pltpu.make_async_copy(a, b, sem.at[i]) for i, (a, b) in enumerate(pairs)]
+    for copy in copies:
+        copy.start()
     sources, capacity = x_ref.shape[0], x_ref.shape[1]
+    copies[0].wait()
     for s in range(sources):
         rows_ref[s * capacity : (s + 1) * capacity, :] = x_ref[s].astype(F32)
-    projected = dot(rows_ref[...].astype(BF16), w_in_ref[0])
+    x = rows_ref[...].astype(BF16)
+    copies[1].wait()
+    projected = dot(x, w_in_ref[0])
     half = projected.shape[1] // 2
     g, u = projected[:, 0:half], projected[:, half:]
     act = (g * jax.nn.sigmoid(g) * u).astype(BF16)
+    copies[2].wait()
     out = dot(act, w_out_ref[0])
     for s in range(sources):
         out_ref[s] = out[s * capacity : (s + 1) * capacity, :].astype(BF16)
@@ -419,7 +473,7 @@
     return pl.BlockSpec(shape, lambda i: (0,) * len(shape))
 
 
-def call(kernel, outs, *args, ins=(), scratch=(), mib=48):
+def call(kernel, outs, *args, ins=(), scratch=(), mib=32):
     specs = list(ins) + [block(a.shape) for a in args[len(ins) :]]
     return pl.pallas_call(
         kernel,
@@ -490,12 +544,12 @@
         return apart(a, 1)
 
     normed = call(norm_kernel, shaped((n_chips, local_rows, width)), x, stay(gain_attn))
+    weights = [w_query.T, key_projection_weight.T, value_projection_weight.T]
+    prompt = [prompt_key_cache[0], prompt_value_cache[0]]
+    normed, *traded = lax.optimization_barrier((normed, *weights, *prompt, w_output))
     normed_all = exchange_chips(normed)
-    weights = [w_query.T, key_projection_weight.T, value_projection_weight.T]
-    other_weights = [of_other_core(w) for w in weights]
-    prompt = [prompt_key_cache[0], prompt_value_cache[0]]
-    other_prompt = [of_other_core(a) for a in prompt]
-    other_w_output = of_other_core(w_output)
+    traded = [of_other_core(a) for a in traded]
+    other_weights, other_prompt, other_w_output = traded[:3], traded[3:5], traded[5]
     own = call(
         pack_kernel,
         shaped((2, here, tail, kv_width)),
@@ -543,36 +597,31 @@
         final,
     )
 
-    held = pl.BlockSpec((keys, 128), lambda p: (0, p))
-    held_own = pl.BlockSpec((2, here, tail, 128), lambda p: (0, 0, 0, p))
+    resident = pl.BlockSpec(memory_space=pltpu.VMEM)
+    operands = (bias, extra, q_all, own, other_own, pick)
+    partial_shape = shaped((n_chips, rows + local_rows, 512))
     partial = pl.pallas_call(
         attend_kernel,
-        grid=(kv_width // 128,),
-        out_shape=shaped((n_chips, rows + local_rows, 512)),
-        in_specs=[
-            pl.BlockSpec((8, 2 * keys), lambda p: (0, 0)),
-            pl.BlockSpec((rows, 128), lambda p: (0, 0)),
-            pl.BlockSpec((1, 3 * rows, 128), lambda p: (p, 0, 0)),
-            held,
-            held,
-            held,
-            held,
-            held_own,
-            held_own,
-            pl.BlockSpec((1, local_rows, 512), lambda p: (p, 0, 0)),
-        ],
-        out_specs=pl.BlockSpec((1, rows + local_rows, 512), lambda p: (p, 0, 0)),
-        scratch_shapes=[
+        grid=(1,),
+        out_shape=partial_shape,
+        in_specs=[resident] * len(operands) + [anywhere] * 4,
+        out_specs=block(partial_shape.shape),
+        scratch_shapes=[pltpu.VMEM((keys, kv_width), BF16)] * 4
+        + [
+            pltpu.VMEM((6 * rows, 2 * keys + 128), F32),
             pltpu.VMEM((6 * rows, 2 * keys + 128), F32),
             pltpu.VMEM((6 * rows, 2 * keys + 128), BF16),
+            pltpu.VMEM((6 * rows, 2 * keys + 128), BF16),
+            pltpu.VMEM((6 * rows, 128), F32),
+            pltpu.SemaphoreType.DMA((kv_width // 128, 4)),
         ],
-        compiler_params=params(48),
+        compiler_params=params(32),
         cost_estimate=pl.CostEstimate(
             flops=4 * 24 * rows * 2 * keys * HEAD,
             bytes_accessed=8 * keys * kv_width,
             transcendentals=24 * rows * 2 * keys,
         ),
-    )(bias, extra, q_all, *map(stay, prompt), *other_prompt, own, other_own, pick)
+    )(*operands, *map(stay, prompt), *other_prompt)
     parts = exchange_chips(partial)
     sums = call(
         join_kernel,
@@ -611,7 +660,14 @@
         buffer,
         stay(w_in),
         stay(w_out),
-        scratch=[pltpu.VMEM((slots, width), F32)],
+        ins=[anywhere] * 3,
+        scratch=[
+            pltpu.VMEM(buffer.shape, BF16),
+            pltpu.VMEM(w_in.shape, BF16),
+            pltpu.VMEM(w_out.shape, BF16),
+            pltpu.VMEM((slots, width), F32),
+            pltpu.SemaphoreType.DMA((3,)),
+        ],
     )
     back, *even = lax.optimization_barrier((back, *even))
     odd = [other_own] + [apart(a, 1) for a in even[1:]]

time: 112 us -> 112 us (level)
  transfers between devices with their start and end apart: 21 -> 21, of which waited for: 11 -> 11; matrix products, arithmetic and copies ran while one was open for 0% -> 0% of each run, Pallas kernels for 21% -> 20%
where the time goes in v5:
time: 112 us; the launch traced here: 111 us
  starting transfers between devices  40.6 us (36%)
  waiting for transfers between devices  39.7 us (35%)
  Pallas kernels  28.5 us (25%)
  local copies, waits for them, and re-layouts  1.61 us (1%)
    all_to_all x4, waiting for transfers between devices, exchange_chips(): lax.all_to_all(a, 'seq', split_axis=0, concat_axis=0, tiled=True, axis_in...  28.6 us
    all_to_all x4, starting transfers between devices, exchange_chips(): lax.all_to_all(a, 'seq', split_axis=0, concat_axis=0, tiled=True, axis_in...  18.4 us
    pallas_call x11, Pallas kernels, call(): pl.pallas_call(kernel, grid=(1,), out_shape=outs, in_specs=specs, out_spe...  18.4 us
    all_to_all x2, starting transfers between devices, exchange(): return lax.all_to_all(a, axis, split_axis=0, concat_axis=0, tiled=True)  12.8 us
    pallas_call x1, Pallas kernels, local(): pl.pallas_call(attend_kernel, grid=(1,), out_shape=partial_shape, in_spec...  10.1 us
    ppermute x15, starting transfers between devices, apart(): return lax.ppermute(a, 'seq', [(i, i ^ distance) for i in range(n_seq)])  9.33 us
    all_to_all x2, waiting for transfers between devices, exchange(): return lax.all_to_all(a, axis, split_axis=0, concat_axis=0, tiled=True)  9.01 us
  transfers between devices with their start and end apart: 21, of which 11 were waited for; matrix products, arithmetic and copies ran while one was open for 0% of the time, Pallas kernels for 20%

profile of v5, /device:TPU:8, one launch (start us, length us, event | category | flops | bytes accessed | tf_op | source)
XLA Modules:
  0.0 111.1 jit_solution(9025266935364864645)
XLA Ops:
  0.7 1.5 %shard_map.202.order_ref = bf16[4,8,1536]{2,1,0:T(8,128)(2,1)} custom-call(bf16[2,4,1536]{2,1,0:T(4,128)(2,1)} %bitcast.31, f32[1536]{0:T(1024)} %gain_ref.2), custom_call_target="tpu_custom_call" | custom-call | flops 1048576 | bytes 1048576 | tf_op jit(solution)/shard_map/pallas_call | solution.py:478
  2.2 0.5 collective-permute-start.7
  3.2 8.5 %all-to-all-start = ((bf16[4,8,1536]{2,1,0:T(8,128)(2,1)}), bf16[4,8,1536]{2,1,0:T(8,128)(2,1)S(1)}, u32[]{:S(2)}, u32[]{:S(2)}) async-start(bf16[4,8,1536]{2,1,0:T(8,128)(2,1)} %shard_map.202.order_ref), calls=%async_computation | async-start | bytes 196608 | tf_op jit(solution)/shard_map/all_to_all | solution.py:536
  11.6 0.7 copy-done
  12.5 8.0 %all-to-all-done.x_ref = bf16[4,8,1536]{2,1,0:T(8,128)(2,1)S(1)} async-done(((bf16[4,8,1536]{2,1,0:T(8,128)(2,1)}), bf16[4,8,1536]{2,1,0:T(8,128)(2,1)S(1)}, u32[]{:S(2)}, u32[]{:S(2)}) %all-to-all-start) | async-done | bytes 98336 | tf_op jit(solution)/shard_map/all_to_all | solution.py:536
  20.6 0.9 copy-done.1
  21.5 2.7 %shard_map.204 = (bf16[4,96,128]{2,1,0:T(8,128)(2,1)}, bf16[2,32,128]{2,1,0:T(8,128)(2,1)S(1)}) custom-call(bf16[4,8,1536]{2,1,0:T(8,128)(2,1)S(1)} %all-to-all-done.x_ref, s32[1]{0:T(128)} %bitcast.6.seq_ref, bf16[192,1536]{1,0:T(8,128)(2,1)} %bitcast.26, bf16[64,1536]{1,0:T(8,128)(2,1)} %bitcast.28, bf16[64,1536]{1,0:T(8,128)(2,1)} %bitcast.30, ...), custom_call_target="tpu_custom_call" | custom-call | flops 1048576 | bytes 1048576 | tf_op jit(solution)/shard_map/pallas_call | solution.py:478
  24.2 3.3 %all-to-all-start.1 = ((bf16[4,96,128]{2,1,0:T(8,128)(2,1)}), bf16[4,96,128]{2,1,0:T(8,128)(2,1)S(1)}, u32[]{:S(2)}, u32[]{:S(2)}) async-start(bf16[4,96,128]{2,1,0:T(8,128)(2,1)} %get-tuple-element.37.q_ref), calls=%async_computation.1 | async-start | bytes 196608 | tf_op jit(solution)/shard_map/all_to_all | solution.py:536
  27.5 0.8 shard_map.205.own_ref.refs_0_
  28.8 0.8 collective-permute-done.other_len_ref
  30.0 0.8 shard_map.203
  30.8 1.3 %shard_map.206 = (bf16[32,512]{1,0:T(8,128)(2,1)S(1)}, bf16[4,8,512]{2,1,0:T(8,128)(2,1)S(1)}) custom-call(bf16[4,96,128]{2,1,0:T(8,128)(2,1)} %get-tuple-element.37.q_ref, bf16[2,32,128]{2,1,0:T(8,128)(2,1)S(1)} %get-tuple-element.38.kv_ref, bf16[2,32,128]{2,1,0:T(8,128)(2,1)S(1)} %collective-permute-done.5.other_ref, ...), custom_call_target="tpu_custom_call" | custom-call | flops 1048576 | bytes 1048576 | tf_op jit(solution)/shard_map/pallas_call | solution.py:478
  32.1 3.9 %all-to-all-done.1.q_ref = bf16[4,96,128]{2,1,0:T(8,128)(2,1)S(1)} async-done(((bf16[4,96,128]{2,1,0:T(8,128)(2,1)}), bf16[4,96,128]{2,1,0:T(8,128)(2,1)S(1)}, u32[]{:S(2)}, u32[]{:S(2)}) %all-to-all-start.1) | async-done | bytes 98336 | tf_op jit(solution)/shard_map/all_to_all | solution.py:536
  36.0 10.1 %shard_map.207 = bf16[4,40,512]{2,1,0:T(8,128)(2,1)} custom-call(f32[8,4096]{1,0:T(8,128)S(1)} %get-tuple-element.32.bias_ref, f32[32,128]{1,0:T(8,128)S(1)} %get-tuple-element.33.extra_ref, bf16[4,96,128]{2,1,0:T(8,128)(2,1)S(1)} %all-to-all-done.1.q_ref, bf16[2,2,16,512]{3,2,1,0:T(8,128)(2,1)S(1)} %shard_map.205.own_ref.refs_0_, ...), custom_call_target="tpu_custom_call" | custom-call | flops 805306368 | bytes 8388608 | tf_op jit(solution)/shard_map/pallas_call | solution.py:603
  46.1 3.4 %all-to-all-start.2 = ((bf16[4,40,512]{2,1,0:T(8,128)(2,1)}), bf16[4,40,512]{2,1,0:T(8,128)(2,1)S(1)}, u32[]{:S(2)}, u32[]{:S(2)}) async-start(bf16[4,40,512]{2,1,0:T(8,128)(2,1)} %shard_map.207), calls=%async_computation.2 | async-start | bytes 327680 | tf_op jit(solution)/shard_map/all_to_all | solution.py:536
  49.5 9.2 %all-to-all-done.2.part_ref = bf16[4,40,512]{2,1,0:T(8,128)(2,1)S(1)} async-done(((bf16[4,40,512]{2,1,0:T(8,128)(2,1)}), bf16[4,40,512]{2,1,0:T(8,128)(2,1)S(1)}, u32[]{:S(2)}, u32[]{:S(2)}) %all-to-all-start.2) | async-done | bytes 163872 | tf_op jit(solution)/shard_map/all_to_all | solution.py:536
  58.7 2.4 %shard_map.208.order_ref = bf16[4,8,1536]{2,1,0:T(8,128)(2,1)} custom-call(bf16[4,40,512]{2,1,0:T(8,128)(2,1)S(1)} %all-to-all-done.2.part_ref, bf16[32,512]{1,0:T(8,128)(2,1)S(1)} %get-tuple-element.44.fresh_ref, s32[1]{0:T(128)} %bitcast.6.seq_ref, bf16[192,1536]{1,0:T(8,128)(2,1)} %w_ref.1, bf16[192,1536]{1,0:T(8,128)(2,1)S(1)} %collective-permute-done.8.other_w_ref), custom_call_target="tpu_custom_call" | custom-call | flops 1048576 | bytes 1048576 | tf_op jit(solution)/shard_map/pallas_call | solution.py:478
  61.0 3.3 %all-to-all-start.3 = ((bf16[4,8,1536]{2,1,0:T(8,128)(2,1)}), bf16[4,8,1536]{2,1,0:T(8,128)(2,1)S(1)}, u32[]{:S(2)}, u32[]{:S(2)}) async-start(bf16[4,8,1536]{2,1,0:T(8,128)(2,1)} %shard_map.208.order_ref), calls=%async_computation.3 | async-start | bytes 196608 | tf_op jit(solution)/shard_map/all_to_all | solution.py:536
  64.4 1.0 shard_map.209
  65.4 7.4 %all-to-all-done.3.sums_ref = bf16[4,8,1536]{2,1,0:T(8,128)(2,1)S(1)} async-done(((bf16[4,8,1536]{2,1,0:T(8,128)(2,1)}), bf16[4,8,1536]{2,1,0:T(8,128)(2,1)S(1)}, u32[]{:S(2)}, u32[]{:S(2)}) %all-to-all-start.3) | async-done | bytes 98336 | tf_op jit(solution)/shard_map/all_to_all | solution.py:536
  72.8 1.8 %shard_map.210 = (f32[8,1536]{1,0:T(8,128)S(1)}, bf16[32,4,1536]{2,1,0:T(4,128)(2,1)}) custom-call(bf16[2,4,1536]{2,1,0:T(4,128)(2,1)} %bitcast.32, bf16[4,8,1536]{2,1,0:T(8,128)(2,1)S(1)} %all-to-all-done.3.sums_ref, f32[1536]{0:T(1024)} %gain_ref.3, bf16[128,8]{1,0:T(8,128)(2,1)S(1)} %get-tuple-element.46.place_ref), custom_call_target="tpu_custom_call" | custom-call | flops 1048576 | bytes 1048576 | tf_op jit(solution)/shard_map/pallas_call | solution.py:478
  74.6 7.7 %all-to-all-start.4 = ((bf16[32,4,1536]{2,1,0:T(4,128)(2,1)}), bf16[32,4,1536]{2,1,0:T(4,128)(2,1)S(1)}, u32[]{:S(2)}, u32[]{:S(2)}) async-start(bf16[32,4,1536]{2,1,0:T(4,128)(2,1)} %get-tuple-element.50), calls=%async_computation.4 | async-start | bytes 786432 | tf_op jit(solution)/shard_map/all_to_all | solution.py:533
  82.4 0.6 collective-permute-start.10
  83.0 3.9 %collective-permute-start.11 = (bf16[2,2,16,512]{3,2,1,0:T(8,128)(2,1)S(1)}, bf16[2,2,16,512]{3,2,1,0:T(8,128)(2,1)S(1)}, u32[]{:S(2)}, u32[]{:S(2)}) collective-permute-start(bf16[2,2,16,512]{3,2,1,0:T(8,128)(2,1)S(1)} %shard_map.205.own_ref.refs_0_), channel_id=1, source_target_pairs={{0,192},{32,224},{64,128},{96,160},{128,64},{160,96},{192,0},{224,... | collective-permute-start | bytes 196616 | tf_op jit(solution)/shard_map/ppermute | solution.py:541
  86.8 2.1 %collective-permute-start.9 = (bf16[2,2,16,512]{3,2,1,0:T(8,128)(2,1)S(1)}, bf16[2,2,16,512]{3,2,1,0:T(8,128)(2,1)S(1)}, u32[]{:S(2)}, u32[]{:S(2)}) collective-permute-start(bf16[2,2,16,512]{3,2,1,0:T(8,128)(2,1)S(1)} %shard_map.205.own_ref.refs_0_), channel_id=1, source_target_pairs={{0,64},{32,96},{64,0},{96,32},{128,192},{160,224},{192,128},{224,1... | collective-permute-start | bytes 196616 | tf_op jit(solution)/shard_map/ppermute | solution.py:541
  89.0 3.5 %all-to-all-done.4.x_hbm = bf16[32,4,1536]{2,1,0:T(4,128)(2,1)S(1)} async-done(((bf16[32,4,1536]{2,1,0:T(4,128)(2,1)}), bf16[32,4,1536]{2,1,0:T(4,128)(2,1)S(1)}, u32[]{:S(2)}, u32[]{:S(2)}) %all-to-all-start.4) | async-done | bytes 393248 | tf_op jit(solution)/shard_map/all_to_all | solution.py:533
  92.5 3.8 %shard_map.211 = bf16[32,4,1536]{2,1,0:T(4,128)(2,1)} custom-call(bf16[32,4,1536]{2,1,0:T(4,128)(2,1)S(1)} %all-to-all-done.4.x_hbm, bf16[1,1536,1024]{2,1,0:T(8,128)(2,1)} %w_in_hbm.1, bf16[1,512,1536]{2,1,0:T(8,128)(2,1)} %w_out_hbm.1), custom_call_target="tpu_custom_call" | custom-call | flops 1048576 | bytes 1048576 | tf_op jit(solution)/shard_map/pallas_call | solution.py:478
  96.3 5.1 %all-to-all-start.5 = ((bf16[32,4,1536]{2,1,0:T(4,128)(2,1)}), bf16[32,4,1536]{2,1,0:T(4,128)(2,1)S(1)}, u32[]{:S(2)}, u32[]{:S(2)}) async-start(bf16[32,4,1536]{2,1,0:T(4,128)(2,1)} %shard_map.211), calls=%async_computation.5 | async-start | bytes 786432 | tf_op jit(solution)/shard_map/all_to_all | solution.py:533
  102.1 0.6 collective-permute-done.12.refs_3_
  103.2 1.4 %shard_map.213 = (bf16[20,2,512]{2,1,0:T(2,128)(2,1)}, bf16[20,2,512]{2,1,0:T(2,128)(2,1)}) custom-call(s32[1]{0:T(128)} %bitcast.6.seq_ref, s32[4,16]{1,0:T(4,128)S(1)} %bitcast.20, bf16[4,40,512]{2,1,0:T(8,128)(2,1)S(1)} %all-to-all-done.2.part_ref, bf16[2,2,16,512]{3,2,1,0:T(8,128)(2,1)S(1)} %shard_map.205.own_ref.refs_0_, ...), custom_call_target="tpu_custom_call" | custom-call | flops 1048576 | bytes 1048576 | tf_op jit(solution)/shard_map/pallas_call | solution.py:478
  104.6 5.5 %all-to-all-done.5.back_ref = bf16[32,4,1536]{2,1,0:T(4,128)(2,1)S(1)} async-done(((bf16[32,4,1536]{2,1,0:T(4,128)(2,1)}), bf16[32,4,1536]{2,1,0:T(4,128)(2,1)S(1)}, u32[]{:S(2)}, u32[]{:S(2)}) %all-to-all-start.5) | async-done | bytes 393248 | tf_op jit(solution)/shard_map/all_to_all | solution.py:533
  110.1 1.0 shard_map.212
  (30 shorter events, 2.9 us)
Async XLA Ops:
  0.6 27.7 %copy-start.3 = (s32[1,16]{1,0:T(1,128)S(1)}, s32[1,16]{1,0:T(1,128)}, u32[]{:S(2)}) copy-start(s32[1,16]{1,0:T(1,128)} %len_ref.1) | copy-start | bytes 196
  0.6 29.3 %copy-start.2 = (s32[1,4,16]{2,1,0:T(4,128)S(1)}, s32[1,4,16]{2,1,0:T(4,128)}, u32[]{:S(2)}) copy-start(s32[1,4,16]{2,1,0:T(4,128)} %param.20) | copy-start | bytes 772
  2.2 33.8 %collective-permute-start.6 = (bf16[2048,512]{1,0:T(8,128)(2,1)}, bf16[2048,512]{1,0:T(8,128)(2,1)S(1)}, u32[]{:S(2)}, u32[]{:S(2)}) collective-permute-start(bf16[2048,512]{1,0:T(8,128)(2,1)} %bitcast.21), channel_id=1, source_target_pairs={{0,32},{32,0},{64,96},{96,64},{128,160},{160,128},{192,224},{224,1... | collective-permute-start | bytes 6291464 | tf_op jit(solution)/shard_map/ppermute | solution.py:541
  2.2 33.8 %collective-permute-start.7 = (bf16[2048,512]{1,0:T(8,128)(2,1)}, bf16[2048,512]{1,0:T(8,128)(2,1)}, u32[]{:S(2)}, u32[]{:S(2)}) collective-permute-start(bf16[2048,512]{1,0:T(8,128)(2,1)} %bitcast.23), channel_id=1, source_target_pairs={{0,32},{32,0},{64,96},{96,64},{128,160},{160,128},{192,224},{224,1... | collective-permute-start | bytes 6291464 | tf_op jit(solution)/shard_map/ppermute | solution.py:541
  2.7 17.9 %collective-permute-start.1 = (bf16[192,1536]{1,0:T(8,128)(2,1)}, bf16[192,1536]{1,0:T(8,128)(2,1)S(1)}, u32[]{:S(2)}, u32[]{:S(2)}) collective-permute-start(bf16[192,1536]{1,0:T(8,128)(2,1)} %bitcast.25), channel_id=1, source_target_pairs={{0,32},{32,0},{64,96},{96,64},{128,160},{160,128},{192,224},{224,1... | collective-permute-start | bytes 1769480 | tf_op jit(solution)/shard_map/ppermute | solution.py:541
  2.7 9.0 %collective-permute-start.2 = (bf16[64,1536]{1,0:T(8,128)(2,1)}, bf16[64,1536]{1,0:T(8,128)(2,1)S(1)}, u32[]{:S(2)}, u32[]{:S(2)}) collective-permute-start(bf16[64,1536]{1,0:T(8,128)(2,1)} %bitcast.27), channel_id=1, source_target_pairs={{0,32},{32,0},{64,96},{96,64},{128,160},{160,128},{192,224},{224,1... | collective-permute-start | bytes 589832 | tf_op jit(solution)/shard_map/ppermute | solution.py:541
  3.2 17.4 %collective-permute-start.3 = (bf16[64,1536]{1,0:T(8,128)(2,1)}, bf16[64,1536]{1,0:T(8,128)(2,1)}, u32[]{:S(2)}, u32[]{:S(2)}) collective-permute-start(bf16[64,1536]{1,0:T(8,128)(2,1)} %bitcast.29), channel_id=1, source_target_pairs={{0,32},{32,0},{64,96},{96,64},{128,160},{160,128},{192,224},{224,1... | collective-permute-start | bytes 589832 | tf_op jit(solution)/shard_map/ppermute | solution.py:541
  3.2 17.4 %all-to-all-start = ((bf16[4,8,1536]{2,1,0:T(8,128)(2,1)}), bf16[4,8,1536]{2,1,0:T(8,128)(2,1)S(1)}, u32[]{:S(2)}, u32[]{:S(2)}) async-start(bf16[4,8,1536]{2,1,0:T(8,128)(2,1)} %shard_map.202.order_ref), calls=%async_computation | async-start | bytes 196608 | tf_op jit(solution)/shard_map/all_to_all | solution.py:536
  11.6 0.7 copy-start
  12.3 37.1 %collective-permute-start.8 = (bf16[192,1536]{1,0:T(8,128)(2,1)}, bf16[192,1536]{1,0:T(8,128)(2,1)S(1)}, u32[]{:S(2)}, u32[]{:S(2)}) collective-permute-start(bf16[192,1536]{1,0:T(8,128)(2,1)} %w_ref.1), channel_id=1, source_target_pairs={{0,32},{32,0},{64,96},{96,64},{128,160},{160,128},{192,224},{224,1... | collective-permute-start | bytes 1769480 | tf_op jit(solution)/shard_map/ppermute | solution.py:541
  20.6 0.9 copy-start.1
  24.2 11.7 %all-to-all-start.1 = ((bf16[4,96,128]{2,1,0:T(8,128)(2,1)}), bf16[4,96,128]{2,1,0:T(8,128)(2,1)S(1)}, u32[]{:S(2)}, u32[]{:S(2)}) async-start(bf16[4,96,128]{2,1,0:T(8,128)(2,1)} %get-tuple-element.37.q_ref), calls=%async_computation.1 | async-start | bytes 196608 | tf_op jit(solution)/shard_map/all_to_all | solution.py:536
  28.3 3.8 %collective-permute-start.4 = (bf16[2,2,16,512]{3,2,1,0:T(8,128)(2,1)S(1)}, bf16[2,2,16,512]{3,2,1,0:T(8,128)(2,1)S(1)}, u32[]{:S(2)}, u32[]{:S(2)}) collective-permute-start(bf16[2,2,16,512]{3,2,1,0:T(8,128)(2,1)S(1)} %shard_map.205.own_ref.refs_0_), channel_id=1, source_target_pairs={{0,32},{32,0},{64,96},{96,64},{128,160},{160,128},{192,224},{224,1... | collective-permute-start | bytes 196616 | tf_op jit(solution)/shard_map/ppermute | solution.py:541
  28.3 1.3 %collective-permute-start = (s32[1,16]{1,0:T(1,128)S(1)}, s32[1,16]{1,0:T(1,128)S(1)}, u32[]{:S(2)}, u32[]{:S(2)}) collective-permute-start(s32[1,16]{1,0:T(1,128)S(1)} %copy-done.3), channel_id=1, source_target_pairs={{0,32},{32,0},{64,96},{96,64},{128,160},{160,128},{192,224},{224,1... | collective-permute-start | bytes 200 | tf_op jit(solution)/shard_map/ppermute | solution.py:541
  29.7 1.2 %collective-permute-start.5 = (bf16[2,32,128]{2,1,0:T(8,128)(2,1)S(1)}, bf16[2,32,128]{2,1,0:T(8,128)(2,1)S(1)}, u32[]{:S(2)}, u32[]{:S(2)}) collective-permute-start(bf16[2,32,128]{2,1,0:T(8,128)(2,1)S(1)} %get-tuple-element.38.kv_ref), channel_id=1, source_target_pairs={{0,32},{32,0},{64,96},{96,64},{128,160},{160,128},{192,224},{224,1... | collective-permute-start | bytes 49160 | tf_op jit(solution)/shard_map/ppermute | solution.py:541
  46.1 12.6 %all-to-all-start.2 = ((bf16[4,40,512]{2,1,0:T(8,128)(2,1)}), bf16[4,40,512]{2,1,0:T(8,128)(2,1)S(1)}, u32[]{:S(2)}, u32[]{:S(2)}) async-start(bf16[4,40,512]{2,1,0:T(8,128)(2,1)} %shard_map.207), calls=%async_computation.2 | async-start | bytes 327680 | tf_op jit(solution)/shard_map/all_to_all | solution.py:536
  61.0 11.7 %all-to-all-start.3 = ((bf16[4,8,1536]{2,1,0:T(8,128)(2,1)}), bf16[4,8,1536]{2,1,0:T(8,128)(2,1)S(1)}, u32[]{:S(2)}, u32[]{:S(2)}) async-start(bf16[4,8,1536]{2,1,0:T(8,128)(2,1)} %shard_map.208.order_ref), calls=%async_computation.3 | async-start | bytes 196608 | tf_op jit(solution)/shard_map/all_to_all | solution.py:536
  74.6 17.8 %all-to-all-start.4 = ((bf16[32,4,1536]{2,1,0:T(4,128)(2,1)}), bf16[32,4,1536]{2,1,0:T(4,128)(2,1)S(1)}, u32[]{:S(2)}, u32[]{:S(2)}) async-start(bf16[32,4,1536]{2,1,0:T(4,128)(2,1)} %get-tuple-element.50), calls=%async_computation.4 | async-start | bytes 786432 | tf_op jit(solution)/shard_map/all_to_all | solution.py:533
  82.4 13.9 %collective-permute-start.10 = (bf16[2,2,16,512]{3,2,1,0:T(8,128)(2,1)S(1)}, bf16[2,2,16,512]{3,2,1,0:T(8,128)(2,1)S(1)}, u32[]{:S(2)}, u32[]{:S(2)}) collective-permute-start(bf16[2,2,16,512]{3,2,1,0:T(8,128)(2,1)S(1)} %shard_map.205.own_ref.refs_0_), channel_id=1, source_target_pairs={{0,128},{32,160},{64,192},{96,224},{128,0},{160,32},{192,64},{224,... | collective-permute-start | bytes 196616 | tf_op jit(solution)/shard_map/ppermute | solution.py:541
  83.0 13.3 %collective-permute-start.11 = (bf16[2,2,16,512]{3,2,1,0:T(8,128)(2,1)S(1)}, bf16[2,2,16,512]{3,2,1,0:T(8,128)(2,1)S(1)}, u32[]{:S(2)}, u32[]{:S(2)}) collective-permute-start(bf16[2,2,16,512]{3,2,1,0:T(8,128)(2,1)S(1)} %shard_map.205.own_ref.refs_0_), channel_id=1, source_target_pairs={{0,192},{32,224},{64,128},{96,160},{128,64},{160,96},{192,0},{224,... | collective-permute-start | bytes 196616 | tf_op jit(solution)/shard_map/ppermute | solution.py:541
  86.8 9.5 %collective-permute-start.9 = (bf16[2,2,16,512]{3,2,1,0:T(8,128)(2,1)S(1)}, bf16[2,2,16,512]{3,2,1,0:T(8,128)(2,1)S(1)}, u32[]{:S(2)}, u32[]{:S(2)}) collective-permute-start(bf16[2,2,16,512]{3,2,1,0:T(8,128)(2,1)S(1)} %shard_map.205.own_ref.refs_0_), channel_id=1, source_target_pairs={{0,64},{32,96},{64,0},{96,32},{128,192},{160,224},{192,128},{224,1... | collective-permute-start | bytes 196616 | tf_op jit(solution)/shard_map/ppermute | solution.py:541
  96.3 13.8 %all-to-all-start.5 = ((bf16[32,4,1536]{2,1,0:T(4,128)(2,1)}), bf16[32,4,1536]{2,1,0:T(4,128)(2,1)S(1)}, u32[]{:S(2)}, u32[]{:S(2)}) async-start(bf16[32,4,1536]{2,1,0:T(4,128)(2,1)} %shard_map.211), calls=%async_computation.5 | async-start | bytes 786432 | tf_op jit(solution)/shard_map/all_to_all | solution.py:533
  101.4 1.3 %collective-permute-start.12 = (bf16[2,2,16,512]{3,2,1,0:T(8,128)(2,1)S(1)}, bf16[2,2,16,512]{3,2,1,0:T(8,128)(2,1)S(1)}, u32[]{:S(2)}, u32[]{:S(2)}) collective-permute-start(bf16[2,2,16,512]{3,2,1,0:T(8,128)(2,1)S(1)} %collective-permute-done.9.refs_2_), channel_id=1, source_target_pairs={{0,32},{32,0},{64,96},{96,64},{128,160},{160,128},{192,224},{224,1... | collective-permute-start | bytes 196616 | tf_op jit(solution)/shard_map/ppermute | solution.py:541
  101.5 1.4 %collective-permute-start.13 = (bf16[2,2,16,512]{3,2,1,0:T(8,128)(2,1)S(1)}, bf16[2,2,16,512]{3,2,1,0:T(8,128)(2,1)S(1)}, u32[]{:S(2)}, u32[]{:S(2)}) collective-permute-start(bf16[2,2,16,512]{3,2,1,0:T(8,128)(2,1)S(1)} %collective-permute-done.10.refs_4_), channel_id=1, source_target_pairs={{0,32},{32,0},{64,96},{96,64},{128,160},{160,128},{192,224},{224,1... | collective-permute-start | bytes 196616 | tf_op jit(solution)/shard_map/ppermute | solution.py:541
  102.0 1.3 %collective-permute-start.14 = (bf16[2,2,16,512]{3,2,1,0:T(8,128)(2,1)S(1)}, bf16[2,2,16,512]{3,2,1,0:T(8,128)(2,1)S(1)}, u32[]{:S(2)}, u32[]{:S(2)}) collective-permute-start(bf16[2,2,16,512]{3,2,1,0:T(8,128)(2,1)S(1)} %collective-permute-done.11.refs_6_), channel_id=1, source_target_pairs={{0,32},{32,0},{64,96},{96,64},{128,160},{160,128},{192,224},{224,1... | collective-permute-start | bytes 196616 | tf_op jit(solution)/shard_map/ppermute | solution.py:541

commit v6 on v5

--- a/solution.py
+++ b/solution.py
@@ -233,9 +233,9 @@
     pick_ref,
     *refs,
 ):
-    sources, out_ref, held = refs[0:4], refs[4], refs[5:9]
-    score_refs, prob_refs, top_ref, sem = refs[9:11], refs[11:13], refs[13], refs[14]
-    k_ref, v_ref, other_k_ref, other_v_ref = held
+    other_k_ref, sources, out_ref, held = refs[0], refs[1:4], refs[4], refs[5:8]
+    score_refs, prob_refs, top_ref, sem = refs[8:10], refs[10:12], refs[12], refs[13]
+    k_ref, v_ref, other_v_ref = held
     rows = extra_ref.shape[0]
     half = k_ref.shape[0]
     keys = 2 * half
@@ -250,11 +250,17 @@
 
     copies = {}
     for pair in range(pairs):
-        for i in (0, 2, 1, 3):
+        for i in range(3):
             copies[pair, i] = pltpu.make_async_copy(
                 sources[i].at[:, lane_span(pair)], held[i].at[:, lane_span(pair)], sem.at[pair, i]
             )
-            copies[pair, i].start()
+
+    def needed(turn):
+        keys_of = [copies[turn, 0]] if turn < pairs else []
+        return keys_of + [copies[turn - 1, i] for i in (1, 2) if 1 <= turn <= pairs]
+
+    for copy in needed(0) + needed(1):
+        copy.start()
 
     def extra(pair, i):
         both = [r[i, :, :, lane_span(pair)].reshape(own_keys, 128) for r in (own_ref, other_own_ref)]
@@ -269,7 +275,6 @@
     def score(pair, i):
         s_ref = score_refs[pair % 2]
         if i == 0:
-            copies[pair, 0].wait()
             queries[pair] = split_heads(q_ref.at[pair], rows)
             s = dot_t(queries[pair], extra(pair, 0))
             s = s + jnp.concatenate([extra_ref[...]] * 6, axis=0)
@@ -279,8 +284,6 @@
             top = top_ref[...]
         at = i * chunk
         source, start = (k_ref, at) if at < half else (other_k_ref, at - half)
-        if at == half:
-            copies[pair, 2].wait()
         s = dot_t(queries[pair], source[start : start + chunk, lane_span(pair)])
         s = s + bias_ref[0:1, at : at + chunk]
         s_ref[:, at : at + chunk] = s
@@ -303,7 +306,6 @@
 
     def weigh(pair, part):
         p_ref = prob_refs[pair % 2]
-        copies[pair, 1 + 2 * part].wait()
         if part == 0:
             summed[pair] = dot(p_ref[:, 0:half], v_ref[:, lane_span(pair)])
             return
@@ -319,6 +321,10 @@
         out_ref[pair, rows:, :] = pick_ref[pair]
 
     for turn in range(pairs + 2):
+        for copy in needed(turn):
+            copy.wait()
+        for copy in needed(turn + 2):
+            copy.start()
         for i in range(chunks):
             if turn < pairs:
                 score(turn, i)
@@ -398,22 +404,26 @@
         out_ref[e] = buffer[e * capacity : (e + 1) * capacity, :].astype(BF16)
 
 
-def expert_kernel(x_hbm, w_in_hbm, w_out_hbm, out_ref, x_ref, w_in_ref, w_out_ref, rows_ref, sem):
-    pairs = ((x_hbm, x_ref), (w_in_hbm, w_in_ref), (w_out_hbm, w_out_ref))
-    copies = [pltpu.make_async_copy(a, b, sem.at[i]) for i, (a, b) in enumerate(pairs)]
+def expert_kernel(x_ref, w_in_hbm, w_out_ref, out_ref, w_in_ref, rows_ref, sem):
+    depth = w_in_ref.shape[1] // 3
+    spans = [slice(i * depth, (i + 1) * depth) for i in range(3)]
+    copies = [
+        pltpu.make_async_copy(w_in_hbm.at[:, span], w_in_ref.at[:, span], sem.at[i])
+        for i, span in enumerate(spans)
+    ]
     for copy in copies:
         copy.start()
     sources, capacity = x_ref.shape[0], x_ref.shape[1]
-    copies[0].wait()
     for s in range(sources):
         rows_ref[s * capacity : (s + 1) * capacity, :] = x_ref[s].astype(F32)
     x = rows_ref[...].astype(BF16)
-    copies[1].wait()
-    projected = dot(x, w_in_ref[0])
+    projected = jnp.zeros((sources * capacity, w_in_ref.shape[2]), F32)
+    for copy, span in zip(copies, spans):
+        copy.wait()
+        projected = projected + dot(x[:, span], w_in_ref[0, span, :])
     half = projected.shape[1] // 2
     g, u = projected[:, 0:half], projected[:, half:]
     act = (g * jax.nn.sigmoid(g) * u).astype(BF16)
-    copies[2].wait()
     out = dot(act, w_out_ref[0])
     for s in range(sources):
         out_ref[s] = out[s * capacity : (s + 1) * capacity, :].astype(BF16)
@@ -598,22 +608,22 @@
     )
 
     resident = pl.BlockSpec(memory_space=pltpu.VMEM)
-    operands = (bias, extra, q_all, own, other_own, pick)
+    operands = (bias, extra, q_all, own, other_own, pick, other_prompt[0])
     partial_shape = shaped((n_chips, rows + local_rows, 512))
     partial = pl.pallas_call(
         attend_kernel,
         grid=(1,),
         out_shape=partial_shape,
-        in_specs=[resident] * len(operands) + [anywhere] * 4,
+        in_specs=[resident] * len(operands) + [anywhere] * 3,
         out_specs=block(partial_shape.shape),
-        scratch_shapes=[pltpu.VMEM((keys, kv_width), BF16)] * 4
+        scratch_shapes=[pltpu.VMEM((keys, kv_width), BF16)] * 3
         + [
             pltpu.VMEM((6 * rows, 2 * keys + 128), F32),
             pltpu.VMEM((6 * rows, 2 * keys + 128), F32),
             pltpu.VMEM((6 * rows, 2 * keys + 128), BF16),
             pltpu.VMEM((6 * rows, 2 * keys + 128), BF16),
             pltpu.VMEM((6 * rows, 128), F32),
-            pltpu.SemaphoreType.DMA((kv_width // 128, 4)),
+            pltpu.SemaphoreType.DMA((kv_width // 128, 3)),
         ],
         compiler_params=params(32),
         cost_estimate=pl.CostEstimate(
@@ -621,7 +631,7 @@
             bytes_accessed=8 * keys * kv_width,
             transcendentals=24 * rows * 2 * keys,
         ),
-    )(*operands, *map(stay, prompt), *other_prompt)
+    )(*operands, *map(stay, prompt), other_prompt[1])
     parts = exchange_chips(partial)
     sums = call(
         join_kernel,
@@ -659,12 +669,10 @@
         shaped(buffer.shape),
         buffer,
         stay(w_in),
-        stay(w_out),
-        ins=[anywhere] * 3,
+        w_out,
+        ins=[resident, anywhere, resident],
         scratch=[
-            pltpu.VMEM(buffer.shape, BF16),
             pltpu.VMEM(w_in.shape, BF16),
-            pltpu.VMEM(w_out.shape, BF16),
             pltpu.VMEM((slots, width), F32),
             pltpu.SemaphoreType.DMA((3,)),
         ],

time: 112 us -> 110 us (0.982)
  Pallas kernels: 28.5 us -> 25.9 us
    pallas_call x1, Pallas kernels: 10.1 us -> 8.06 us  [local(): pl.pallas_call(attend_kernel, grid=(1,), out_shape=partial_shape, in_spec...]
  transfers between devices with their start and end apart: 21 -> 21, of which waited for: 11 -> 11; matrix products, arithmetic and copies ran while one was open for 0% -> 0% of each run, Pallas kernels for 20% -> 18%
where the time goes in v6:
time: 110 us; the launch traced here: 108 us
  starting transfers between devices  40.5 us (37%)
  waiting for transfers between devices  39.6 us (36%)
  Pallas kernels  25.9 us (24%)
  local copies, waits for them, and re-layouts  1.63 us (1%)
    all_to_all x4, waiting for transfers between devices, exchange_chips(): lax.all_to_all(a, 'seq', split_axis=0, concat_axis=0, tiled=True, axis_in...  28.5 us
    all_to_all x4, starting transfers between devices, exchange_chips(): lax.all_to_all(a, 'seq', split_axis=0, concat_axis=0, tiled=True, axis_in...  18.6 us
    pallas_call x11, Pallas kernels, call(): pl.pallas_call(kernel, grid=(1,), out_shape=outs, in_specs=specs, out_spe...  17.9 us
    all_to_all x2, starting transfers between devices, exchange(): return lax.all_to_all(a, axis, split_axis=0, concat_axis=0, tiled=True)  12.6 us
    ppermute x15, starting transfers between devices, apart(): return lax.ppermute(a, 'seq', [(i, i ^ distance) for i in range(n_seq)])  9.33 us
    all_to_all x2, waiting for transfers between devices, exchange(): return lax.all_to_all(a, axis, split_axis=0, concat_axis=0, tiled=True)  8.99 us
    pallas_call x1, Pallas kernels, local(): pl.pallas_call(attend_kernel, grid=(1,), out_shape=partial_shape, in_spec...  8.06 us
  transfers between devices with their start and end apart: 21, of which 11 were waited for; matrix products, arithmetic and copies ran while one was open for 0% of the time, Pallas kernels for 18%

profile of v6, /device:TPU:8, one launch (start us, length us, event | category | flops | bytes accessed | tf_op | source)
XLA Modules:
  0.0 108.5 jit_solution(4964102144587119674)
XLA Ops:
  0.7 1.5 %shard_map.202.order_ref = bf16[4,8,1536]{2,1,0:T(8,128)(2,1)} custom-call(bf16[2,4,1536]{2,1,0:T(4,128)(2,1)} %bitcast.31, f32[1536]{0:T(1024)} %gain_ref.2), custom_call_target="tpu_custom_call" | custom-call | flops 1048576 | bytes 1048576 | tf_op jit(solution)/shard_map/pallas_call | solution.py:488
  2.2 0.5 collective-permute-start.7
  3.2 8.5 %all-to-all-start = ((bf16[4,8,1536]{2,1,0:T(8,128)(2,1)}), bf16[4,8,1536]{2,1,0:T(8,128)(2,1)S(1)}, u32[]{:S(2)}, u32[]{:S(2)}) async-start(bf16[4,8,1536]{2,1,0:T(8,128)(2,1)} %shard_map.202.order_ref), calls=%async_computation | async-start | bytes 196608 | tf_op jit(solution)/shard_map/all_to_all | solution.py:546
  11.6 0.7 copy-done.1
  12.6 8.0 %all-to-all-done.x_ref = bf16[4,8,1536]{2,1,0:T(8,128)(2,1)S(1)} async-done(((bf16[4,8,1536]{2,1,0:T(8,128)(2,1)}), bf16[4,8,1536]{2,1,0:T(8,128)(2,1)S(1)}, u32[]{:S(2)}, u32[]{:S(2)}) %all-to-all-start) | async-done | bytes 98336 | tf_op jit(solution)/shard_map/all_to_all | solution.py:546
  20.6 0.9 copy-done.2
  21.5 2.7 %shard_map.204 = (bf16[4,96,128]{2,1,0:T(8,128)(2,1)}, bf16[2,32,128]{2,1,0:T(8,128)(2,1)S(1)}) custom-call(bf16[4,8,1536]{2,1,0:T(8,128)(2,1)S(1)} %all-to-all-done.x_ref, s32[1]{0:T(128)} %bitcast.6.seq_ref, bf16[192,1536]{1,0:T(8,128)(2,1)} %bitcast.26, bf16[64,1536]{1,0:T(8,128)(2,1)} %bitcast.28, bf16[64,1536]{1,0:T(8,128)(2,1)} %bitcast.30, ...), custom_call_target="tpu_custom_call" | custom-call | flops 1048576 | bytes 1048576 | tf_op jit(solution)/shard_map/pallas_call | solution.py:488
  24.2 3.3 %all-to-all-start.1 = ((bf16[4,96,128]{2,1,0:T(8,128)(2,1)}), bf16[4,96,128]{2,1,0:T(8,128)(2,1)S(1)}, u32[]{:S(2)}, u32[]{:S(2)}) async-start(bf16[4,96,128]{2,1,0:T(8,128)(2,1)} %get-tuple-element.37.q_ref), calls=%async_computation.1 | async-start | bytes 196608 | tf_op jit(solution)/shard_map/all_to_all | solution.py:546
  27.5 0.8 shard_map.205.own_ref.refs_0_
  28.8 0.8 collective-permute-done.other_len_ref
  30.0 0.8 shard_map.203
  30.8 1.3 %shard_map.206 = (bf16[32,512]{1,0:T(8,128)(2,1)S(1)}, bf16[4,8,512]{2,1,0:T(8,128)(2,1)S(1)}) custom-call(bf16[4,96,128]{2,1,0:T(8,128)(2,1)} %get-tuple-element.37.q_ref, bf16[2,32,128]{2,1,0:T(8,128)(2,1)S(1)} %get-tuple-element.38.kv_ref, bf16[2,32,128]{2,1,0:T(8,128)(2,1)S(1)} %collective-permute-done.5.other_ref, ...), custom_call_target="tpu_custom_call" | custom-call | flops 1048576 | bytes 1048576 | tf_op jit(solution)/shard_map/pallas_call | solution.py:488
  32.1 3.9 %all-to-all-done.1.q_ref = bf16[4,96,128]{2,1,0:T(8,128)(2,1)S(1)} async-done(((bf16[4,96,128]{2,1,0:T(8,128)(2,1)}), bf16[4,96,128]{2,1,0:T(8,128)(2,1)S(1)}, u32[]{:S(2)}, u32[]{:S(2)}) %all-to-all-start.1) | async-done | bytes 98336 | tf_op jit(solution)/shard_map/all_to_all | solution.py:546
  36.0 8.1 %shard_map.207 = bf16[4,40,512]{2,1,0:T(8,128)(2,1)} custom-call(f32[8,4096]{1,0:T(8,128)S(1)} %get-tuple-element.32.bias_ref, f32[32,128]{1,0:T(8,128)S(1)} %get-tuple-element.33.extra_ref, bf16[4,96,128]{2,1,0:T(8,128)(2,1)S(1)} %all-to-all-done.1.q_ref, bf16[2,2,16,512]{3,2,1,0:T(8,128)(2,1)S(1)} %shard_map.205.own_ref.refs_0_, ...), custom_call_target="tpu_custom_call" | custom-call | flops 805306368 | bytes 8388608 | tf_op jit(solution)/shard_map/pallas_call | solution.py:613
  44.1 3.5 %all-to-all-start.2 = ((bf16[4,40,512]{2,1,0:T(8,128)(2,1)}), bf16[4,40,512]{2,1,0:T(8,128)(2,1)S(1)}, u32[]{:S(2)}, u32[]{:S(2)}) async-start(bf16[4,40,512]{2,1,0:T(8,128)(2,1)} %shard_map.207), calls=%async_computation.2 | async-start | bytes 327680 | tf_op jit(solution)/shard_map/all_to_all | solution.py:546
  47.6 9.2 %all-to-all-done.2.part_ref = bf16[4,40,512]{2,1,0:T(8,128)(2,1)S(1)} async-done(((bf16[4,40,512]{2,1,0:T(8,128)(2,1)}), bf16[4,40,512]{2,1,0:T(8,128)(2,1)S(1)}, u32[]{:S(2)}, u32[]{:S(2)}) %all-to-all-start.2) | async-done | bytes 163872 | tf_op jit(solution)/shard_map/all_to_all | solution.py:546
  56.8 2.3 %shard_map.208.order_ref = bf16[4,8,1536]{2,1,0:T(8,128)(2,1)} custom-call(bf16[4,40,512]{2,1,0:T(8,128)(2,1)S(1)} %all-to-all-done.2.part_ref, bf16[32,512]{1,0:T(8,128)(2,1)S(1)} %get-tuple-element.44.fresh_ref, s32[1]{0:T(128)} %bitcast.6.seq_ref, bf16[192,1536]{1,0:T(8,128)(2,1)} %w_ref.1, bf16[192,1536]{1,0:T(8,128)(2,1)S(1)} %collective-permute-done.8.other_w_ref), custom_call_target="tpu_custom_call" | custom-call | flops 1048576 | bytes 1048576 | tf_op jit(solution)/shard_map/pallas_call | solution.py:488
  59.1 3.3 %all-to-all-start.3 = ((bf16[4,8,1536]{2,1,0:T(8,128)(2,1)}), bf16[4,8,1536]{2,1,0:T(8,128)(2,1)S(1)}, u32[]{:S(2)}, u32[]{:S(2)}) async-start(bf16[4,8,1536]{2,1,0:T(8,128)(2,1)} %shard_map.208.order_ref), calls=%async_computation.3 | async-start | bytes 196608 | tf_op jit(solution)/shard_map/all_to_all | solution.py:546
  62.5 1.0 shard_map.209
  63.5 7.4 %all-to-all-done.3.sums_ref = bf16[4,8,1536]{2,1,0:T(8,128)(2,1)S(1)} async-done(((bf16[4,8,1536]{2,1,0:T(8,128)(2,1)}), bf16[4,8,1536]{2,1,0:T(8,128)(2,1)S(1)}, u32[]{:S(2)}, u32[]{:S(2)}) %all-to-all-start.3) | async-done | bytes 98336 | tf_op jit(solution)/shard_map/all_to_all | solution.py:546
  70.9 1.8 %shard_map.210 = (f32[8,1536]{1,0:T(8,128)S(1)}, bf16[32,4,1536]{2,1,0:T(4,128)(2,1)}) custom-call(bf16[2,4,1536]{2,1,0:T(4,128)(2,1)} %bitcast.32, bf16[4,8,1536]{2,1,0:T(8,128)(2,1)S(1)} %all-to-all-done.3.sums_ref, f32[1536]{0:T(1024)} %gain_ref.3, bf16[128,8]{1,0:T(8,128)(2,1)S(1)} %get-tuple-element.46.place_ref), custom_call_target="tpu_custom_call" | custom-call | flops 1048576 | bytes 1048576 | tf_op jit(solution)/shard_map/pallas_call | solution.py:488
  72.7 7.7 %all-to-all-start.4 = ((bf16[32,4,1536]{2,1,0:T(4,128)(2,1)}), bf16[32,4,1536]{2,1,0:T(4,128)(2,1)S(1)}, u32[]{:S(2)}, u32[]{:S(2)}) async-start(bf16[32,4,1536]{2,1,0:T(4,128)(2,1)} %get-tuple-element.50), calls=%async_computation.4 | async-start | bytes 786432 | tf_op jit(solution)/shard_map/all_to_all | solution.py:543
  80.5 1.0 collective-permute-start.10
  81.5 3.5 %collective-permute-start.11 = (bf16[2,2,16,512]{3,2,1,0:T(8,128)(2,1)S(1)}, bf16[2,2,16,512]{3,2,1,0:T(8,128)(2,1)S(1)}, u32[]{:S(2)}, u32[]{:S(2)}) collective-permute-start(bf16[2,2,16,512]{3,2,1,0:T(8,128)(2,1)S(1)} %shard_map.205.own_ref.refs_0_), channel_id=1, source_target_pairs={{0,192},{32,224},{64,128},{96,160},{128,64},{160,96},{192,0},{224,... | collective-permute-start | bytes 196616 | tf_op jit(solution)/shard_map/ppermute | solution.py:551
  84.9 2.1 %collective-permute-start.9 = (bf16[2,2,16,512]{3,2,1,0:T(8,128)(2,1)S(1)}, bf16[2,2,16,512]{3,2,1,0:T(8,128)(2,1)S(1)}, u32[]{:S(2)}, u32[]{:S(2)}) collective-permute-start(bf16[2,2,16,512]{3,2,1,0:T(8,128)(2,1)S(1)} %shard_map.205.own_ref.refs_0_), channel_id=1, source_target_pairs={{0,64},{32,96},{64,0},{96,32},{128,192},{160,224},{192,128},{224,1... | collective-permute-start | bytes 196616 | tf_op jit(solution)/shard_map/ppermute | solution.py:551
  87.1 3.5 %all-to-all-done.4.x_ref = bf16[32,4,1536]{2,1,0:T(4,128)(2,1)S(1)} async-done(((bf16[32,4,1536]{2,1,0:T(4,128)(2,1)}), bf16[32,4,1536]{2,1,0:T(4,128)(2,1)S(1)}, u32[]{:S(2)}, u32[]{:S(2)}) %all-to-all-start.4) | async-done | bytes 393248 | tf_op jit(solution)/shard_map/all_to_all | solution.py:543
  90.6 3.3 %shard_map.211 = bf16[32,4,1536]{2,1,0:T(4,128)(2,1)} custom-call(bf16[32,4,1536]{2,1,0:T(4,128)(2,1)S(1)} %all-to-all-done.4.x_ref, bf16[1,1536,1024]{2,1,0:T(8,128)(2,1)} %w_in_hbm.1, bf16[1,512,1536]{2,1,0:T(8,128)(2,1)S(1)} %copy-done), custom_call_target="tpu_custom_call" | custom-call | flops 1048576 | bytes 1048576 | tf_op jit(solution)/shard_map/pallas_call | solution.py:488
  93.9 4.9 %all-to-all-start.5 = ((bf16[32,4,1536]{2,1,0:T(4,128)(2,1)}), bf16[32,4,1536]{2,1,0:T(4,128)(2,1)S(1)}, u32[]{:S(2)}, u32[]{:S(2)}) async-start(bf16[32,4,1536]{2,1,0:T(4,128)(2,1)} %shard_map.211), calls=%async_computation.5 | async-start | bytes 786432 | tf_op jit(solution)/shard_map/all_to_all | solution.py:543
  99.4 0.6 collective-permute-done.12.refs_3_
  100.6 1.4 %shard_map.213 = (bf16[20,2,512]{2,1,0:T(2,128)(2,1)}, bf16[20,2,512]{2,1,0:T(2,128)(2,1)}) custom-call(s32[1]{0:T(128)} %bitcast.6.seq_ref, s32[4,16]{1,0:T(4,128)S(1)} %bitcast.20, bf16[4,40,512]{2,1,0:T(8,128)(2,1)S(1)} %all-to-all-done.2.part_ref, bf16[2,2,16,512]{3,2,1,0:T(8,128)(2,1)S(1)} %shard_map.205.own_ref.refs_0_, ...), custom_call_target="tpu_custom_call" | custom-call | flops 1048576 | bytes 1048576 | tf_op jit(solution)/shard_map/pallas_call | solution.py:488
  102.0 5.5 %all-to-all-done.5.back_ref = bf16[32,4,1536]{2,1,0:T(4,128)(2,1)S(1)} async-done(((bf16[32,4,1536]{2,1,0:T(4,128)(2,1)}), bf16[32,4,1536]{2,1,0:T(4,128)(2,1)S(1)}, u32[]{:S(2)}, u32[]{:S(2)}) %all-to-all-start.5) | async-done | bytes 393248 | tf_op jit(solution)/shard_map/all_to_all | solution.py:543
  107.5 1.0 shard_map.212
  (32 shorter events, 2.9 us)
Async XLA Ops:
  0.6 27.7 %copy-start.4 = (s32[1,16]{1,0:T(1,128)S(1)}, s32[1,16]{1,0:T(1,128)}, u32[]{:S(2)}) copy-start(s32[1,16]{1,0:T(1,128)} %len_ref.1) | copy-start | bytes 196
  0.6 29.3 %copy-start.3 = (s32[1,4,16]{2,1,0:T(4,128)S(1)}, s32[1,4,16]{2,1,0:T(4,128)}, u32[]{:S(2)}) copy-start(s32[1,4,16]{2,1,0:T(4,128)} %param.20) | copy-start | bytes 772
  2.1 33.8 %collective-permute-start.6 = (bf16[2048,512]{1,0:T(8,128)(2,1)}, bf16[2048,512]{1,0:T(8,128)(2,1)S(1)}, u32[]{:S(2)}, u32[]{:S(2)}) collective-permute-start(bf16[2048,512]{1,0:T(8,128)(2,1)} %bitcast.21), channel_id=1, source_target_pairs={{0,32},{32,0},{64,96},{96,64},{128,160},{160,128},{192,224},{224,1... | collective-permute-start | bytes 6291464 | tf_op jit(solution)/shard_map/ppermute | solution.py:551
  2.2 33.8 %collective-permute-start.7 = (bf16[2048,512]{1,0:T(8,128)(2,1)}, bf16[2048,512]{1,0:T(8,128)(2,1)}, u32[]{:S(2)}, u32[]{:S(2)}) collective-permute-start(bf16[2048,512]{1,0:T(8,128)(2,1)} %bitcast.23), channel_id=1, source_target_pairs={{0,32},{32,0},{64,96},{96,64},{128,160},{160,128},{192,224},{224,1... | collective-permute-start | bytes 6291464 | tf_op jit(solution)/shard_map/ppermute | solution.py:551
  2.7 17.9 %collective-permute-start.1 = (bf16[192,1536]{1,0:T(8,128)(2,1)}, bf16[192,1536]{1,0:T(8,128)(2,1)S(1)}, u32[]{:S(2)}, u32[]{:S(2)}) collective-permute-start(bf16[192,1536]{1,0:T(8,128)(2,1)} %bitcast.25), channel_id=1, source_target_pairs={{0,32},{32,0},{64,96},{96,64},{128,160},{160,128},{192,224},{224,1... | collective-permute-start | bytes 1769480 | tf_op jit(solution)/shard_map/ppermute | solution.py:551
  2.7 9.0 %collective-permute-start.2 = (bf16[64,1536]{1,0:T(8,128)(2,1)}, bf16[64,1536]{1,0:T(8,128)(2,1)S(1)}, u32[]{:S(2)}, u32[]{:S(2)}) collective-permute-start(bf16[64,1536]{1,0:T(8,128)(2,1)} %bitcast.27), channel_id=1, source_target_pairs={{0,32},{32,0},{64,96},{96,64},{128,160},{160,128},{192,224},{224,1... | collective-permute-start | bytes 589832 | tf_op jit(solution)/shard_map/ppermute | solution.py:551
  3.2 17.4 %collective-permute-start.3 = (bf16[64,1536]{1,0:T(8,128)(2,1)}, bf16[64,1536]{1,0:T(8,128)(2,1)}, u32[]{:S(2)}, u32[]{:S(2)}) collective-permute-start(bf16[64,1536]{1,0:T(8,128)(2,1)} %bitcast.29), channel_id=1, source_target_pairs={{0,32},{32,0},{64,96},{96,64},{128,160},{160,128},{192,224},{224,1... | collective-permute-start | bytes 589832 | tf_op jit(solution)/shard_map/ppermute | solution.py:551
  3.2 17.4 %all-to-all-start = ((bf16[4,8,1536]{2,1,0:T(8,128)(2,1)}), bf16[4,8,1536]{2,1,0:T(8,128)(2,1)S(1)}, u32[]{:S(2)}, u32[]{:S(2)}) async-start(bf16[4,8,1536]{2,1,0:T(8,128)(2,1)} %shard_map.202.order_ref), calls=%async_computation | async-start | bytes 196608 | tf_op jit(solution)/shard_map/all_to_all | solution.py:546
  11.6 0.7 copy-start.1
  12.3 35.2 %collective-permute-start.8 = (bf16[192,1536]{1,0:T(8,128)(2,1)}, bf16[192,1536]{1,0:T(8,128)(2,1)S(1)}, u32[]{:S(2)}, u32[]{:S(2)}) collective-permute-start(bf16[192,1536]{1,0:T(8,128)(2,1)} %w_ref.1), channel_id=1, source_target_pairs={{0,32},{32,0},{64,96},{96,64},{128,160},{160,128},{192,224},{224,1... | collective-permute-start | bytes 1769480 | tf_op jit(solution)/shard_map/ppermute | solution.py:551
  20.6 0.9 copy-start.2
  24.2 11.7 %all-to-all-start.1 = ((bf16[4,96,128]{2,1,0:T(8,128)(2,1)}), bf16[4,96,128]{2,1,0:T(8,128)(2,1)S(1)}, u32[]{:S(2)}, u32[]{:S(2)}) async-start(bf16[4,96,128]{2,1,0:T(8,128)(2,1)} %get-tuple-element.37.q_ref), calls=%async_computation.1 | async-start | bytes 196608 | tf_op jit(solution)/shard_map/all_to_all | solution.py:546
  28.3 3.8 %collective-permute-start.4 = (bf16[2,2,16,512]{3,2,1,0:T(8,128)(2,1)S(1)}, bf16[2,2,16,512]{3,2,1,0:T(8,128)(2,1)S(1)}, u32[]{:S(2)}, u32[]{:S(2)}) collective-permute-start(bf16[2,2,16,512]{3,2,1,0:T(8,128)(2,1)S(1)} %shard_map.205.own_ref.refs_0_), channel_id=1, source_target_pairs={{0,32},{32,0},{64,96},{96,64},{128,160},{160,128},{192,224},{224,1... | collective-permute-start | bytes 196616 | tf_op jit(solution)/shard_map/ppermute | solution.py:551
  28.3 1.3 %collective-permute-start = (s32[1,16]{1,0:T(1,128)S(1)}, s32[1,16]{1,0:T(1,128)S(1)}, u32[]{:S(2)}, u32[]{:S(2)}) collective-permute-start(s32[1,16]{1,0:T(1,128)S(1)} %copy-done.4), channel_id=1, source_target_pairs={{0,32},{32,0},{64,96},{96,64},{128,160},{160,128},{192,224},{224,1... | collective-permute-start | bytes 200 | tf_op jit(solution)/shard_map/ppermute | solution.py:551
  29.6 1.2 %collective-permute-start.5 = (bf16[2,32,128]{2,1,0:T(8,128)(2,1)S(1)}, bf16[2,32,128]{2,1,0:T(8,128)(2,1)S(1)}, u32[]{:S(2)}, u32[]{:S(2)}) collective-permute-start(bf16[2,32,128]{2,1,0:T(8,128)(2,1)S(1)} %get-tuple-element.38.kv_ref), channel_id=1, source_target_pairs={{0,32},{32,0},{64,96},{96,64},{128,160},{160,128},{192,224},{224,1... | collective-permute-start | bytes 49160 | tf_op jit(solution)/shard_map/ppermute | solution.py:551
  44.0 46.5 %copy-start = (bf16[1,512,1536]{2,1,0:T(8,128)(2,1)S(1)}, bf16[1,512,1536]{2,1,0:T(8,128)(2,1)}, u32[]{:S(2)}) copy-start(bf16[1,512,1536]{2,1,0:T(8,128)(2,1)} %w_out_ref.1) | copy-start | bytes 4718596
  44.1 12.8 %all-to-all-start.2 = ((bf16[4,40,512]{2,1,0:T(8,128)(2,1)}), bf16[4,40,512]{2,1,0:T(8,128)(2,1)S(1)}, u32[]{:S(2)}, u32[]{:S(2)}) async-start(bf16[4,40,512]{2,1,0:T(8,128)(2,1)} %shard_map.207), calls=%async_computation.2 | async-start | bytes 327680 | tf_op jit(solution)/shard_map/all_to_all | solution.py:546
  59.1 11.7 %all-to-all-start.3 = ((bf16[4,8,1536]{2,1,0:T(8,128)(2,1)}), bf16[4,8,1536]{2,1,0:T(8,128)(2,1)S(1)}, u32[]{:S(2)}, u32[]{:S(2)}) async-start(bf16[4,8,1536]{2,1,0:T(8,128)(2,1)} %shard_map.208.order_ref), calls=%async_computation.3 | async-start | bytes 196608 | tf_op jit(solution)/shard_map/all_to_all | solution.py:546
  72.7 17.8 %all-to-all-start.4 = ((bf16[32,4,1536]{2,1,0:T(4,128)(2,1)}), bf16[32,4,1536]{2,1,0:T(4,128)(2,1)S(1)}, u32[]{:S(2)}, u32[]{:S(2)}) async-start(bf16[32,4,1536]{2,1,0:T(4,128)(2,1)} %get-tuple-element.50), calls=%async_computation.4 | async-start | bytes 786432 | tf_op jit(solution)/shard_map/all_to_all | solution.py:543
  80.5 13.4 %collective-permute-start.10 = (bf16[2,2,16,512]{3,2,1,0:T(8,128)(2,1)S(1)}, bf16[2,2,16,512]{3,2,1,0:T(8,128)(2,1)S(1)}, u32[]{:S(2)}, u32[]{:S(2)}) collective-permute-start(bf16[2,2,16,512]{3,2,1,0:T(8,128)(2,1)S(1)} %shard_map.205.own_ref.refs_0_), channel_id=1, source_target_pairs={{0,128},{32,160},{64,192},{96,224},{128,0},{160,32},{192,64},{224,... | collective-permute-start | bytes 196616 | tf_op jit(solution)/shard_map/ppermute | solution.py:551
  81.5 12.4 %collective-permute-start.11 = (bf16[2,2,16,512]{3,2,1,0:T(8,128)(2,1)S(1)}, bf16[2,2,16,512]{3,2,1,0:T(8,128)(2,1)S(1)}, u32[]{:S(2)}, u32[]{:S(2)}) collective-permute-start(bf16[2,2,16,512]{3,2,1,0:T(8,128)(2,1)S(1)} %shard_map.205.own_ref.refs_0_), channel_id=1, source_target_pairs={{0,192},{32,224},{64,128},{96,160},{128,64},{160,96},{192,0},{224,... | collective-permute-start | bytes 196616 | tf_op jit(solution)/shard_map/ppermute | solution.py:551
  84.9 8.9 %collective-permute-start.9 = (bf16[2,2,16,512]{3,2,1,0:T(8,128)(2,1)S(1)}, bf16[2,2,16,512]{3,2,1,0:T(8,128)(2,1)S(1)}, u32[]{:S(2)}, u32[]{:S(2)}) collective-permute-start(bf16[2,2,16,512]{3,2,1,0:T(8,128)(2,1)S(1)} %shard_map.205.own_ref.refs_0_), channel_id=1, source_target_pairs={{0,64},{32,96},{64,0},{96,32},{128,192},{160,224},{192,128},{224,1... | collective-permute-start | bytes 196616 | tf_op jit(solution)/shard_map/ppermute | solution.py:551
  93.9 13.6 %all-to-all-start.5 = ((bf16[32,4,1536]{2,1,0:T(4,128)(2,1)}), bf16[32,4,1536]{2,1,0:T(4,128)(2,1)S(1)}, u32[]{:S(2)}, u32[]{:S(2)}) async-start(bf16[32,4,1536]{2,1,0:T(4,128)(2,1)} %shard_map.211), calls=%async_computation.5 | async-start | bytes 786432 | tf_op jit(solution)/shard_map/all_to_all | solution.py:543
  98.7 1.3 %collective-permute-start.12 = (bf16[2,2,16,512]{3,2,1,0:T(8,128)(2,1)S(1)}, bf16[2,2,16,512]{3,2,1,0:T(8,128)(2,1)S(1)}, u32[]{:S(2)}, u32[]{:S(2)}) collective-permute-start(bf16[2,2,16,512]{3,2,1,0:T(8,128)(2,1)S(1)} %collective-permute-done.9.refs_2_), channel_id=1, source_target_pairs={{0,32},{32,0},{64,96},{96,64},{128,160},{160,128},{192,224},{224,1... | collective-permute-start | bytes 196616 | tf_op jit(solution)/shard_map/ppermute | solution.py:551
  98.8 1.4 %collective-permute-start.13 = (bf16[2,2,16,512]{3,2,1,0:T(8,128)(2,1)S(1)}, bf16[2,2,16,512]{3,2,1,0:T(8,128)(2,1)S(1)}, u32[]{:S(2)}, u32[]{:S(2)}) collective-permute-start(bf16[2,2,16,512]{3,2,1,0:T(8,128)(2,1)S(1)} %collective-permute-done.10.refs_4_), channel_id=1, source_target_pairs={{0,32},{32,0},{64,96},{96,64},{128,160},{160,128},{192,224},{224,1... | collective-permute-start | bytes 196616 | tf_op jit(solution)/shard_map/ppermute | solution.py:551
  99.3 1.3 %collective-permute-start.14 = (bf16[2,2,16,512]{3,2,1,0:T(8,128)(2,1)S(1)}, bf16[2,2,16,512]{3,2,1,0:T(8,128)(2,1)S(1)}, u32[]{:S(2)}, u32[]{:S(2)}) collective-permute-start(bf16[2,2,16,512]{3,2,1,0:T(8,128)(2,1)S(1)} %collective-permute-done.11.refs_6_), channel_id=1, source_target_pairs={{0,32},{32,0},{64,96},{96,64},{128,160},{160,128},{192,224},{224,1... | collective-permute-start | bytes 196616 | tf_op jit(solution)/shard_map/ppermute | solution.py:551

commit v7 on v6

--- a/solution.py
+++ b/solution.py
@@ -336,7 +336,13 @@
             tops[turn] = jnp.max(top_ref[...], axis=-1, keepdims=True)
 
 
-def join_kernel(part_ref, fresh_ref, seq_ref, w_ref, other_w_ref, out_ref):
+def join_kernel(part_ref, fresh_ref, seq_ref, w_hbm, other_w_hbm, out_ref, w_ref, other_w_ref, sem):
+    copies = [
+        pltpu.make_async_copy(w_hbm, w_ref, sem.at[0]),
+        pltpu.make_async_copy(other_w_hbm, other_w_ref, sem.at[1]),
+    ]
+    for copy in copies:
+        copy.start()
     sources, rows = part_ref.shape[0], fresh_ref.shape[0]
     core = seq_ref[0] % 2
     low = lanes((rows, 128)) < HEAD
@@ -351,14 +357,18 @@
     top = functools.reduce(jnp.maximum, lse)
     weight = [jnp.exp(x - top) for x in lse]
     inverse = 1.0 / functools.reduce(jnp.add, weight)
-    out = jnp.zeros((rows, w_ref.shape[1]), F32)
+    heads = []
     for j in range(3):
         total = jnp.zeros((rows, 128), F32)
         for s in range(sources + 1):
             w = weight[s] * inverse
             even, odd = w[:, 3 * j : 3 * j + 1], w[:, 9 + 3 * j : 10 + 3 * j]
             total = total + tile(s, j) * jnp.where(low, even, odd)
-        total = jnp.where(core == 0, total, swap(total)).astype(BF16)
+        heads.append(jnp.where(core == 0, total, swap(total)).astype(BF16))
+    for copy in copies:
+        copy.wait()
+    out = jnp.zeros((rows, w_ref.shape[1]), F32)
+    for j, total in enumerate(heads):
         span = slice(j * HEAD, (j + 1) * HEAD)
         out = out + dot(total, jnp.concatenate([w_ref[span, :], other_w_ref[span, :]], axis=0))
     out = out.astype(BF16)
@@ -389,11 +399,19 @@
     place_ref[...] = jnp.where(placed, 1.0, 0.0).T.astype(BF16)
 
 
-def dispatch_kernel(x_ref, sums_ref, gain_ref, place_ref, hidden_ref, out_ref):
+def dispatch_kernel(x_hbm, sums_ref, gain_hbm, place_ref, hidden_ref, out_ref, x_ref, gain_ref, sem):
+    copies = [
+        pltpu.make_async_copy(x_hbm, x_ref, sem.at[0]),
+        pltpu.make_async_copy(gain_hbm, gain_ref, sem.at[1]),
+    ]
+    for copy in copies:
+        copy.start()
     beams = x_ref.shape[0]
     total = sums_ref[0].astype(F32)
     for s in range(1, sums_ref.shape[0]):
         total = total + sums_ref[s].astype(F32)
+    for copy in copies:
+        copy.wait()
     inputs = jnp.concatenate([x_ref[b].astype(F32) for b in range(beams)], axis=0)
     hidden = inputs + total
     hidden_ref[...] = hidden
@@ -591,7 +609,8 @@
         normed_all,
         seq,
         *[stay(w) for w in weights],
-        *other_weights,
+        other_weights[0],
+        *map(stay, other_weights[1:]),
         stay(cosine),
         stay(sine),
         ins=[block(normed_all.shape), scalars()],
@@ -641,7 +660,8 @@
         seq,
         stay(w_output),
         other_w_output,
-        ins=[block(parts.shape), block(fresh.shape), scalars()],
+        ins=[resident, resident, scalars(), anywhere, anywhere],
+        scratch=[pltpu.VMEM(w_output.shape, BF16)] * 2 + [pltpu.SemaphoreType.DMA((2,))],
     )
     slots = n_req * capacity
     place, mix = call(
@@ -660,6 +680,12 @@
         sums,
         stay(gain_moe),
         place,
+        ins=[anywhere, resident, anywhere, resident],
+        scratch=[
+            pltpu.VMEM(x.shape, BF16),
+            pltpu.VMEM((width,), F32),
+            pltpu.SemaphoreType.DMA((2,)),
+        ],
     )
     own, buffer = lax.optimization_barrier((own, buffer))
     even = [own] + [apart(own, k) for k in range(2, n_seq, 2)]
@@ -687,6 +713,7 @@
         hidden,
         mix,
         back,
+        ins=[resident] * 3,
         scratch=[pltpu.VMEM((slots, width), F32)],
     )
     final_k, final_v = call(

time: 110 us -> 108 us (0.982)
  local copies, waits for them, and re-layouts: 1.63 us -> 0.01 us
    unnamed x10 -> x6, local copies, waits for them, and re-layouts: 1.63 us -> 0.01 us
where the time goes in v7:
time: 108 us; the launch traced here: 107 us
  starting transfers between devices  40.5 us (38%)
  waiting for transfers between devices  40.4 us (37%)
  Pallas kernels  25.6 us (24%)
    all_to_all x4, waiting for transfers between devices, exchange_chips(): lax.all_to_all(a, 'seq', split_axis=0, concat_axis=0, tiled=True, axis_in...  29.2 us
    all_to_all x4, starting transfers between devices, exchange_chips(): lax.all_to_all(a, 'seq', split_axis=0, concat_axis=0, tiled=True, axis_in...  18.6 us
    pallas_call x11, Pallas kernels, call(): pl.pallas_call(kernel, grid=(1,), out_shape=outs, in_specs=specs, out_spe...  17.6 us
    all_to_all x2, starting transfers between devices, exchange(): return lax.all_to_all(a, axis, split_axis=0, concat_axis=0, tiled=True)  12.6 us
    ppermute x15, starting transfers between devices, apart(): return lax.ppermute(a, 'seq', [(i, i ^ distance) for i in range(n_seq)])  9.33 us
    all_to_all x2, waiting for transfers between devices, exchange(): return lax.all_to_all(a, axis, split_axis=0, concat_axis=0, tiled=True)  9.03 us
    pallas_call x1, Pallas kernels, local(): pl.pallas_call(attend_kernel, grid=(1,), out_shape=partial_shape, in_spec...  8.05 us
  transfers between devices with their start and end apart: 21, of which 11 were waited for; matrix products, arithmetic and copies ran while one was open for 0% of the time, Pallas kernels for 18%

profile of v7, /device:TPU:8, one launch (start us, length us, event | category | flops | bytes accessed | tf_op | source)
XLA Modules:
  0.0 107.3 jit_solution(15917818312500420577)
XLA Ops:
  0.7 1.5 %shard_map.202.order_ref = bf16[4,8,1536]{2,1,0:T(8,128)(2,1)} custom-call(bf16[2,4,1536]{2,1,0:T(4,128)(2,1)} %bitcast.31, f32[1536]{0:T(1024)} %gain_ref.1), custom_call_target="tpu_custom_call" | custom-call | flops 1048576 | bytes 1048576 | tf_op jit(solution)/shard_map/pallas_call | solution.py:506
  2.2 0.5 collective-permute-start.7
  2.7 0.5 collective-permute-start.2
  3.2 8.5 %all-to-all-start = ((bf16[4,8,1536]{2,1,0:T(8,128)(2,1)}), bf16[4,8,1536]{2,1,0:T(8,128)(2,1)S(1)}, u32[]{:S(2)}, u32[]{:S(2)}) async-start(bf16[4,8,1536]{2,1,0:T(8,128)(2,1)} %shard_map.202.order_ref), calls=%async_computation | async-start | bytes 196608 | tf_op jit(solution)/shard_map/all_to_all | solution.py:564
  11.9 8.7 %all-to-all-done.x_ref = bf16[4,8,1536]{2,1,0:T(8,128)(2,1)S(1)} async-done(((bf16[4,8,1536]{2,1,0:T(8,128)(2,1)}), bf16[4,8,1536]{2,1,0:T(8,128)(2,1)S(1)}, u32[]{:S(2)}, u32[]{:S(2)}) %all-to-all-start) | async-done | bytes 98336 | tf_op jit(solution)/shard_map/all_to_all | solution.py:564
  20.6 2.8 %shard_map.204 = (bf16[4,96,128]{2,1,0:T(8,128)(2,1)}, bf16[2,32,128]{2,1,0:T(8,128)(2,1)S(1)}) custom-call(bf16[4,8,1536]{2,1,0:T(8,128)(2,1)S(1)} %all-to-all-done.x_ref, s32[1]{0:T(128)} %bitcast.6.seq_ref, bf16[192,1536]{1,0:T(8,128)(2,1)} %bitcast.26, bf16[64,1536]{1,0:T(8,128)(2,1)} %bitcast.28, bf16[64,1536]{1,0:T(8,128)(2,1)} %bitcast.30, ...), custom_call_target="tpu_custom_call" | custom-call | flops 1048576 | bytes 1048576 | tf_op jit(solution)/shard_map/pallas_call | solution.py:506
  23.4 3.3 %all-to-all-start.1 = ((bf16[4,96,128]{2,1,0:T(8,128)(2,1)}), bf16[4,96,128]{2,1,0:T(8,128)(2,1)S(1)}, u32[]{:S(2)}, u32[]{:S(2)}) async-start(bf16[4,96,128]{2,1,0:T(8,128)(2,1)} %get-tuple-element.37.q_ref), calls=%async_computation.1 | async-start | bytes 196608 | tf_op jit(solution)/shard_map/all_to_all | solution.py:564
  26.7 0.8 shard_map.205.own_ref.refs_0_
  27.5 0.5 collective-permute-start
  28.0 0.8 collective-permute-done.other_len_ref
  29.1 0.8 shard_map.203
  30.0 1.3 %shard_map.206 = (bf16[32,512]{1,0:T(8,128)(2,1)S(1)}, bf16[4,8,512]{2,1,0:T(8,128)(2,1)S(1)}) custom-call(bf16[4,96,128]{2,1,0:T(8,128)(2,1)} %get-tuple-element.37.q_ref, bf16[2,32,128]{2,1,0:T(8,128)(2,1)S(1)} %get-tuple-element.38.kv_ref, bf16[2,32,128]{2,1,0:T(8,128)(2,1)S(1)} %collective-permute-done.5.other_ref, ...), custom_call_target="tpu_custom_call" | custom-call | flops 1048576 | bytes 1048576 | tf_op jit(solution)/shard_map/pallas_call | solution.py:506
  31.2 3.9 %all-to-all-done.1.q_ref = bf16[4,96,128]{2,1,0:T(8,128)(2,1)S(1)} async-done(((bf16[4,96,128]{2,1,0:T(8,128)(2,1)}), bf16[4,96,128]{2,1,0:T(8,128)(2,1)S(1)}, u32[]{:S(2)}, u32[]{:S(2)}) %all-to-all-start.1) | async-done | bytes 98336 | tf_op jit(solution)/shard_map/all_to_all | solution.py:564
  35.1 8.1 %shard_map.207 = bf16[4,40,512]{2,1,0:T(8,128)(2,1)} custom-call(f32[8,4096]{1,0:T(8,128)S(1)} %get-tuple-element.32.bias_ref, f32[32,128]{1,0:T(8,128)S(1)} %get-tuple-element.33.extra_ref, bf16[4,96,128]{2,1,0:T(8,128)(2,1)S(1)} %all-to-all-done.1.q_ref, bf16[2,2,16,512]{3,2,1,0:T(8,128)(2,1)S(1)} %shard_map.205.own_ref.refs_0_, ...), custom_call_target="tpu_custom_call" | custom-call | flops 805306368 | bytes 8388608 | tf_op jit(solution)/shard_map/pallas_call | solution.py:632
  43.2 3.5 %all-to-all-start.2 = ((bf16[4,40,512]{2,1,0:T(8,128)(2,1)}), bf16[4,40,512]{2,1,0:T(8,128)(2,1)S(1)}, u32[]{:S(2)}, u32[]{:S(2)}) async-start(bf16[4,40,512]{2,1,0:T(8,128)(2,1)} %shard_map.207), calls=%async_computation.2 | async-start | bytes 327680 | tf_op jit(solution)/shard_map/all_to_all | solution.py:564
  46.7 9.2 %all-to-all-done.2.part_ref = bf16[4,40,512]{2,1,0:T(8,128)(2,1)S(1)} async-done(((bf16[4,40,512]{2,1,0:T(8,128)(2,1)}), bf16[4,40,512]{2,1,0:T(8,128)(2,1)S(1)}, u32[]{:S(2)}, u32[]{:S(2)}) %all-to-all-start.2) | async-done | bytes 163872 | tf_op jit(solution)/shard_map/all_to_all | solution.py:564
  55.9 2.0 %shard_map.208.order_ref = bf16[4,8,1536]{2,1,0:T(8,128)(2,1)} custom-call(bf16[4,40,512]{2,1,0:T(8,128)(2,1)S(1)} %all-to-all-done.2.part_ref, bf16[32,512]{1,0:T(8,128)(2,1)S(1)} %get-tuple-element.44.fresh_ref, s32[1]{0:T(128)} %bitcast.6.seq_ref, bf16[192,1536]{1,0:T(8,128)(2,1)} %w_hbm.1, bf16[192,1536]{1,0:T(8,128)(2,1)S(1)} %collective-permute-done.8.other_w_hbm), custom_call_target="tpu_custom_call" | custom-call | flops 1048576 | bytes 1048576 | tf_op jit(solution)/shard_map/pallas_call | solution.py:506
  57.9 3.3 %all-to-all-start.3 = ((bf16[4,8,1536]{2,1,0:T(8,128)(2,1)}), bf16[4,8,1536]{2,1,0:T(8,128)(2,1)S(1)}, u32[]{:S(2)}, u32[]{:S(2)}) async-start(bf16[4,8,1536]{2,1,0:T(8,128)(2,1)} %shard_map.208.order_ref), calls=%async_computation.3 | async-start | bytes 196608 | tf_op jit(solution)/shard_map/all_to_all | solution.py:564
  61.3 1.0 shard_map.209
  62.3 7.4 %all-to-all-done.3.sums_ref = bf16[4,8,1536]{2,1,0:T(8,128)(2,1)S(1)} async-done(((bf16[4,8,1536]{2,1,0:T(8,128)(2,1)}), bf16[4,8,1536]{2,1,0:T(8,128)(2,1)S(1)}, u32[]{:S(2)}, u32[]{:S(2)}) %all-to-all-start.3) | async-done | bytes 98336 | tf_op jit(solution)/shard_map/all_to_all | solution.py:564
  69.7 1.8 %shard_map.210 = (f32[8,1536]{1,0:T(8,128)S(1)}, bf16[32,4,1536]{2,1,0:T(4,128)(2,1)}) custom-call(bf16[2,4,1536]{2,1,0:T(4,128)(2,1)} %bitcast.32, bf16[4,8,1536]{2,1,0:T(8,128)(2,1)S(1)} %all-to-all-done.3.sums_ref, f32[1536]{0:T(1024)} %gain_hbm.1, bf16[128,8]{1,0:T(8,128)(2,1)S(1)} %get-tuple-element.46.place_ref), custom_call_target="tpu_custom_call" | custom-call | flops 1048576 | bytes 1048576 | tf_op jit(solution)/shard_map/pallas_call | solution.py:506
  71.6 7.7 %all-to-all-start.4 = ((bf16[32,4,1536]{2,1,0:T(4,128)(2,1)}), bf16[32,4,1536]{2,1,0:T(4,128)(2,1)S(1)}, u32[]{:S(2)}, u32[]{:S(2)}) async-start(bf16[32,4,1536]{2,1,0:T(4,128)(2,1)} %get-tuple-element.50), calls=%async_computation.4 | async-start | bytes 786432 | tf_op jit(solution)/shard_map/all_to_all | solution.py:561
  79.3 1.0 collective-permute-start.10
  80.3 3.5 %collective-permute-start.11 = (bf16[2,2,16,512]{3,2,1,0:T(8,128)(2,1)S(1)}, bf16[2,2,16,512]{3,2,1,0:T(8,128)(2,1)S(1)}, u32[]{:S(2)}, u32[]{:S(2)}) collective-permute-start(bf16[2,2,16,512]{3,2,1,0:T(8,128)(2,1)S(1)} %shard_map.205.own_ref.refs_0_), channel_id=1, source_target_pairs={{0,192},{32,224},{64,128},{96,160},{128,64},{160,96},{192,0},{224,... | collective-permute-start | bytes 196616 | tf_op jit(solution)/shard_map/ppermute | solution.py:569
  83.8 2.1 %collective-permute-start.9 = (bf16[2,2,16,512]{3,2,1,0:T(8,128)(2,1)S(1)}, bf16[2,2,16,512]{3,2,1,0:T(8,128)(2,1)S(1)}, u32[]{:S(2)}, u32[]{:S(2)}) collective-permute-start(bf16[2,2,16,512]{3,2,1,0:T(8,128)(2,1)S(1)} %shard_map.205.own_ref.refs_0_), channel_id=1, source_target_pairs={{0,64},{32,96},{64,0},{96,32},{128,192},{160,224},{192,128},{224,1... | collective-permute-start | bytes 196616 | tf_op jit(solution)/shard_map/ppermute | solution.py:569
  85.9 3.5 %all-to-all-done.4.x_ref = bf16[32,4,1536]{2,1,0:T(4,128)(2,1)S(1)} async-done(((bf16[32,4,1536]{2,1,0:T(4,128)(2,1)}), bf16[32,4,1536]{2,1,0:T(4,128)(2,1)S(1)}, u32[]{:S(2)}, u32[]{:S(2)}) %all-to-all-start.4) | async-done | bytes 393248 | tf_op jit(solution)/shard_map/all_to_all | solution.py:561
  89.4 3.3 %shard_map.211 = bf16[32,4,1536]{2,1,0:T(4,128)(2,1)} custom-call(bf16[32,4,1536]{2,1,0:T(4,128)(2,1)S(1)} %all-to-all-done.4.x_ref, bf16[1,1536,1024]{2,1,0:T(8,128)(2,1)} %w_in_hbm.1, bf16[1,512,1536]{2,1,0:T(8,128)(2,1)S(1)} %copy-done), custom_call_target="tpu_custom_call" | custom-call | flops 1048576 | bytes 1048576 | tf_op jit(solution)/shard_map/pallas_call | solution.py:506
  92.7 4.9 %all-to-all-start.5 = ((bf16[32,4,1536]{2,1,0:T(4,128)(2,1)}), bf16[32,4,1536]{2,1,0:T(4,128)(2,1)S(1)}, u32[]{:S(2)}, u32[]{:S(2)}) async-start(bf16[32,4,1536]{2,1,0:T(4,128)(2,1)} %shard_map.211), calls=%async_computation.5 | async-start | bytes 786432 | tf_op jit(solution)/shard_map/all_to_all | solution.py:561
  98.3 0.6 collective-permute-done.12.refs_3_
  99.5 1.4 %shard_map.213 = (bf16[20,2,512]{2,1,0:T(2,128)(2,1)}, bf16[20,2,512]{2,1,0:T(2,128)(2,1)}) custom-call(s32[1]{0:T(128)} %bitcast.6.seq_ref, s32[4,16]{1,0:T(4,128)S(1)} %bitcast.20, bf16[4,40,512]{2,1,0:T(8,128)(2,1)S(1)} %all-to-all-done.2.part_ref, bf16[2,2,16,512]{3,2,1,0:T(8,128)(2,1)S(1)} %shard_map.205.own_ref.refs_0_, ...), custom_call_target="tpu_custom_call" | custom-call | flops 1048576 | bytes 1048576 | tf_op jit(solution)/shard_map/pallas_call | solution.py:506
  100.8 5.5 %all-to-all-done.5.back_ref = bf16[32,4,1536]{2,1,0:T(4,128)(2,1)S(1)} async-done(((bf16[32,4,1536]{2,1,0:T(4,128)(2,1)}), bf16[32,4,1536]{2,1,0:T(4,128)(2,1)S(1)}, u32[]{:S(2)}, u32[]{:S(2)}) %all-to-all-start.5) | async-done | bytes 393248 | tf_op jit(solution)/shard_map/all_to_all | solution.py:561
  106.4 1.0 shard_map.212
  (28 shorter events, 1.9 us)
Async XLA Ops:
  0.6 26.8 %copy-start.2 = (s32[1,16]{1,0:T(1,128)S(1)}, s32[1,16]{1,0:T(1,128)}, u32[]{:S(2)}) copy-start(s32[1,16]{1,0:T(1,128)} %len_ref.1) | copy-start | bytes 196
  0.6 28.5 %copy-start.1 = (s32[1,4,16]{2,1,0:T(4,128)S(1)}, s32[1,4,16]{2,1,0:T(4,128)}, u32[]{:S(2)}) copy-start(s32[1,4,16]{2,1,0:T(4,128)} %param.20) | copy-start | bytes 772
  2.1 33.0 %collective-permute-start.6 = (bf16[2048,512]{1,0:T(8,128)(2,1)}, bf16[2048,512]{1,0:T(8,128)(2,1)S(1)}, u32[]{:S(2)}, u32[]{:S(2)}) collective-permute-start(bf16[2048,512]{1,0:T(8,128)(2,1)} %bitcast.21), channel_id=1, source_target_pairs={{0,32},{32,0},{64,96},{96,64},{128,160},{160,128},{192,224},{224,1... | collective-permute-start | bytes 6291464 | tf_op jit(solution)/shard_map/ppermute | solution.py:569
  2.2 33.0 %collective-permute-start.7 = (bf16[2048,512]{1,0:T(8,128)(2,1)}, bf16[2048,512]{1,0:T(8,128)(2,1)}, u32[]{:S(2)}, u32[]{:S(2)}) collective-permute-start(bf16[2048,512]{1,0:T(8,128)(2,1)} %bitcast.23), channel_id=1, source_target_pairs={{0,32},{32,0},{64,96},{96,64},{128,160},{160,128},{192,224},{224,1... | collective-permute-start | bytes 6291464 | tf_op jit(solution)/shard_map/ppermute | solution.py:569
  2.7 17.9 %collective-permute-start.1 = (bf16[192,1536]{1,0:T(8,128)(2,1)}, bf16[192,1536]{1,0:T(8,128)(2,1)S(1)}, u32[]{:S(2)}, u32[]{:S(2)}) collective-permute-start(bf16[192,1536]{1,0:T(8,128)(2,1)} %bitcast.25), channel_id=1, source_target_pairs={{0,32},{32,0},{64,96},{96,64},{128,160},{160,128},{192,224},{224,1... | collective-permute-start | bytes 1769480 | tf_op jit(solution)/shard_map/ppermute | solution.py:569
  2.7 9.0 %collective-permute-start.2 = (bf16[64,1536]{1,0:T(8,128)(2,1)}, bf16[64,1536]{1,0:T(8,128)(2,1)}, u32[]{:S(2)}, u32[]{:S(2)}) collective-permute-start(bf16[64,1536]{1,0:T(8,128)(2,1)} %bitcast.27), channel_id=1, source_target_pairs={{0,32},{32,0},{64,96},{96,64},{128,160},{160,128},{192,224},{224,1... | collective-permute-start | bytes 589832 | tf_op jit(solution)/shard_map/ppermute | solution.py:569
  3.2 17.4 %collective-permute-start.3 = (bf16[64,1536]{1,0:T(8,128)(2,1)}, bf16[64,1536]{1,0:T(8,128)(2,1)}, u32[]{:S(2)}, u32[]{:S(2)}) collective-permute-start(bf16[64,1536]{1,0:T(8,128)(2,1)} %bitcast.29), channel_id=1, source_target_pairs={{0,32},{32,0},{64,96},{96,64},{128,160},{160,128},{192,224},{224,1... | collective-permute-start | bytes 589832 | tf_op jit(solution)/shard_map/ppermute | solution.py:569
  3.2 17.4 %all-to-all-start = ((bf16[4,8,1536]{2,1,0:T(8,128)(2,1)}), bf16[4,8,1536]{2,1,0:T(8,128)(2,1)S(1)}, u32[]{:S(2)}, u32[]{:S(2)}) async-start(bf16[4,8,1536]{2,1,0:T(8,128)(2,1)} %shard_map.202.order_ref), calls=%async_computation | async-start | bytes 196608 | tf_op jit(solution)/shard_map/all_to_all | solution.py:564
  11.6 35.0 %collective-permute-start.8 = (bf16[192,1536]{1,0:T(8,128)(2,1)}, bf16[192,1536]{1,0:T(8,128)(2,1)S(1)}, u32[]{:S(2)}, u32[]{:S(2)}) collective-permute-start(bf16[192,1536]{1,0:T(8,128)(2,1)} %w_hbm.1), channel_id=1, source_target_pairs={{0,32},{32,0},{64,96},{96,64},{128,160},{160,128},{192,224},{224,1... | collective-permute-start | bytes 1769480 | tf_op jit(solution)/shard_map/ppermute | solution.py:569
  23.4 11.7 %all-to-all-start.1 = ((bf16[4,96,128]{2,1,0:T(8,128)(2,1)}), bf16[4,96,128]{2,1,0:T(8,128)(2,1)S(1)}, u32[]{:S(2)}, u32[]{:S(2)}) async-start(bf16[4,96,128]{2,1,0:T(8,128)(2,1)} %get-tuple-element.37.q_ref), calls=%async_computation.1 | async-start | bytes 196608 | tf_op jit(solution)/shard_map/all_to_all | solution.py:564
  27.5 3.8 %collective-permute-start.4 = (bf16[2,2,16,512]{3,2,1,0:T(8,128)(2,1)S(1)}, bf16[2,2,16,512]{3,2,1,0:T(8,128)(2,1)S(1)}, u32[]{:S(2)}, u32[]{:S(2)}) collective-permute-start(bf16[2,2,16,512]{3,2,1,0:T(8,128)(2,1)S(1)} %shard_map.205.own_ref.refs_0_), channel_id=1, source_target_pairs={{0,32},{32,0},{64,96},{96,64},{128,160},{160,128},{192,224},{224,1... | collective-permute-start | bytes 196616 | tf_op jit(solution)/shard_map/ppermute | solution.py:569
  27.5 1.3 %collective-permute-start = (s32[1,16]{1,0:T(1,128)S(1)}, s32[1,16]{1,0:T(1,128)S(1)}, u32[]{:S(2)}, u32[]{:S(2)}) collective-permute-start(s32[1,16]{1,0:T(1,128)S(1)} %copy-done.2), channel_id=1, source_target_pairs={{0,32},{32,0},{64,96},{96,64},{128,160},{160,128},{192,224},{224,1... | collective-permute-start | bytes 200 | tf_op jit(solution)/shard_map/ppermute | solution.py:569
  28.8 1.2 %collective-permute-start.5 = (bf16[2,32,128]{2,1,0:T(8,128)(2,1)S(1)}, bf16[2,32,128]{2,1,0:T(8,128)(2,1)S(1)}, u32[]{:S(2)}, u32[]{:S(2)}) collective-permute-start(bf16[2,32,128]{2,1,0:T(8,128)(2,1)S(1)} %get-tuple-element.38.kv_ref), channel_id=1, source_target_pairs={{0,32},{32,0},{64,96},{96,64},{128,160},{160,128},{192,224},{224,1... | collective-permute-start | bytes 49160 | tf_op jit(solution)/shard_map/ppermute | solution.py:569
  43.2 46.2 %copy-start = (bf16[1,512,1536]{2,1,0:T(8,128)(2,1)S(1)}, bf16[1,512,1536]{2,1,0:T(8,128)(2,1)}, u32[]{:S(2)}) copy-start(bf16[1,512,1536]{2,1,0:T(8,128)(2,1)} %w_out_ref.1) | copy-start | bytes 4718596
  43.2 12.7 %all-to-all-start.2 = ((bf16[4,40,512]{2,1,0:T(8,128)(2,1)}), bf16[4,40,512]{2,1,0:T(8,128)(2,1)S(1)}, u32[]{:S(2)}, u32[]{:S(2)}) async-start(bf16[4,40,512]{2,1,0:T(8,128)(2,1)} %shard_map.207), calls=%async_computation.2 | async-start | bytes 327680 | tf_op jit(solution)/shard_map/all_to_all | solution.py:564
  57.9 11.8 %all-to-all-start.3 = ((bf16[4,8,1536]{2,1,0:T(8,128)(2,1)}), bf16[4,8,1536]{2,1,0:T(8,128)(2,1)S(1)}, u32[]{:S(2)}, u32[]{:S(2)}) async-start(bf16[4,8,1536]{2,1,0:T(8,128)(2,1)} %shard_map.208.order_ref), calls=%async_computation.3 | async-start | bytes 196608 | tf_op jit(solution)/shard_map/all_to_all | solution.py:564
  71.6 17.9 %all-to-all-start.4 = ((bf16[32,4,1536]{2,1,0:T(4,128)(2,1)}), bf16[32,4,1536]{2,1,0:T(4,128)(2,1)S(1)}, u32[]{:S(2)}, u32[]{:S(2)}) async-start(bf16[32,4,1536]{2,1,0:T(4,128)(2,1)} %get-tuple-element.50), calls=%async_computation.4 | async-start | bytes 786432 | tf_op jit(solution)/shard_map/all_to_all | solution.py:561
  79.3 13.4 %collective-permute-start.10 = (bf16[2,2,16,512]{3,2,1,0:T(8,128)(2,1)S(1)}, bf16[2,2,16,512]{3,2,1,0:T(8,128)(2,1)S(1)}, u32[]{:S(2)}, u32[]{:S(2)}) collective-permute-start(bf16[2,2,16,512]{3,2,1,0:T(8,128)(2,1)S(1)} %shard_map.205.own_ref.refs_0_), channel_id=1, source_target_pairs={{0,128},{32,160},{64,192},{96,224},{128,0},{160,32},{192,64},{224,... | collective-permute-start | bytes 196616 | tf_op jit(solution)/shard_map/ppermute | solution.py:569
  80.3 12.4 %collective-permute-start.11 = (bf16[2,2,16,512]{3,2,1,0:T(8,128)(2,1)S(1)}, bf16[2,2,16,512]{3,2,1,0:T(8,128)(2,1)S(1)}, u32[]{:S(2)}, u32[]{:S(2)}) collective-permute-start(bf16[2,2,16,512]{3,2,1,0:T(8,128)(2,1)S(1)} %shard_map.205.own_ref.refs_0_), channel_id=1, source_target_pairs={{0,192},{32,224},{64,128},{96,160},{128,64},{160,96},{192,0},{224,... | collective-permute-start | bytes 196616 | tf_op jit(solution)/shard_map/ppermute | solution.py:569
  83.8 8.9 %collective-permute-start.9 = (bf16[2,2,16,512]{3,2,1,0:T(8,128)(2,1)S(1)}, bf16[2,2,16,512]{3,2,1,0:T(8,128)(2,1)S(1)}, u32[]{:S(2)}, u32[]{:S(2)}) collective-permute-start(bf16[2,2,16,512]{3,2,1,0:T(8,128)(2,1)S(1)} %shard_map.205.own_ref.refs_0_), channel_id=1, source_target_pairs={{0,64},{32,96},{64,0},{96,32},{128,192},{160,224},{192,128},{224,1... | collective-permute-start | bytes 196616 | tf_op jit(solution)/shard_map/ppermute | solution.py:569
  92.7 13.6 %all-to-all-start.5 = ((bf16[32,4,1536]{2,1,0:T(4,128)(2,1)}), bf16[32,4,1536]{2,1,0:T(4,128)(2,1)S(1)}, u32[]{:S(2)}, u32[]{:S(2)}) async-start(bf16[32,4,1536]{2,1,0:T(4,128)(2,1)} %shard_map.211), calls=%async_computation.5 | async-start | bytes 786432 | tf_op jit(solution)/shard_map/all_to_all | solution.py:561
  97.6 1.3 %collective-permute-start.12 = (bf16[2,2,16,512]{3,2,1,0:T(8,128)(2,1)S(1)}, bf16[2,2,16,512]{3,2,1,0:T(8,128)(2,1)S(1)}, u32[]{:S(2)}, u32[]{:S(2)}) collective-permute-start(bf16[2,2,16,512]{3,2,1,0:T(8,128)(2,1)S(1)} %collective-permute-done.9.refs_2_), channel_id=1, source_target_pairs={{0,32},{32,0},{64,96},{96,64},{128,160},{160,128},{192,224},{224,1... | collective-permute-start | bytes 196616 | tf_op jit(solution)/shard_map/ppermute | solution.py:569
  97.7 1.4 %collective-permute-start.13 = (bf16[2,2,16,512]{3,2,1,0:T(8,128)(2,1)S(1)}, bf16[2,2,16,512]{3,2,1,0:T(8,128)(2,1)S(1)}, u32[]{:S(2)}, u32[]{:S(2)}) collective-permute-start(bf16[2,2,16,512]{3,2,1,0:T(8,128)(2,1)S(1)} %collective-permute-done.10.refs_4_), channel_id=1, source_target_pairs={{0,32},{32,0},{64,96},{96,64},{128,160},{160,128},{192,224},{224,1... | collective-permute-start | bytes 196616 | tf_op jit(solution)/shard_map/ppermute | solution.py:569
  98.2 1.3 %collective-permute-start.14 = (bf16[2,2,16,512]{3,2,1,0:T(8,128)(2,1)S(1)}, bf16[2,2,16,512]{3,2,1,0:T(8,128)(2,1)S(1)}, u32[]{:S(2)}, u32[]{:S(2)}) collective-permute-start(bf16[2,2,16,512]{3,2,1,0:T(8,128)(2,1)S(1)} %collective-permute-done.11.refs_6_), channel_id=1, source_target_pairs={{0,32},{32,0},{64,96},{96,64},{128,160},{160,128},{192,224},{224,1... | collective-permute-start | bytes 196616 | tf_op jit(solution)/shard_map/ppermute | solution.py:569

commit v8 on v7

--- a/solution.py
+++ b/solution.py
@@ -55,6 +55,12 @@
 def pack_kernel(order_ref, own_k_ref, own_v_ref, out_ref):
     out_ref[0] = own_k_ref[...]
     out_ref[1] = own_v_ref[...]
+
+
+def stage_kernel(order_ref, source, out_ref, sem):
+    copy = pltpu.make_async_copy(source.at[:, 0 : out_ref.shape[1]], out_ref, sem)
+    copy.start()
+    copy.wait()
 
 
 def swap(x):
@@ -233,8 +239,9 @@
     pick_ref,
     *refs,
 ):
-    other_k_ref, sources, out_ref, held = refs[0], refs[1:4], refs[4], refs[5:8]
-    score_refs, prob_refs, top_ref, sem = refs[8:10], refs[10:12], refs[12], refs[13]
+    other_k_ref, first_k_ref, sources = refs[0], refs[1], refs[2:5]
+    out_ref, held = refs[5], refs[6:9]
+    score_refs, prob_refs, top_ref, sem = refs[9:11], refs[11:13], refs[13], refs[14]
     k_ref, v_ref, other_v_ref = held
     rows = extra_ref.shape[0]
     half = k_ref.shape[0]
@@ -255,8 +262,10 @@
                 sources[i].at[:, lane_span(pair)], held[i].at[:, lane_span(pair)], sem.at[pair, i]
             )
 
+    staged = first_k_ref.shape[1] // 128
+
     def needed(turn):
-        keys_of = [copies[turn, 0]] if turn < pairs else []
+        keys_of = [copies[turn, 0]] if staged <= turn < pairs else []
         return keys_of + [copies[turn - 1, i] for i in (1, 2) if 1 <= turn <= pairs]
 
     for copy in needed(0) + needed(1):
@@ -283,7 +292,8 @@
         else:
             top = top_ref[...]
         at = i * chunk
-        source, start = (k_ref, at) if at < half else (other_k_ref, at - half)
+        own_k_ref = first_k_ref if pair < staged else k_ref
+        source, start = (own_k_ref, at) if at < half else (other_k_ref, at - half)
         s = dot_t(queries[pair], source[start : start + chunk, lane_span(pair)])
         s = s + bias_ref[0:1, at : at + chunk]
         s_ref[:, at : at + chunk] = s
@@ -609,8 +619,7 @@
         normed_all,
         seq,
         *[stay(w) for w in weights],
-        other_weights[0],
-        *map(stay, other_weights[1:]),
+        *other_weights,
         stay(cosine),
         stay(sine),
         ins=[block(normed_all.shape), scalars()],
@@ -627,7 +636,15 @@
     )
 
     resident = pl.BlockSpec(memory_space=pltpu.VMEM)
-    operands = (bias, extra, q_all, own, other_own, pick, other_prompt[0])
+    first_k = pl.pallas_call(
+        stage_kernel,
+        out_shape=shaped((keys, 128)),
+        in_specs=[anywhere] * 2,
+        out_specs=resident,
+        scratch_shapes=[pltpu.SemaphoreType.DMA],
+        compiler_params=params(4),
+    )(q, stay(prompt[0]))
+    operands = (bias, extra, q_all, own, other_own, pick, other_prompt[0], first_k)
     partial_shape = shaped((n_chips, rows + local_rows, 512))
     partial = pl.pallas_call(
         attend_kernel,

time: 108 us -> 110 us (1.019)
  starting transfers between devices: 40.5 us -> 42.5 us
  waiting for transfers between devices: 40.4 us -> 38.4 us
  Pallas kernels: 25.6 us -> 26.9 us
    all_to_all x4, waiting for transfers between devices: 29.2 us -> 28 us  [exchange_chips(): lax.all_to_all(a, 'seq', split_axis=0, concat_axis=0, tiled=True, axis_in...]
  transfers between devices with their start and end apart: 21 -> 21, of which waited for: 11 -> 10; matrix products, arithmetic and copies ran while one was open for 0% -> 0% of each run, Pallas kernels for 18% -> 18%
where the time goes in v8:
time: 110 us; the launch traced here: 109 us
  starting transfers between devices  42.5 us (39%)
  waiting for transfers between devices  38.4 us (35%)
  Pallas kernels  26.9 us (24%)
    all_to_all x4, waiting for transfers between devices, exchange_chips(): lax.all_to_all(a, 'seq', split_axis=0, concat_axis=0, tiled=True, axis_in...  28 us
    all_to_all x4, starting transfers between devices, exchange_chips(): lax.all_to_all(a, 'seq', split_axis=0, concat_axis=0, tiled=True, axis_in...  19.5 us
    pallas_call x11, Pallas kernels, call(): pl.pallas_call(kernel, grid=(1,), out_shape=outs, in_specs=specs, out_spe...  18 us
    all_to_all x2, starting transfers between devices, exchange(): return lax.all_to_all(a, axis, split_axis=0, concat_axis=0, tiled=True)  13.7 us
    ppermute x15, starting transfers between devices, apart(): return lax.ppermute(a, 'seq', [(i, i ^ distance) for i in range(n_seq)])  9.33 us
    all_to_all x2, waiting for transfers between devices, exchange(): return lax.all_to_all(a, axis, split_axis=0, concat_axis=0, tiled=True)  8.38 us
    pallas_call x1, Pallas kernels, local(): pl.pallas_call(attend_kernel, grid=(1,), out_shape=partial_shape, in_spec...  7.89 us
  transfers between devices with their start and end apart: 21, of which 10 were waited for; matrix products, arithmetic and copies ran while one was open for 0% of the time, Pallas kernels for 18%

profile of v8, /device:TPU:8, one launch (start us, length us, event | category | flops | bytes accessed | tf_op | source)
XLA Modules:
  0.0 108.7 jit_solution(3947270493205180907)
XLA Ops:
  0.7 1.5 %shard_map.202.order_ref = bf16[4,8,1536]{2,1,0:T(8,128)(2,1)} custom-call(bf16[2,4,1536]{2,1,0:T(4,128)(2,1)} %bitcast.32, f32[1536]{0:T(1024)} %gain_ref.1), custom_call_target="tpu_custom_call" | custom-call | flops 1048576 | bytes 1048576 | tf_op jit(solution)/shard_map/pallas_call | solution.py:516
  2.1 0.5 collective-permute-start.7
  2.7 0.5 collective-permute-start.2
  3.2 8.5 %all-to-all-start = ((bf16[4,8,1536]{2,1,0:T(8,128)(2,1)}), bf16[4,8,1536]{2,1,0:T(8,128)(2,1)S(1)}, u32[]{:S(2)}, u32[]{:S(2)}) async-start(bf16[4,8,1536]{2,1,0:T(8,128)(2,1)} %shard_map.202.order_ref), calls=%async_computation | async-start | bytes 196608 | tf_op jit(solution)/shard_map/all_to_all | solution.py:574
  11.9 8.7 %all-to-all-done.x_ref = bf16[4,8,1536]{2,1,0:T(8,128)(2,1)S(1)} async-done(((bf16[4,8,1536]{2,1,0:T(8,128)(2,1)}), bf16[4,8,1536]{2,1,0:T(8,128)(2,1)S(1)}, u32[]{:S(2)}, u32[]{:S(2)}) %all-to-all-start) | async-done | bytes 98336 | tf_op jit(solution)/shard_map/all_to_all | solution.py:574
  20.6 2.6 %shard_map.204 = (bf16[4,96,128]{2,1,0:T(8,128)(2,1)}, bf16[2,32,128]{2,1,0:T(8,128)(2,1)S(1)}) custom-call(bf16[4,8,1536]{2,1,0:T(8,128)(2,1)S(1)} %all-to-all-done.x_ref, s32[1]{0:T(128)} %bitcast.6.seq_ref, bf16[192,1536]{1,0:T(8,128)(2,1)} %bitcast.27, bf16[64,1536]{1,0:T(8,128)(2,1)} %bitcast.29, bf16[64,1536]{1,0:T(8,128)(2,1)} %bitcast.31, ...), custom_call_target="tpu_custom_call" | custom-call | flops 1048576 | bytes 1048576 | tf_op jit(solution)/shard_map/pallas_call | solution.py:516
  23.2 3.3 %all-to-all-start.1 = ((bf16[4,96,128]{2,1,0:T(8,128)(2,1)}), bf16[4,96,128]{2,1,0:T(8,128)(2,1)S(1)}, u32[]{:S(2)}, u32[]{:S(2)}) async-start(bf16[4,96,128]{2,1,0:T(8,128)(2,1)} %get-tuple-element.37.q_ref.order_ref), calls=%async_computation.1 | async-start | bytes 196608 | tf_op jit(solution)/shard_map/all_to_all | solution.py:574
  26.5 0.8 shard_map.205.own_ref.refs_0_
  27.3 0.5 collective-permute-start
  27.8 0.8 collective-permute-done.other_len_ref
  28.9 0.8 shard_map.203
  29.7 1.1 shard_map.207.refs_1_
  30.8 1.3 %shard_map.206 = (bf16[32,512]{1,0:T(8,128)(2,1)S(1)}, bf16[4,8,512]{2,1,0:T(8,128)(2,1)S(1)}) custom-call(bf16[4,96,128]{2,1,0:T(8,128)(2,1)} %get-tuple-element.37.q_ref.order_ref, bf16[2,32,128]{2,1,0:T(8,128)(2,1)S(1)} %get-tuple-element.38.kv_ref, bf16[2,32,128]{2,1,0:T(8,128)(2,1)S(1)} %collective-permute-done.5.other_ref, ...), custom_call_target="tpu_custom_call" | custom-call | flops 1048576 | bytes 1048576 | tf_op jit(solution)/shard_map/pallas_call | solution.py:516
  32.0 2.9 %all-to-all-done.1.q_ref = bf16[4,96,128]{2,1,0:T(8,128)(2,1)S(1)} async-done(((bf16[4,96,128]{2,1,0:T(8,128)(2,1)}), bf16[4,96,128]{2,1,0:T(8,128)(2,1)S(1)}, u32[]{:S(2)}, u32[]{:S(2)}) %all-to-all-start.1) | async-done | bytes 98336 | tf_op jit(solution)/shard_map/all_to_all | solution.py:574
  35.0 7.9 %shard_map.208 = bf16[4,40,512]{2,1,0:T(8,128)(2,1)} custom-call(f32[8,4096]{1,0:T(8,128)S(1)} %get-tuple-element.32.bias_ref, f32[32,128]{1,0:T(8,128)S(1)} %get-tuple-element.33.extra_ref, bf16[4,96,128]{2,1,0:T(8,128)(2,1)S(1)} %all-to-all-done.1.q_ref, bf16[2,2,16,512]{3,2,1,0:T(8,128)(2,1)S(1)} %shard_map.205.own_ref.refs_0_, ...), custom_call_target="tpu_custom_call" | custom-call | flops 805306368 | bytes 8388608 | tf_op jit(solution)/shard_map/pallas_call | solution.py:649
  42.9 4.4 %all-to-all-start.2 = ((bf16[4,40,512]{2,1,0:T(8,128)(2,1)}), bf16[4,40,512]{2,1,0:T(8,128)(2,1)S(1)}, u32[]{:S(2)}, u32[]{:S(2)}) async-start(bf16[4,40,512]{2,1,0:T(8,128)(2,1)} %shard_map.208), calls=%async_computation.2 | async-start | bytes 327680 | tf_op jit(solution)/shard_map/all_to_all | solution.py:574
  47.3 9.3 %all-to-all-done.2.part_ref = bf16[4,40,512]{2,1,0:T(8,128)(2,1)S(1)} async-done(((bf16[4,40,512]{2,1,0:T(8,128)(2,1)}), bf16[4,40,512]{2,1,0:T(8,128)(2,1)S(1)}, u32[]{:S(2)}, u32[]{:S(2)}) %all-to-all-start.2) | async-done | bytes 163872 | tf_op jit(solution)/shard_map/all_to_all | solution.py:574
  56.6 2.6 %shard_map.209.order_ref = bf16[4,8,1536]{2,1,0:T(8,128)(2,1)} custom-call(bf16[4,40,512]{2,1,0:T(8,128)(2,1)S(1)} %all-to-all-done.2.part_ref, bf16[32,512]{1,0:T(8,128)(2,1)S(1)} %get-tuple-element.44.fresh_ref, s32[1]{0:T(128)} %bitcast.6.seq_ref, bf16[192,1536]{1,0:T(8,128)(2,1)} %w_hbm.1, bf16[192,1536]{1,0:T(8,128)(2,1)} %collective-permute-done.8.other_w_hbm), custom_call_target="tpu_custom_call" | custom-call | flops 1048576 | bytes 1048576 | tf_op jit(solution)/shard_map/pallas_call | solution.py:516
  59.1 3.3 %all-to-all-start.3 = ((bf16[4,8,1536]{2,1,0:T(8,128)(2,1)}), bf16[4,8,1536]{2,1,0:T(8,128)(2,1)S(1)}, u32[]{:S(2)}, u32[]{:S(2)}) async-start(bf16[4,8,1536]{2,1,0:T(8,128)(2,1)} %shard_map.209.order_ref), calls=%async_computation.3 | async-start | bytes 196608 | tf_op jit(solution)/shard_map/all_to_all | solution.py:574
  62.5 1.0 shard_map.210
  63.5 7.2 %all-to-all-done.3.sums_ref = bf16[4,8,1536]{2,1,0:T(8,128)(2,1)S(1)} async-done(((bf16[4,8,1536]{2,1,0:T(8,128)(2,1)}), bf16[4,8,1536]{2,1,0:T(8,128)(2,1)S(1)}, u32[]{:S(2)}, u32[]{:S(2)}) %all-to-all-start.3) | async-done | bytes 98336 | tf_op jit(solution)/shard_map/all_to_all | solution.py:574
  70.6 1.8 %shard_map.211 = (f32[8,1536]{1,0:T(8,128)S(1)}, bf16[32,4,1536]{2,1,0:T(4,128)(2,1)}) custom-call(bf16[2,4,1536]{2,1,0:T(4,128)(2,1)} %bitcast.33, bf16[4,8,1536]{2,1,0:T(8,128)(2,1)S(1)} %all-to-all-done.3.sums_ref, f32[1536]{0:T(1024)} %gain_hbm.1, bf16[128,8]{1,0:T(8,128)(2,1)S(1)} %get-tuple-element.46.place_ref), custom_call_target="tpu_custom_call" | custom-call | flops 1048576 | bytes 1048576 | tf_op jit(solution)/shard_map/pallas_call | solution.py:516
  72.5 8.3 %all-to-all-start.4 = ((bf16[32,4,1536]{2,1,0:T(4,128)(2,1)}), bf16[32,4,1536]{2,1,0:T(4,128)(2,1)S(1)}, u32[]{:S(2)}, u32[]{:S(2)}) async-start(bf16[32,4,1536]{2,1,0:T(4,128)(2,1)} %get-tuple-element.50), calls=%async_computation.4 | async-start | bytes 786432 | tf_op jit(solution)/shard_map/all_to_all | solution.py:571
  80.9 3.9 %collective-permute-start.11 = (bf16[2,2,16,512]{3,2,1,0:T(8,128)(2,1)S(1)}, bf16[2,2,16,512]{3,2,1,0:T(8,128)(2,1)S(1)}, u32[]{:S(2)}, u32[]{:S(2)}) collective-permute-start(bf16[2,2,16,512]{3,2,1,0:T(8,128)(2,1)S(1)} %shard_map.205.own_ref.refs_0_), channel_id=1, source_target_pairs={{0,192},{32,224},{64,128},{96,160},{128,64},{160,96},{192,0},{224,... | collective-permute-start | bytes 196616 | tf_op jit(solution)/shard_map/ppermute | solution.py:579
  84.9 2.5 %collective-permute-start.9 = (bf16[2,2,16,512]{3,2,1,0:T(8,128)(2,1)S(1)}, bf16[2,2,16,512]{3,2,1,0:T(8,128)(2,1)S(1)}, u32[]{:S(2)}, u32[]{:S(2)}) collective-permute-start(bf16[2,2,16,512]{3,2,1,0:T(8,128)(2,1)S(1)} %shard_map.205.own_ref.refs_0_), channel_id=1, source_target_pairs={{0,64},{32,96},{64,0},{96,32},{128,192},{160,224},{192,128},{224,1... | collective-permute-start | bytes 196616 | tf_op jit(solution)/shard_map/ppermute | solution.py:579
  87.3 2.9 %all-to-all-done.4.x_ref = bf16[32,4,1536]{2,1,0:T(4,128)(2,1)S(1)} async-done(((bf16[32,4,1536]{2,1,0:T(4,128)(2,1)}), bf16[32,4,1536]{2,1,0:T(4,128)(2,1)S(1)}, u32[]{:S(2)}, u32[]{:S(2)}) %all-to-all-start.4) | async-done | bytes 393248 | tf_op jit(solution)/shard_map/all_to_all | solution.py:571
  90.2 3.3 %shard_map.212 = bf16[32,4,1536]{2,1,0:T(4,128)(2,1)} custom-call(bf16[32,4,1536]{2,1,0:T(4,128)(2,1)S(1)} %all-to-all-done.4.x_ref, bf16[1,1536,1024]{2,1,0:T(8,128)(2,1)} %w_in_hbm.1, bf16[1,512,1536]{2,1,0:T(8,128)(2,1)S(1)} %copy-done), custom_call_target="tpu_custom_call" | custom-call | flops 1048576 | bytes 1048576 | tf_op jit(solution)/shard_map/pallas_call | solution.py:516
  93.5 5.4 %all-to-all-start.5 = ((bf16[32,4,1536]{2,1,0:T(4,128)(2,1)}), bf16[32,4,1536]{2,1,0:T(4,128)(2,1)S(1)}, u32[]{:S(2)}, u32[]{:S(2)}) async-start(bf16[32,4,1536]{2,1,0:T(4,128)(2,1)} %shard_map.212), calls=%async_computation.5 | async-start | bytes 786432 | tf_op jit(solution)/shard_map/all_to_all | solution.py:571
  99.7 0.6 collective-permute-done.12.refs_3_
  100.8 1.4 %shard_map.214 = (bf16[20,2,512]{2,1,0:T(2,128)(2,1)}, bf16[20,2,512]{2,1,0:T(2,128)(2,1)}) custom-call(s32[1]{0:T(128)} %bitcast.6.seq_ref, s32[4,16]{1,0:T(4,128)S(1)} %bitcast.20, bf16[4,40,512]{2,1,0:T(8,128)(2,1)S(1)} %all-to-all-done.2.part_ref, bf16[2,2,16,512]{3,2,1,0:T(8,128)(2,1)S(1)} %shard_map.205.own_ref.refs_0_, ...), custom_call_target="tpu_custom_call" | custom-call | flops 1048576 | bytes 1048576 | tf_op jit(solution)/shard_map/pallas_call | solution.py:516
  102.2 5.5 %all-to-all-done.5.back_ref = bf16[32,4,1536]{2,1,0:T(4,128)(2,1)S(1)} async-done(((bf16[32,4,1536]{2,1,0:T(4,128)(2,1)}), bf16[32,4,1536]{2,1,0:T(4,128)(2,1)S(1)}, u32[]{:S(2)}, u32[]{:S(2)}) %all-to-all-start.5) | async-done | bytes 393248 | tf_op jit(solution)/shard_map/all_to_all | solution.py:571
  107.7 1.0 shard_map.213
  (29 shorter events, 2.0 us)
Async XLA Ops:
  0.6 26.7 %copy-start.2 = (s32[1,16]{1,0:T(1,128)S(1)}, s32[1,16]{1,0:T(1,128)}, u32[]{:S(2)}) copy-start(s32[1,16]{1,0:T(1,128)} %len_ref.1) | copy-start | bytes 196
  0.6 28.3 %copy-start.1 = (s32[1,4,16]{2,1,0:T(4,128)S(1)}, s32[1,4,16]{2,1,0:T(4,128)}, u32[]{:S(2)}) copy-start(s32[1,4,16]{2,1,0:T(4,128)} %param.20) | copy-start | bytes 772
  2.1 32.8 %collective-permute-start.6 = (bf16[2048,512]{1,0:T(8,128)(2,1)}, bf16[2048,512]{1,0:T(8,128)(2,1)S(1)}, u32[]{:S(2)}, u32[]{:S(2)}) collective-permute-start(bf16[2048,512]{1,0:T(8,128)(2,1)} %bitcast.21), channel_id=1, source_target_pairs={{0,32},{32,0},{64,96},{96,64},{128,160},{160,128},{192,224},{224,1... | collective-permute-start | bytes 6291464 | tf_op jit(solution)/shard_map/ppermute | solution.py:579
  2.1 32.8 %collective-permute-start.7 = (bf16[2048,512]{1,0:T(8,128)(2,1)}, bf16[2048,512]{1,0:T(8,128)(2,1)}, u32[]{:S(2)}, u32[]{:S(2)}) collective-permute-start(bf16[2048,512]{1,0:T(8,128)(2,1)} %bitcast.24), channel_id=1, source_target_pairs={{0,32},{32,0},{64,96},{96,64},{128,160},{160,128},{192,224},{224,1... | collective-permute-start | bytes 6291464 | tf_op jit(solution)/shard_map/ppermute | solution.py:579
  2.7 17.9 %collective-permute-start.1 = (bf16[192,1536]{1,0:T(8,128)(2,1)}, bf16[192,1536]{1,0:T(8,128)(2,1)S(1)}, u32[]{:S(2)}, u32[]{:S(2)}) collective-permute-start(bf16[192,1536]{1,0:T(8,128)(2,1)} %bitcast.26), channel_id=1, source_target_pairs={{0,32},{32,0},{64,96},{96,64},{128,160},{160,128},{192,224},{224,1... | collective-permute-start | bytes 1769480 | tf_op jit(solution)/shard_map/ppermute | solution.py:579
  2.7 9.0 %collective-permute-start.2 = (bf16[64,1536]{1,0:T(8,128)(2,1)}, bf16[64,1536]{1,0:T(8,128)(2,1)S(1)}, u32[]{:S(2)}, u32[]{:S(2)}) collective-permute-start(bf16[64,1536]{1,0:T(8,128)(2,1)} %bitcast.28), channel_id=1, source_target_pairs={{0,32},{32,0},{64,96},{96,64},{128,160},{160,128},{192,224},{224,1... | collective-permute-start | bytes 589832 | tf_op jit(solution)/shard_map/ppermute | solution.py:579
  3.2 17.4 %collective-permute-start.3 = (bf16[64,1536]{1,0:T(8,128)(2,1)}, bf16[64,1536]{1,0:T(8,128)(2,1)S(1)}, u32[]{:S(2)}, u32[]{:S(2)}) collective-permute-start(bf16[64,1536]{1,0:T(8,128)(2,1)} %bitcast.30), channel_id=1, source_target_pairs={{0,32},{32,0},{64,96},{96,64},{128,160},{160,128},{192,224},{224,1... | collective-permute-start | bytes 589832 | tf_op jit(solution)/shard_map/ppermute | solution.py:579
  3.2 17.4 %all-to-all-start = ((bf16[4,8,1536]{2,1,0:T(8,128)(2,1)}), bf16[4,8,1536]{2,1,0:T(8,128)(2,1)S(1)}, u32[]{:S(2)}, u32[]{:S(2)}) async-start(bf16[4,8,1536]{2,1,0:T(8,128)(2,1)} %shard_map.202.order_ref), calls=%async_computation | async-start | bytes 196608 | tf_op jit(solution)/shard_map/all_to_all | solution.py:574
  11.6 35.7 %collective-permute-start.8 = (bf16[192,1536]{1,0:T(8,128)(2,1)}, bf16[192,1536]{1,0:T(8,128)(2,1)}, u32[]{:S(2)}, u32[]{:S(2)}) collective-permute-start(bf16[192,1536]{1,0:T(8,128)(2,1)} %w_hbm.1), channel_id=1, source_target_pairs={{0,32},{32,0},{64,96},{96,64},{128,160},{160,128},{192,224},{224,1... | collective-permute-start | bytes 1769480 | tf_op jit(solution)/shard_map/ppermute | solution.py:579
  23.2 11.7 %all-to-all-start.1 = ((bf16[4,96,128]{2,1,0:T(8,128)(2,1)}), bf16[4,96,128]{2,1,0:T(8,128)(2,1)S(1)}, u32[]{:S(2)}, u32[]{:S(2)}) async-start(bf16[4,96,128]{2,1,0:T(8,128)(2,1)} %get-tuple-element.37.q_ref.order_ref), calls=%async_computation.1 | async-start | bytes 196608 | tf_op jit(solution)/shard_map/all_to_all | solution.py:574
  27.3 4.7 %collective-permute-start.4 = (bf16[2,2,16,512]{3,2,1,0:T(8,128)(2,1)S(1)}, bf16[2,2,16,512]{3,2,1,0:T(8,128)(2,1)S(1)}, u32[]{:S(2)}, u32[]{:S(2)}) collective-permute-start(bf16[2,2,16,512]{3,2,1,0:T(8,128)(2,1)S(1)} %shard_map.205.own_ref.refs_0_), channel_id=1, source_target_pairs={{0,32},{32,0},{64,96},{96,64},{128,160},{160,128},{192,224},{224,1... | collective-permute-start | bytes 196616 | tf_op jit(solution)/shard_map/ppermute | solution.py:579
  27.3 1.3 %collective-permute-start = (s32[1,16]{1,0:T(1,128)S(1)}, s32[1,16]{1,0:T(1,128)S(1)}, u32[]{:S(2)}, u32[]{:S(2)}) collective-permute-start(s32[1,16]{1,0:T(1,128)S(1)} %copy-done.2), channel_id=1, source_target_pairs={{0,32},{32,0},{64,96},{96,64},{128,160},{160,128},{192,224},{224,1... | collective-permute-start | bytes 200 | tf_op jit(solution)/shard_map/ppermute | solution.py:579
  28.6 2.1 %collective-permute-start.5 = (bf16[2,32,128]{2,1,0:T(8,128)(2,1)S(1)}, bf16[2,32,128]{2,1,0:T(8,128)(2,1)S(1)}, u32[]{:S(2)}, u32[]{:S(2)}) collective-permute-start(bf16[2,32,128]{2,1,0:T(8,128)(2,1)S(1)} %get-tuple-element.38.kv_ref), channel_id=1, source_target_pairs={{0,32},{32,0},{64,96},{96,64},{128,160},{160,128},{192,224},{224,1... | collective-permute-start | bytes 49160 | tf_op jit(solution)/shard_map/ppermute | solution.py:579
  42.9 47.3 %copy-start = (bf16[1,512,1536]{2,1,0:T(8,128)(2,1)S(1)}, bf16[1,512,1536]{2,1,0:T(8,128)(2,1)}, u32[]{:S(2)}) copy-start(bf16[1,512,1536]{2,1,0:T(8,128)(2,1)} %w_out_ref.1) | copy-start | bytes 4718596
  42.9 13.7 %all-to-all-start.2 = ((bf16[4,40,512]{2,1,0:T(8,128)(2,1)}), bf16[4,40,512]{2,1,0:T(8,128)(2,1)S(1)}, u32[]{:S(2)}, u32[]{:S(2)}) async-start(bf16[4,40,512]{2,1,0:T(8,128)(2,1)} %shard_map.208), calls=%async_computation.2 | async-start | bytes 327680 | tf_op jit(solution)/shard_map/all_to_all | solution.py:574
  59.1 11.5 %all-to-all-start.3 = ((bf16[4,8,1536]{2,1,0:T(8,128)(2,1)}), bf16[4,8,1536]{2,1,0:T(8,128)(2,1)S(1)}, u32[]{:S(2)}, u32[]{:S(2)}) async-start(bf16[4,8,1536]{2,1,0:T(8,128)(2,1)} %shard_map.209.order_ref), calls=%async_computation.3 | async-start | bytes 196608 | tf_op jit(solution)/shard_map/all_to_all | solution.py:574
  72.5 17.7 %all-to-all-start.4 = ((bf16[32,4,1536]{2,1,0:T(4,128)(2,1)}), bf16[32,4,1536]{2,1,0:T(4,128)(2,1)S(1)}, u32[]{:S(2)}, u32[]{:S(2)}) async-start(bf16[32,4,1536]{2,1,0:T(4,128)(2,1)} %get-tuple-element.50), calls=%async_computation.4 | async-start | bytes 786432 | tf_op jit(solution)/shard_map/all_to_all | solution.py:571
  80.7 12.8 %collective-permute-start.10 = (bf16[2,2,16,512]{3,2,1,0:T(8,128)(2,1)S(1)}, bf16[2,2,16,512]{3,2,1,0:T(8,128)(2,1)S(1)}, u32[]{:S(2)}, u32[]{:S(2)}) collective-permute-start(bf16[2,2,16,512]{3,2,1,0:T(8,128)(2,1)S(1)} %shard_map.205.own_ref.refs_0_), channel_id=1, source_target_pairs={{0,128},{32,160},{64,192},{96,224},{128,0},{160,32},{192,64},{224,... | collective-permute-start | bytes 196616 | tf_op jit(solution)/shard_map/ppermute | solution.py:579
  80.9 12.6 %collective-permute-start.11 = (bf16[2,2,16,512]{3,2,1,0:T(8,128)(2,1)S(1)}, bf16[2,2,16,512]{3,2,1,0:T(8,128)(2,1)S(1)}, u32[]{:S(2)}, u32[]{:S(2)}) collective-permute-start(bf16[2,2,16,512]{3,2,1,0:T(8,128)(2,1)S(1)} %shard_map.205.own_ref.refs_0_), channel_id=1, source_target_pairs={{0,192},{32,224},{64,128},{96,160},{128,64},{160,96},{192,0},{224,... | collective-permute-start | bytes 196616 | tf_op jit(solution)/shard_map/ppermute | solution.py:579
  84.9 8.6 %collective-permute-start.9 = (bf16[2,2,16,512]{3,2,1,0:T(8,128)(2,1)S(1)}, bf16[2,2,16,512]{3,2,1,0:T(8,128)(2,1)S(1)}, u32[]{:S(2)}, u32[]{:S(2)}) collective-permute-start(bf16[2,2,16,512]{3,2,1,0:T(8,128)(2,1)S(1)} %shard_map.205.own_ref.refs_0_), channel_id=1, source_target_pairs={{0,64},{32,96},{64,0},{96,32},{128,192},{160,224},{192,128},{224,1... | collective-permute-start | bytes 196616 | tf_op jit(solution)/shard_map/ppermute | solution.py:579
  93.5 14.2 %all-to-all-start.5 = ((bf16[32,4,1536]{2,1,0:T(4,128)(2,1)}), bf16[32,4,1536]{2,1,0:T(4,128)(2,1)S(1)}, u32[]{:S(2)}, u32[]{:S(2)}) async-start(bf16[32,4,1536]{2,1,0:T(4,128)(2,1)} %shard_map.212), calls=%async_computation.5 | async-start | bytes 786432 | tf_op jit(solution)/shard_map/all_to_all | solution.py:571
  99.0 1.3 %collective-permute-start.12 = (bf16[2,2,16,512]{3,2,1,0:T(8,128)(2,1)S(1)}, bf16[2,2,16,512]{3,2,1,0:T(8,128)(2,1)S(1)}, u32[]{:S(2)}, u32[]{:S(2)}) collective-permute-start(bf16[2,2,16,512]{3,2,1,0:T(8,128)(2,1)S(1)} %collective-permute-done.9.refs_2_), channel_id=1, source_target_pairs={{0,32},{32,0},{64,96},{96,64},{128,160},{160,128},{192,224},{224,1... | collective-permute-start | bytes 196616 | tf_op jit(solution)/shard_map/ppermute | solution.py:579
  99.1 1.4 %collective-permute-start.13 = (bf16[2,2,16,512]{3,2,1,0:T(8,128)(2,1)S(1)}, bf16[2,2,16,512]{3,2,1,0:T(8,128)(2,1)S(1)}, u32[]{:S(2)}, u32[]{:S(2)}) collective-permute-start(bf16[2,2,16,512]{3,2,1,0:T(8,128)(2,1)S(1)} %collective-permute-done.10.refs_4_), channel_id=1, source_target_pairs={{0,32},{32,0},{64,96},{96,64},{128,160},{160,128},{192,224},{224,1... | collective-permute-start | bytes 196616 | tf_op jit(solution)/shard_map/ppermute | solution.py:579
  99.6 1.3 %collective-permute-start.14 = (bf16[2,2,16,512]{3,2,1,0:T(8,128)(2,1)S(1)}, bf16[2,2,16,512]{3,2,1,0:T(8,128)(2,1)S(1)}, u32[]{:S(2)}, u32[]{:S(2)}) collective-permute-start(bf16[2,2,16,512]{3,2,1,0:T(8,128)(2,1)S(1)} %collective-permute-done.11.refs_6_), channel_id=1, source_target_pairs={{0,32},{32,0},{64,96},{96,64},{128,160},{160,128},{192,224},{224,1... | collective-permute-start | bytes 196616 | tf_op jit(solution)/shard_map/ppermute | solution.py:579

commit v9 on v7

--- a/solution.py
+++ b/solution.py
@@ -241,7 +241,7 @@
     keys = 2 * half
     own_keys = own_ref.shape[1] * own_ref.shape[2]
     pairs = q_ref.shape[0]
-    chunk = 512
+    chunk = 1024
     chunks = keys // chunk
     fill = jnp.zeros((128 - 2 * own_keys, 128), BF16)
 
@@ -328,10 +328,11 @@
         for i in range(chunks):
             if turn < pairs:
                 score(turn, i)
-            if 0 <= turn - 1 < pairs and i < 6:
-                soften(turn - 1, i)
-            if turn >= 2 and i in (3, 6):
-                weigh(turn - 2, 0 if i == 3 else 1)
+            if 0 <= turn - 1 < pairs:
+                for part in range(i * 6 // chunks, (i + 1) * 6 // chunks):
+                    soften(turn - 1, part)
+            if turn >= 2 and i in (1, 3):
+                weigh(turn - 2, i // 2)
         if turn < pairs:
             tops[turn] = jnp.max(top_ref[...], axis=-1, keepdims=True)
 
@@ -672,6 +673,7 @@
         stay(gate_weights[0]),
         ins=[anywhere],
     )
+    sums_here = sums
     sums = exchange_chips(sums)
     hidden, buffer = call(
         dispatch_kernel,
@@ -687,8 +689,9 @@
             pltpu.SemaphoreType.DMA((2,)),
         ],
     )
-    own, buffer = lax.optimization_barrier((own, buffer))
+    own, sums_here = lax.optimization_barrier((own, sums_here))
     even = [own] + [apart(own, k) for k in range(2, n_seq, 2)]
+    buffer, *even = lax.optimization_barrier((buffer, *even))
     buffer = exchange(buffer, "req")
     back = call(
         expert_kernel,
@@ -703,7 +706,6 @@
             pltpu.SemaphoreType.DMA((3,)),
         ],
     )
-    back, *even = lax.optimization_barrier((back, *even))
     odd = [other_own] + [apart(a, 1) for a in even[1:]]
     owns = [a for pair in zip(even, odd) for a in pair]
     back = exchange(back, "req")

time: 108 us -> 110 us (1.019)
  blocking collectives: 0 us -> 16.9 us
  starting transfers between devices: 40.5 us -> 32.7 us
  waiting for transfers between devices: 40.4 us -> 33.3 us
    all_to_all x0 -> x1, blocking collectives: none -> 16.9 us  [exchange(): return lax.all_to_all(a, axis, split_axis=0, concat_axis=0, tiled=True)]
    all_to_all x2 -> x1, starting transfers between devices: 12.6 us -> 4.82 us  [exchange(): return lax.all_to_all(a, axis, split_axis=0, concat_axis=0, tiled=True)]
    all_to_all x4, waiting for transfers between devices: 29.2 us -> 23.5 us  [exchange_chips(): lax.all_to_all(a, 'seq', split_axis=0, concat_axis=0, tiled=True, axis_in...]
    all_to_all x2 -> x1, waiting for transfers between devices: 9.03 us -> 5.5 us  [exchange(): return lax.all_to_all(a, axis, split_axis=0, concat_axis=0, tiled=True)]
    ppermute x15, waiting for transfers between devices: 2.11 us -> 4.32 us  [apart(): return lax.ppermute(a, 'seq', [(i, i ^ distance) for i in range(n_seq)])]
  transfers between devices with their start and end apart: 21 -> 20, of which waited for: 11 -> 12; matrix products, arithmetic and copies ran while one was open for 0% -> 0% of each run, Pallas kernels for 18% -> 16%
where the time goes in v9:
time: 110 us; the launch traced here: 109 us
  waiting for transfers between devices  33.3 us (30%)
  starting transfers between devices  32.7 us (30%)
  Pallas kernels  24.8 us (23%)
  blocking collectives  16.9 us (15%)
    all_to_all x4, waiting for transfers between devices, exchange_chips(): lax.all_to_all(a, 'seq', split_axis=0, concat_axis=0, tiled=True, axis_in...  23.5 us
    all_to_all x4, starting transfers between devices, exchange_chips(): lax.all_to_all(a, 'seq', split_axis=0, concat_axis=0, tiled=True, axis_in...  18.6 us
    all_to_all x1, blocking collectives, exchange(): return lax.all_to_all(a, axis, split_axis=0, concat_axis=0, tiled=True)  16.9 us
    pallas_call x11, Pallas kernels, call(): pl.pallas_call(kernel, grid=(1,), out_shape=outs, in_specs=specs, out_spe...  16.8 us
    ppermute x15, starting transfers between devices, apart(): return lax.ppermute(a, 'seq', [(i, i ^ distance) for i in range(n_seq)])  9.33 us
    pallas_call x1, Pallas kernels, local(): pl.pallas_call(attend_kernel, grid=(1,), out_shape=partial_shape, in_spec...  7.96 us
    all_to_all x1, waiting for transfers between devices, exchange(): return lax.all_to_all(a, axis, split_axis=0, concat_axis=0, tiled=True)  5.5 us
    all_to_all x1, starting transfers between devices, exchange(): return lax.all_to_all(a, axis, split_axis=0, concat_axis=0, tiled=True)  4.82 us
  transfers between devices with their start and end apart: 20, of which 12 were waited for; matrix products, arithmetic and copies ran while one was open for 0% of the time, Pallas kernels for 16%

profile of v9, /device:TPU:8, one launch (start us, length us, event | category | flops | bytes accessed | tf_op | source)
XLA Modules:
  0.0 108.6 jit_solution(14411164828356009291)
XLA Ops:
  0.7 1.5 %shard_map.202.order_ref = bf16[4,8,1536]{2,1,0:T(8,128)(2,1)} custom-call(bf16[2,4,1536]{2,1,0:T(4,128)(2,1)} %bitcast.31, f32[1536]{0:T(1024)} %gain_ref.1), custom_call_target="tpu_custom_call" | custom-call | flops 1048576 | bytes 1048576 | tf_op jit(solution)/shard_map/pallas_call | solution.py:507
  2.2 0.5 collective-permute-start.7
  2.7 0.5 collective-permute-start.2
  3.2 8.5 %all-to-all-start = ((bf16[4,8,1536]{2,1,0:T(8,128)(2,1)}), bf16[4,8,1536]{2,1,0:T(8,128)(2,1)S(1)}, u32[]{:S(2)}, u32[]{:S(2)}) async-start(bf16[4,8,1536]{2,1,0:T(8,128)(2,1)} %shard_map.202.order_ref), calls=%async_computation | async-start | bytes 196608 | tf_op jit(solution)/shard_map/all_to_all | solution.py:565
  11.9 8.7 %all-to-all-done.x_ref = bf16[4,8,1536]{2,1,0:T(8,128)(2,1)S(1)} async-done(((bf16[4,8,1536]{2,1,0:T(8,128)(2,1)}), bf16[4,8,1536]{2,1,0:T(8,128)(2,1)S(1)}, u32[]{:S(2)}, u32[]{:S(2)}) %all-to-all-start) | async-done | bytes 98336 | tf_op jit(solution)/shard_map/all_to_all | solution.py:565
  20.6 2.8 %shard_map.204 = (bf16[4,96,128]{2,1,0:T(8,128)(2,1)}, bf16[2,32,128]{2,1,0:T(8,128)(2,1)S(1)}) custom-call(bf16[4,8,1536]{2,1,0:T(8,128)(2,1)S(1)} %all-to-all-done.x_ref, s32[1]{0:T(128)} %bitcast.6.seq_ref, bf16[192,1536]{1,0:T(8,128)(2,1)} %bitcast.26, bf16[64,1536]{1,0:T(8,128)(2,1)} %bitcast.28, bf16[64,1536]{1,0:T(8,128)(2,1)} %bitcast.30, ...), custom_call_target="tpu_custom_call" | custom-call | flops 1048576 | bytes 1048576 | tf_op jit(solution)/shard_map/pallas_call | solution.py:507
  23.4 3.3 %all-to-all-start.1 = ((bf16[4,96,128]{2,1,0:T(8,128)(2,1)}), bf16[4,96,128]{2,1,0:T(8,128)(2,1)S(1)}, u32[]{:S(2)}, u32[]{:S(2)}) async-start(bf16[4,96,128]{2,1,0:T(8,128)(2,1)} %get-tuple-element.36.q_ref), calls=%async_computation.1 | async-start | bytes 196608 | tf_op jit(solution)/shard_map/all_to_all | solution.py:565
  26.7 0.8 shard_map.205.own_ref.refs_0_
  27.5 0.5 collective-permute-start
  28.0 0.8 collective-permute-done.other_len_ref
  29.1 0.8 shard_map.203
  30.0 1.3 %shard_map.206 = (bf16[32,512]{1,0:T(8,128)(2,1)S(1)}, bf16[4,8,512]{2,1,0:T(8,128)(2,1)S(1)}) custom-call(bf16[4,96,128]{2,1,0:T(8,128)(2,1)} %get-tuple-element.36.q_ref, bf16[2,32,128]{2,1,0:T(8,128)(2,1)S(1)} %get-tuple-element.37.kv_ref, bf16[2,32,128]{2,1,0:T(8,128)(2,1)S(1)} %collective-permute-done.5.other_ref, ...), custom_call_target="tpu_custom_call" | custom-call | flops 1048576 | bytes 1048576 | tf_op jit(solution)/shard_map/pallas_call | solution.py:507
  31.2 3.9 %all-to-all-done.1.q_ref = bf16[4,96,128]{2,1,0:T(8,128)(2,1)S(1)} async-done(((bf16[4,96,128]{2,1,0:T(8,128)(2,1)}), bf16[4,96,128]{2,1,0:T(8,128)(2,1)S(1)}, u32[]{:S(2)}, u32[]{:S(2)}) %all-to-all-start.1) | async-done | bytes 98336 | tf_op jit(solution)/shard_map/all_to_all | solution.py:565
  35.1 8.0 %shard_map.207 = bf16[4,40,512]{2,1,0:T(8,128)(2,1)} custom-call(f32[8,4096]{1,0:T(8,128)S(1)} %get-tuple-element.31.bias_ref, f32[32,128]{1,0:T(8,128)S(1)} %get-tuple-element.32.extra_ref, bf16[4,96,128]{2,1,0:T(8,128)(2,1)S(1)} %all-to-all-done.1.q_ref, bf16[2,2,16,512]{3,2,1,0:T(8,128)(2,1)S(1)} %shard_map.205.own_ref.refs_0_, ...), custom_call_target="tpu_custom_call" | custom-call | flops 805306368 | bytes 8388608 | tf_op jit(solution)/shard_map/pallas_call | solution.py:633
  43.1 3.5 %all-to-all-start.2 = ((bf16[4,40,512]{2,1,0:T(8,128)(2,1)}), bf16[4,40,512]{2,1,0:T(8,128)(2,1)S(1)}, u32[]{:S(2)}, u32[]{:S(2)}) async-start(bf16[4,40,512]{2,1,0:T(8,128)(2,1)} %shard_map.207), calls=%async_computation.2 | async-start | bytes 327680 | tf_op jit(solution)/shard_map/all_to_all | solution.py:565
  46.6 9.3 %all-to-all-done.2.part_ref = bf16[4,40,512]{2,1,0:T(8,128)(2,1)S(1)} async-done(((bf16[4,40,512]{2,1,0:T(8,128)(2,1)}), bf16[4,40,512]{2,1,0:T(8,128)(2,1)S(1)}, u32[]{:S(2)}, u32[]{:S(2)}) %all-to-all-start.2) | async-done | bytes 163872 | tf_op jit(solution)/shard_map/all_to_all | solution.py:565
  55.9 2.0 %shard_map.208.order_ref = bf16[4,8,1536]{2,1,0:T(8,128)(2,1)} custom-call(bf16[4,40,512]{2,1,0:T(8,128)(2,1)S(1)} %all-to-all-done.2.part_ref, bf16[32,512]{1,0:T(8,128)(2,1)S(1)} %get-tuple-element.43.fresh_ref, s32[1]{0:T(128)} %bitcast.6.seq_ref, bf16[192,1536]{1,0:T(8,128)(2,1)} %w_hbm.1, bf16[192,1536]{1,0:T(8,128)(2,1)S(1)} %collective-permute-done.8.other_w_hbm), custom_call_target="tpu_custom_call" | custom-call | flops 1048576 | bytes 1048576 | tf_op jit(solution)/shard_map/pallas_call | solution.py:507
  57.9 3.3 %all-to-all-start.3 = ((bf16[4,8,1536]{2,1,0:T(8,128)(2,1)}), bf16[4,8,1536]{2,1,0:T(8,128)(2,1)S(1)}, u32[]{:S(2)}, u32[]{:S(2)}) async-start(bf16[4,8,1536]{2,1,0:T(8,128)(2,1)} %shard_map.208.order_ref), calls=%async_computation.3 | async-start | bytes 196608 | tf_op jit(solution)/shard_map/all_to_all | solution.py:565
  61.2 5.9 %collective-permute-start.10 = (bf16[2,2,16,512]{3,2,1,0:T(8,128)(2,1)S(1)}, bf16[2,2,16,512]{3,2,1,0:T(8,128)(2,1)S(1)}, u32[]{:S(2)}, u32[]{:S(2)}) collective-permute-start(bf16[2,2,16,512]{3,2,1,0:T(8,128)(2,1)S(1)} %shard_map.205.own_ref.refs_0_), channel_id=1, source_target_pairs={{0,128},{32,160},{64,192},{96,224},{128,0},{160,32},{192,64},{224,... | collective-permute-start | bytes 196616 | tf_op jit(solution)/shard_map/ppermute | solution.py:570
  67.1 0.6 collective-permute-start.11
  67.8 1.0 shard_map.209
  68.8 1.7 %all-to-all-done.3.sums_ref = bf16[4,8,1536]{2,1,0:T(8,128)(2,1)S(1)} async-done(((bf16[4,8,1536]{2,1,0:T(8,128)(2,1)}), bf16[4,8,1536]{2,1,0:T(8,128)(2,1)S(1)}, u32[]{:S(2)}, u32[]{:S(2)}) %all-to-all-start.3) | async-done | bytes 98336 | tf_op jit(solution)/shard_map/all_to_all | solution.py:565
  70.5 1.1 %shard_map.210 = (f32[8,1536]{1,0:T(8,128)S(1)}, bf16[32,4,1536]{2,1,0:T(4,128)(2,1)S(1)}) custom-call(bf16[2,4,1536]{2,1,0:T(4,128)(2,1)} %bitcast.32, bf16[4,8,1536]{2,1,0:T(8,128)(2,1)S(1)} %all-to-all-done.3.sums_ref, f32[1536]{0:T(1024)} %gain_hbm.1, bf16[128,8]{1,0:T(8,128)(2,1)S(1)} %get-tuple-element.45.place_ref), custom_call_target="tpu_custom_call" | custom-call | flops 1048576 | bytes 1048576 | tf_op jit(solution)/shard_map/pallas_call | solution.py:507
  71.9 1.9 %collective-permute-done.11.refs_6_ = bf16[2,2,16,512]{3,2,1,0:T(8,128)(2,1)S(1)} collective-permute-done((bf16[2,2,16,512]{3,2,1,0:T(8,128)(2,1)S(1)}, bf16[2,2,16,512]{3,2,1,0:T(8,128)(2,1)S(1)}, u32[]{:S(2)}, u32[]{:S(2)}) %collective-permute-start.11) | collective-permute-done | bytes 65568 | tf_op jit(solution)/shard_map/ppermute | solution.py:570
  73.8 16.9 %all_to_all.30.x_ref = bf16[32,4,1536]{2,1,0:T(4,128)(2,1)S(1)} all-to-all(bf16[32,4,1536]{2,1,0:T(4,128)(2,1)S(1)} %get-tuple-element.50), channel_id=1, replica_groups=mesh['seq'=8,'req'=32] {'req'}, dimensions={0} | all-to-all | bytes 786432 | tf_op jit(solution)/shard_map/all_to_all | solution.py:562
  90.7 3.3 %shard_map.211 = bf16[32,4,1536]{2,1,0:T(4,128)(2,1)} custom-call(bf16[32,4,1536]{2,1,0:T(4,128)(2,1)S(1)} %all_to_all.30.x_ref, bf16[1,1536,1024]{2,1,0:T(8,128)(2,1)} %w_in_hbm.1, bf16[1,512,1536]{2,1,0:T(8,128)(2,1)S(1)} %copy-done), custom_call_target="tpu_custom_call" | custom-call | flops 1048576 | bytes 1048576 | tf_op jit(solution)/shard_map/pallas_call | solution.py:507
  94.0 4.8 %all-to-all-start.5 = ((bf16[32,4,1536]{2,1,0:T(4,128)(2,1)}), bf16[32,4,1536]{2,1,0:T(4,128)(2,1)S(1)}, u32[]{:S(2)}, u32[]{:S(2)}) async-start(bf16[32,4,1536]{2,1,0:T(4,128)(2,1)} %shard_map.211), calls=%async_computation.5 | async-start | bytes 786432 | tf_op jit(solution)/shard_map/all_to_all | solution.py:562
  98.9 0.5 collective-permute-start.13
  99.5 0.6 collective-permute-done.12.refs_3_
  100.7 1.4 %shard_map.213 = (bf16[20,2,512]{2,1,0:T(2,128)(2,1)}, bf16[20,2,512]{2,1,0:T(2,128)(2,1)}) custom-call(s32[1]{0:T(128)} %bitcast.6.seq_ref, s32[4,16]{1,0:T(4,128)S(1)} %bitcast.20, bf16[4,40,512]{2,1,0:T(8,128)(2,1)S(1)} %all-to-all-done.2.part_ref, bf16[2,2,16,512]{3,2,1,0:T(8,128)(2,1)S(1)} %shard_map.205.own_ref.refs_0_, ...), custom_call_target="tpu_custom_call" | custom-call | flops 1048576 | bytes 1048576 | tf_op jit(solution)/shard_map/pallas_call | solution.py:507
  102.1 5.5 %all-to-all-done.5.back_ref = bf16[32,4,1536]{2,1,0:T(4,128)(2,1)S(1)} async-done(((bf16[32,4,1536]{2,1,0:T(4,128)(2,1)}), bf16[32,4,1536]{2,1,0:T(4,128)(2,1)S(1)}, u32[]{:S(2)}, u32[]{:S(2)}) %all-to-all-start.5) | async-done | bytes 393248 | tf_op jit(solution)/shard_map/all_to_all | solution.py:562
  107.6 1.0 shard_map.212
  (27 shorter events, 1.8 us)
Async XLA Ops:
  0.6 26.8 %copy-start.2 = (s32[1,16]{1,0:T(1,128)S(1)}, s32[1,16]{1,0:T(1,128)}, u32[]{:S(2)}) copy-start(s32[1,16]{1,0:T(1,128)} %len_ref.1) | copy-start | bytes 196
  0.6 28.5 %copy-start.1 = (s32[1,4,16]{2,1,0:T(4,128)S(1)}, s32[1,4,16]{2,1,0:T(4,128)}, u32[]{:S(2)}) copy-start(s32[1,4,16]{2,1,0:T(4,128)} %param.20) | copy-start | bytes 772
  2.1 33.0 %collective-permute-start.6 = (bf16[2048,512]{1,0:T(8,128)(2,1)}, bf16[2048,512]{1,0:T(8,128)(2,1)S(1)}, u32[]{:S(2)}, u32[]{:S(2)}) collective-permute-start(bf16[2048,512]{1,0:T(8,128)(2,1)} %bitcast.21), channel_id=1, source_target_pairs={{0,32},{32,0},{64,96},{96,64},{128,160},{160,128},{192,224},{224,1... | collective-permute-start | bytes 6291464 | tf_op jit(solution)/shard_map/ppermute | solution.py:570
  2.2 33.0 %collective-permute-start.7 = (bf16[2048,512]{1,0:T(8,128)(2,1)}, bf16[2048,512]{1,0:T(8,128)(2,1)}, u32[]{:S(2)}, u32[]{:S(2)}) collective-permute-start(bf16[2048,512]{1,0:T(8,128)(2,1)} %bitcast.23), channel_id=1, source_target_pairs={{0,32},{32,0},{64,96},{96,64},{128,160},{160,128},{192,224},{224,1... | collective-permute-start | bytes 6291464 | tf_op jit(solution)/shard_map/ppermute | solution.py:570
  2.7 17.9 %collective-permute-start.1 = (bf16[192,1536]{1,0:T(8,128)(2,1)}, bf16[192,1536]{1,0:T(8,128)(2,1)S(1)}, u32[]{:S(2)}, u32[]{:S(2)}) collective-permute-start(bf16[192,1536]{1,0:T(8,128)(2,1)} %bitcast.25), channel_id=1, source_target_pairs={{0,32},{32,0},{64,96},{96,64},{128,160},{160,128},{192,224},{224,1... | collective-permute-start | bytes 1769480 | tf_op jit(solution)/shard_map/ppermute | solution.py:570
  2.7 9.0 %collective-permute-start.2 = (bf16[64,1536]{1,0:T(8,128)(2,1)}, bf16[64,1536]{1,0:T(8,128)(2,1)}, u32[]{:S(2)}, u32[]{:S(2)}) collective-permute-start(bf16[64,1536]{1,0:T(8,128)(2,1)} %bitcast.27), channel_id=1, source_target_pairs={{0,32},{32,0},{64,96},{96,64},{128,160},{160,128},{192,224},{224,1... | collective-permute-start | bytes 589832 | tf_op jit(solution)/shard_map/ppermute | solution.py:570
  3.2 17.4 %collective-permute-start.3 = (bf16[64,1536]{1,0:T(8,128)(2,1)}, bf16[64,1536]{1,0:T(8,128)(2,1)}, u32[]{:S(2)}, u32[]{:S(2)}) collective-permute-start(bf16[64,1536]{1,0:T(8,128)(2,1)} %bitcast.29), channel_id=1, source_target_pairs={{0,32},{32,0},{64,96},{96,64},{128,160},{160,128},{192,224},{224,1... | collective-permute-start | bytes 589832 | tf_op jit(solution)/shard_map/ppermute | solution.py:570
  3.2 17.4 %all-to-all-start = ((bf16[4,8,1536]{2,1,0:T(8,128)(2,1)}), bf16[4,8,1536]{2,1,0:T(8,128)(2,1)S(1)}, u32[]{:S(2)}, u32[]{:S(2)}) async-start(bf16[4,8,1536]{2,1,0:T(8,128)(2,1)} %shard_map.202.order_ref), calls=%async_computation | async-start | bytes 196608 | tf_op jit(solution)/shard_map/all_to_all | solution.py:565
  11.6 35.0 %collective-permute-start.8 = (bf16[192,1536]{1,0:T(8,128)(2,1)}, bf16[192,1536]{1,0:T(8,128)(2,1)S(1)}, u32[]{:S(2)}, u32[]{:S(2)}) collective-permute-start(bf16[192,1536]{1,0:T(8,128)(2,1)} %w_hbm.1), channel_id=1, source_target_pairs={{0,32},{32,0},{64,96},{96,64},{128,160},{160,128},{192,224},{224,1... | collective-permute-start | bytes 1769480 | tf_op jit(solution)/shard_map/ppermute | solution.py:570
  23.4 11.7 %all-to-all-start.1 = ((bf16[4,96,128]{2,1,0:T(8,128)(2,1)}), bf16[4,96,128]{2,1,0:T(8,128)(2,1)S(1)}, u32[]{:S(2)}, u32[]{:S(2)}) async-start(bf16[4,96,128]{2,1,0:T(8,128)(2,1)} %get-tuple-element.36.q_ref), calls=%async_computation.1 | async-start | bytes 196608 | tf_op jit(solution)/shard_map/all_to_all | solution.py:565
  27.5 3.8 %collective-permute-start.4 = (bf16[2,2,16,512]{3,2,1,0:T(8,128)(2,1)S(1)}, bf16[2,2,16,512]{3,2,1,0:T(8,128)(2,1)S(1)}, u32[]{:S(2)}, u32[]{:S(2)}) collective-permute-start(bf16[2,2,16,512]{3,2,1,0:T(8,128)(2,1)S(1)} %shard_map.205.own_ref.refs_0_), channel_id=1, source_target_pairs={{0,32},{32,0},{64,96},{96,64},{128,160},{160,128},{192,224},{224,1... | collective-permute-start | bytes 196616 | tf_op jit(solution)/shard_map/ppermute | solution.py:570
  27.5 1.3 %collective-permute-start = (s32[1,16]{1,0:T(1,128)S(1)}, s32[1,16]{1,0:T(1,128)S(1)}, u32[]{:S(2)}, u32[]{:S(2)}) collective-permute-start(s32[1,16]{1,0:T(1,128)S(1)} %copy-done.2), channel_id=1, source_target_pairs={{0,32},{32,0},{64,96},{96,64},{128,160},{160,128},{192,224},{224,1... | collective-permute-start | bytes 200 | tf_op jit(solution)/shard_map/ppermute | solution.py:570
  28.8 1.2 %collective-permute-start.5 = (bf16[2,32,128]{2,1,0:T(8,128)(2,1)S(1)}, bf16[2,32,128]{2,1,0:T(8,128)(2,1)S(1)}, u32[]{:S(2)}, u32[]{:S(2)}) collective-permute-start(bf16[2,32,128]{2,1,0:T(8,128)(2,1)S(1)} %get-tuple-element.37.kv_ref), channel_id=1, source_target_pairs={{0,32},{32,0},{64,96},{96,64},{128,160},{160,128},{192,224},{224,1... | collective-permute-start | bytes 49160 | tf_op jit(solution)/shard_map/ppermute | solution.py:570
  43.1 47.6 %copy-start = (bf16[1,512,1536]{2,1,0:T(8,128)(2,1)S(1)}, bf16[1,512,1536]{2,1,0:T(8,128)(2,1)}, u32[]{:S(2)}) copy-start(bf16[1,512,1536]{2,1,0:T(8,128)(2,1)} %w_out_ref.1) | copy-start | bytes 4718596
  43.1 12.8 %all-to-all-start.2 = ((bf16[4,40,512]{2,1,0:T(8,128)(2,1)}), bf16[4,40,512]{2,1,0:T(8,128)(2,1)S(1)}, u32[]{:S(2)}, u32[]{:S(2)}) async-start(bf16[4,40,512]{2,1,0:T(8,128)(2,1)} %shard_map.207), calls=%async_computation.2 | async-start | bytes 327680 | tf_op jit(solution)/shard_map/all_to_all | solution.py:565
  57.9 12.6 %all-to-all-start.3 = ((bf16[4,8,1536]{2,1,0:T(8,128)(2,1)}), bf16[4,8,1536]{2,1,0:T(8,128)(2,1)S(1)}, u32[]{:S(2)}, u32[]{:S(2)}) async-start(bf16[4,8,1536]{2,1,0:T(8,128)(2,1)} %shard_map.208.order_ref), calls=%async_computation.3 | async-start | bytes 196608 | tf_op jit(solution)/shard_map/all_to_all | solution.py:565
  61.2 10.6 %collective-permute-start.10 = (bf16[2,2,16,512]{3,2,1,0:T(8,128)(2,1)S(1)}, bf16[2,2,16,512]{3,2,1,0:T(8,128)(2,1)S(1)}, u32[]{:S(2)}, u32[]{:S(2)}) collective-permute-start(bf16[2,2,16,512]{3,2,1,0:T(8,128)(2,1)S(1)} %shard_map.205.own_ref.refs_0_), channel_id=1, source_target_pairs={{0,128},{32,160},{64,192},{96,224},{128,0},{160,32},{192,64},{224,... | collective-permute-start | bytes 196616 | tf_op jit(solution)/shard_map/ppermute | solution.py:570
  67.1 6.7 %collective-permute-start.11 = (bf16[2,2,16,512]{3,2,1,0:T(8,128)(2,1)S(1)}, bf16[2,2,16,512]{3,2,1,0:T(8,128)(2,1)S(1)}, u32[]{:S(2)}, u32[]{:S(2)}) collective-permute-start(bf16[2,2,16,512]{3,2,1,0:T(8,128)(2,1)S(1)} %shard_map.205.own_ref.refs_0_), channel_id=1, source_target_pairs={{0,192},{32,224},{64,128},{96,160},{128,64},{160,96},{192,0},{224,... | collective-permute-start | bytes 196616 | tf_op jit(solution)/shard_map/ppermute | solution.py:570
  67.7 6.1 %collective-permute-start.9 = (bf16[2,2,16,512]{3,2,1,0:T(8,128)(2,1)S(1)}, bf16[2,2,16,512]{3,2,1,0:T(8,128)(2,1)S(1)}, u32[]{:S(2)}, u32[]{:S(2)}) collective-permute-start(bf16[2,2,16,512]{3,2,1,0:T(8,128)(2,1)S(1)} %shard_map.205.own_ref.refs_0_), channel_id=1, source_target_pairs={{0,64},{32,96},{64,0},{96,32},{128,192},{160,224},{192,128},{224,1... | collective-permute-start | bytes 196616 | tf_op jit(solution)/shard_map/ppermute | solution.py:570
  94.0 13.6 %all-to-all-start.5 = ((bf16[32,4,1536]{2,1,0:T(4,128)(2,1)}), bf16[32,4,1536]{2,1,0:T(4,128)(2,1)S(1)}, u32[]{:S(2)}, u32[]{:S(2)}) async-start(bf16[32,4,1536]{2,1,0:T(4,128)(2,1)} %shard_map.211), calls=%async_computation.5 | async-start | bytes 786432 | tf_op jit(solution)/shard_map/all_to_all | solution.py:562
  98.8 1.3 %collective-permute-start.12 = (bf16[2,2,16,512]{3,2,1,0:T(8,128)(2,1)S(1)}, bf16[2,2,16,512]{3,2,1,0:T(8,128)(2,1)S(1)}, u32[]{:S(2)}, u32[]{:S(2)}) collective-permute-start(bf16[2,2,16,512]{3,2,1,0:T(8,128)(2,1)S(1)} %collective-permute-done.9.refs_2_), channel_id=1, source_target_pairs={{0,32},{32,0},{64,96},{96,64},{128,160},{160,128},{192,224},{224,1... | collective-permute-start | bytes 196616 | tf_op jit(solution)/shard_map/ppermute | solution.py:570
  98.9 1.4 %collective-permute-start.13 = (bf16[2,2,16,512]{3,2,1,0:T(8,128)(2,1)S(1)}, bf16[2,2,16,512]{3,2,1,0:T(8,128)(2,1)S(1)}, u32[]{:S(2)}, u32[]{:S(2)}) collective-permute-start(bf16[2,2,16,512]{3,2,1,0:T(8,128)(2,1)S(1)} %collective-permute-done.10.refs_4_), channel_id=1, source_target_pairs={{0,32},{32,0},{64,96},{96,64},{128,160},{160,128},{192,224},{224,1... | collective-permute-start | bytes 196616 | tf_op jit(solution)/shard_map/ppermute | solution.py:570
  99.4 1.3 %collective-permute-start.14 = (bf16[2,2,16,512]{3,2,1,0:T(8,128)(2,1)S(1)}, bf16[2,2,16,512]{3,2,1,0:T(8,128)(2,1)S(1)}, u32[]{:S(2)}, u32[]{:S(2)}) collective-permute-start(bf16[2,2,16,512]{3,2,1,0:T(8,128)(2,1)S(1)} %collective-permute-done.11.refs_6_), channel_id=1, source_target_pairs={{0,32},{32,0},{64,96},{96,64},{128,160},{160,128},{192,224},{224,1... | collective-permute-start | bytes 196616 | tf_op jit(solution)/shard_map/ppermute | solution.py:570
